TPU v7x, 32 devices: a whole 2x2x4 slice. The times are simulated.
32 devices in a mesh: expert: 4 (over z), dp: 8 (over y, x, core).
Axes of the slice: x: 2, y: 2, z: 4, core: 2. Of those that a mesh axis runs over, the one named last changes fastest.
Arguments:
- tokens: bfloat16 [3072, 2304], P(('expert', 'dp')), may hold values from -6 to 6
- expert_ids: int32 [3072, 2], P(('expert', 'dp')), may hold values from 0 to 3, all different within a row; in each aligned block of 96 rows (0 to 95, 96 to 191, ...) at most 64 rows name the same one
- gate_weights: float32 [3072, 2], P(('expert', 'dp')), may hold values from 0.2 to 1
- request_lengths: int32 [32, 4], P(('expert', 'dp')), may hold values from 1 to 48, 96 in all within a row
- request_adapter: int32 [32, 4], P(('expert', 'dp')), may hold values from 0 to 63
- expert_weights: bfloat16 [4, 2, 2304, 5760], P('expert', None, None, 'dp'), may hold values from -0.125 to 0.125
- expert_down: bfloat16 [4, 5760, 2304], P('expert', 'dp'), may hold values from -0.078125 to 0.078125
- low_down: bfloat16 [4, 2304, 2048], P('expert', None, 'dp'), may hold values from -0.125 to 0.125
- low_up: bfloat16 [4, 2, 1024, 5760], P('expert', None, None, 'dp'), may hold values from -1.5 to 1.5
Outputs:
- mixed: bfloat16 [3072, 2304], P(('expert', 'dp'))
Inputs may be any that keep to these rules, and one draw needn't show every extreme that they name: `expert_ids`: each row names 2 different experts; within the rows of one device no expert is named by more than 64 rows, a bound that some block reaches. `request_lengths`: each row sums to 96, and its largest entry is exactly 48.
All inputs are finite; a program needn't handle non-finite values.
Results may differ from a plain program's by a relative error of at most 0.017.
Values may be sent and summed in bfloat16 or wider, within the bound.
No kernel may reach another device: no remote copies, remote signals or barrier semaphores. Data moves between devices by JAX's collectives and lax.ppermute only.
A program may use at most 192 MiB of HBM per device.

v0:
```python
import jax
import jax.numpy as jnp
from jax import lax
from jax.sharding import PartitionSpec as P

TOP = 2
RANK = 16


def body(
    tokens,
    expert_ids,
    gate_weights,
    request_lengths,
    request_adapter,
    expert_weights,
    expert_down,
    low_down,
    low_up,
):
    ways_expert = lax.axis_size("expert")
    local_tokens = tokens.shape[0]
    width = tokens.shape[1]
    experts_all = ways_expert * expert_down.shape[0]
    capacity = local_tokens * TOP * 4 // (3 * experts_all)
    slots_all = experts_all * capacity
    held = low_down.shape[2] // (2 * RANK)
    adapters_all = low_up.shape[2] // RANK
    values = tokens.astype(jnp.float32)
    normed = (values * lax.rsqrt(jnp.mean(values * values, axis=1, keepdims=True) + 1e-05)).astype(
        jnp.bfloat16
    )
    ends = jnp.cumsum(request_lengths[0])
    place = jnp.arange(local_tokens, dtype=jnp.int32)
    which = jnp.sum((place[:, None] >= ends[None, :]).astype(jnp.int32), axis=1)
    lookup = (
        which[:, None] == jnp.arange(request_lengths.shape[1], dtype=jnp.int32)[None, :]
    ).astype(jnp.int32)
    adapter = jnp.sum(lookup * request_adapter[0][None, :], axis=1)
    flat = expert_ids.reshape(-1)
    onehot = (flat[:, None] == jnp.arange(experts_all, dtype=jnp.int32)[None, :]).astype(jnp.int32)
    slot = jnp.sum((jnp.cumsum(onehot, axis=0) - onehot) * onehot, axis=1)
    target = flat * capacity + slot
    placement_weights = (jnp.arange(slots_all, dtype=jnp.int32)[:, None] == target[None, :]).astype(
        jnp.bfloat16
    )
    pairs = jnp.repeat(normed, TOP, axis=0)
    outgoing = (
        jnp.dot(placement_weights, pairs, preferred_element_type=jnp.float32)
        .astype(jnp.bfloat16)
        .reshape(experts_all, capacity, width)
    )
    pair_adapter = jnp.repeat(adapter, TOP).astype(jnp.float32)
    outgoing_ids = (
        jnp.dot(placement_weights.astype(jnp.float32), pair_adapter)
        .astype(jnp.bfloat16)
        .reshape(experts_all, capacity)
    )
    arrived, arrived_ids = (
        lax.all_to_all(outgoing, "expert", split_axis=0, concat_axis=0, tiled=True),
        lax.all_to_all(outgoing_ids, "expert", split_axis=0, concat_axis=0, tiled=True),
    )
    rows, labels_wire = (
        lax.all_gather(arrived.reshape(-1, width), "dp", axis=0, tiled=True),
        lax.all_gather(arrived_ids.reshape(-1), "dp", axis=0, tiled=True),
    )
    rows_total = rows.shape[0]
    labels = labels_wire.astype(jnp.int32)
    group = lax.axis_index("dp")
    projected = jnp.dot(rows, low_down[0], preferred_element_type=jnp.float32).reshape(
        rows_total, held, 2 * RANK
    )
    owned = (labels[:, None] == group * held + jnp.arange(held, dtype=jnp.int32)[None, :]).astype(
        jnp.float32
    )
    lowrank_part = jnp.sum(owned[:, :, None] * projected, axis=1)
    lowrank = lax.psum(lowrank_part.astype(jnp.bfloat16), "dp")
    marks = (labels[:, None] == jnp.arange(adapters_all, dtype=jnp.int32)[None, :]).astype(
        jnp.bfloat16
    )
    spread_gate = (marks[:, :, None] * lowrank[:, None, :RANK]).reshape(
        lax.axis_size("dp") * (ways_expert * capacity), adapters_all * RANK
    )
    sharded_up_weight = (marks[:, :, None] * lowrank[:, None, RANK:]).reshape(
        lax.axis_size("dp") * (ways_expert * capacity), adapters_all * RANK
    )
    gate = jnp.dot(rows, expert_weights[0, 0], preferred_element_type=jnp.float32) + jnp.dot(
        spread_gate, low_up[0, 0], preferred_element_type=jnp.float32
    )
    up = jnp.dot(rows, expert_weights[0, 1], preferred_element_type=jnp.float32) + jnp.dot(
        sharded_up_weight, low_up[0, 1], preferred_element_type=jnp.float32
    )
    hidden_activations = (jax.nn.silu(gate) * up).astype(jnp.bfloat16)
    mine = lax.psum_scatter(
        jnp.dot(hidden_activations, expert_down[0], preferred_element_type=jnp.float32).astype(
            jnp.bfloat16
        ),
        "dp",
        scatter_dimension=0,
        tiled=True,
    ).astype(jnp.float32)
    mine = mine.astype(jnp.bfloat16).reshape(ways_expert, capacity, width)
    back = lax.all_to_all(mine, "expert", split_axis=0, concat_axis=0, tiled=True)
    picked = jnp.dot(
        placement_weights.T, back.reshape(slots_all, width), preferred_element_type=jnp.float32
    ).reshape(local_tokens, TOP, width)
    mixed = values + jnp.sum(gate_weights[:, :, None] * picked, axis=1)
    return mixed.astype(jnp.bfloat16)


def solution(mesh):
    return jax.shard_map(
        body,
        mesh=mesh,
        in_specs=(
            P(("expert", "dp"), None),
            P(("expert", "dp"), None),
            P(("expert", "dp"), None),
            P(("expert", "dp"), None),
            P(("expert", "dp"), None),
            P("expert", None, None, "dp"),
            P("expert", "dp", None),
            P("expert", None, "dp"),
            P("expert", None, None, "dp"),
        ),
        out_specs=P(("expert", "dp"), None),
        check_vma=False,
    )
```

profile of v0, /device:TPU:0, one launch (start us, length us, event | category | flops | bytes accessed | tf_op | source)
XLA Modules:
  0.0 319.4 jit_solution(102362111478720045)
XLA Ops:
  6.5 0.9 copy.24
  7.6 1.2 reduce-window.18
  9.3 1.2 fusion.24
  10.5 1.2 fusion.25
  11.7 1.4 broadcast_in_dim.4
  13.1 3.1 reshape.195
  16.2 1.6 convolution_convert_fusion.1
  17.9 34.8 %all_to_all.20 = bf16[4,64,2304]{2,1,0:T(8,128)(2,1)} all-to-all(bf16[4,64,2304]{2,1,0:T(8,128)(2,1)S(1)} %bitcast.58), channel_id=1, replica_groups=mesh['expert'=4,'dp'=8] {'expert'}, dimensions={0} | all-to-all | bytes 2359296 | tf_op jit(solution)/shard_map/all_to_all | solution.py:60
  52.7 0.2 reduce-window.20
  53.1 0.2 reshape.208
  53.3 0.2 fusion.28
  53.4 0.7 all_to_all.16
  54.1 3.2 %all-to-all-start.1 = ((bf16[4,1,64]{2,1,0:T(2,128)(2,1)}), bf16[4,1,64]{2,1,0:T(2,128)(2,1)S(1)}, u32[]{:S(2)}, u32[]{:S(2)}) async-start(bf16[4,1,64]{2,1,0:T(2,128)(2,1)} %all_to_all.16), calls=%async_computation.1 | async-start | bytes 4096 | tf_op jit(solution)/shard_map/all_to_all | solution.py:61
  57.4 2.4 copy.28
  59.9 2.9 all-to-all-done.1
  62.9 8.9 %all-gather = bf16[8,1,256]{2,1,0:T(2,128)(2,1)S(1)} all-gather(bf16[1,1,256]{2,1,0:T(2,128)(2,1)S(1)} %reshape.204), channel_id=1, replica_groups=mesh['expert'=4,'dp'=8] {'dp'}, dimensions={0}, use_global_device_ids=true | all-gather | bytes 4608 | tf_op jit(solution)/shard_map/all_gather | solution.py:65
  71.9 0.8 fusion.27
  72.6 38.1 %all-gather.3.cloned.1.call-done = bf16[2048,2304]{1,0:T(8,128)(2,1)} async-done(((bf16[256,2304]{1,0:T(8,128)(2,1)}), bf16[2048,2304]{1,0:T(8,128)(2,1)}) %all-gather.3.cloned.1.call-update) | async-done | bytes 9437200 | tf_op jit(solution)/shard_map/all_gather | solution.py:64
  110.8 7.3 %fusion.21 = bf16[2048,32]{0,1:T(8,128)(2,1)} fusion(bf16[8,32,2304]{2,1,0:T(8,128)(2,1)} %bitcast.62, bf16[2048,2304]{1,0:T(8,128)(2,1)} %all-gather.3.cloned.1.call-done, f32[2048,8]{0,1:T(8,128)S(1)} %compare_convert_fusion), kind=kOutput, calls=%fused_computation.23 | convolution fusion | flops 2416902144 | bytes 10813440 | tf_op jit(solution)/shard_map/dot_general | solution.py:70
  118.1 0.2 reduce-scatter.2.cloned.1.call-start
  118.3 12.2 %fusion.3 = f32[2048,720]{0,1:T(8,128)} fusion(bf16[2048,2304]{1,0:T(8,128)(2,1)} %all-gather.3.cloned.1.call-done, bf16[1,2,2304,720]{2,3,1,0:T(8,128)(2,1)} %param.14), kind=kOutput, calls=%fused_computation.7 | convolution fusion | flops 6794772480 | bytes 18653184 | tf_op jit(solution)/shard_map/dot_general | solution.py:90
  130.5 12.2 %fusion.5 = f32[2048,720]{0,1:T(8,128)} fusion(bf16[2048,2304]{1,0:T(8,128)(2,1)} %all-gather.3.cloned.1.call-done, bf16[1,2,2304,720]{2,3,1,0:T(8,128)(2,1)} %param.14), kind=kOutput, calls=%fused_computation.9 | convolution fusion | flops 6794772480 | bytes 18653184 | tf_op jit(solution)/shard_map/dot_general | solution.py:87
  142.8 28.4 %all-reduce.3.cloned.1.call-done = bf16[2048,32]{0,1:T(8,128)(2,1)} async-done(((bf16[2048,32]{0,1:T(8,128)(2,1)}), bf16[2048,32]{0,1:T(8,128)(2,1)}) %all-reduce.3.cloned.1.call-update) | async-done | bytes 131088 | tf_op jit(solution)/shard_map/psum | solution.py:77
  171.2 0.9 fusion.35
  172.1 3.7 %broadcast_multiply_fusion = (bf16[2048,64,16]{0,2,1:T(8,128)(2,1)}, bf16[2048,64,16]{0,2,1:T(8,128)(2,1)S(1)}) fusion(bf16[2048,16]{0,1:T(8,128)(2,1)S(1)} %get-tuple-element.7, bf16[2048,64]{0,1:T(8,128)(2,1)} %fusion.27, bf16[2048,16]{0,1:T(8,128)(2,1)S(1)} %get-tuple-element.8), kind=kLoop, calls=%fused_computation.15 | loop fusion | flops 4194304 | bytes 8781824 | tf_op jit(solution)/shard_map/mul | solution.py:84
  175.8 5.2 %fusion.15 = f32[2048,720]{0,1:T(8,128)} fusion(bf16[2048,1024]{0,1:T(8,128)(2,1)S(1)} %bitcast.61, bf16[1,2,1024,720]{2,3,1,0:T(8,128)(2,1)S(1)} %copy-done.2), kind=kOutput, calls=%fused_computation.18 | convolution fusion | flops 3019898880 | bytes 11567104 | tf_op jit(solution)/shard_map/dot_general | solution.py:87
  181.0 18.9 %convolution_convert_fusion = bf16[2048,2304]{1,0:T(8,128)(2,1)} fusion(bf16[1,720,2304]{2,1,0:T(8,128)(2,1)S(1)} %copy-done, f32[2048,720]{0,1:T(8,128)} %fusion.3, f32[2048,720]{0,1:T(8,128)} %fusion.5, f32[2048,720]{0,1:T(8,128)} %fusion.15, bf16[2048,1024]{0,1:T(8,128)(2,1)} %bitcast.60, bf16[1,2,1024,720]{2,3,1,0:T(8,128)(2,1)} %param.17), kind=kOutput, calls=%fused_computation | convolution fusion | flops 9831186432 | bytes 36118528 | tf_op jit(solution)/shard_map/dot_general | solution.py:95
  199.9 76.0 %reduce-scatter.2.cloned.1.call-done = bf16[256,2304]{1,0:T(8,128)(2,1)} async-done(((bf16[2048,2304]{1,0:T(8,128)(2,1)}), bf16[256,2304]{1,0:T(8,128)(2,1)}) %reduce-scatter.2.cloned.1.call-update) | async-done | bytes 1179664 | tf_op jit(solution)/shard_map/reduce_scatter | solution.py:94
  276.0 4.6 %all-to-all-start.2 = ((bf16[4,64,2304]{2,1,0:T(8,128)(2,1)}), bf16[4,64,2304]{2,1,0:T(8,128)(2,1)}, u32[]{:S(2)}, u32[]{:S(2)}) async-start(bf16[4,64,2304]{2,1,0:T(8,128)(2,1)} %bitcast.63), calls=%async_computation.3 | async-start | bytes 2359296 | tf_op jit(solution)/shard_map/all_to_all | solution.py:103
  280.7 28.5 %all-to-all-done.2 = bf16[4,64,2304]{2,1,0:T(8,128)(2,1)} async-done(((bf16[4,64,2304]{2,1,0:T(8,128)(2,1)}), bf16[4,64,2304]{2,1,0:T(8,128)(2,1)}, u32[]{:S(2)}, u32[]{:S(2)}) %all-to-all-start.2) | async-done | bytes 1179680 | tf_op jit(solution)/shard_map/all_to_all | solution.py:103
  309.2 1.7 fusion.20
  311.0 1.9 fusion.26
  (41 shorter events, 1.3 us)
Async XLA Ops:
  6.5 174.4 %copy-start = (bf16[1,720,2304]{2,1,0:T(8,128)(2,1)S(1)}, bf16[1,720,2304]{2,1,0:T(8,128)(2,1)}, u32[]{:S(2)}) copy-start(bf16[1,720,2304]{2,1,0:T(8,128)(2,1)} %param.15) | copy-start | bytes 9953284
  6.5 104.2 %all-gather.3.cloned.1.call-start = ((), (), s32[]{:S(2)}) async-start(), calls=%async_computation.4 | async-start | bytes 10616832 | tf_op jit(solution)/shard_map/all_gather | solution.py:64
  11.7 41.0 %copy-start.3 = (s32[1,4]{1,0:T(1,128)S(1)}, s32[1,4]{1,0:T(1,128)}, u32[]{:S(2)}) copy-start(s32[1,4]{1,0:T(1,128)} %param.12) | copy-start | bytes 52
  11.7 41.2 %copy-start.4 = (s32[1,4]{1,0:T(1,128)S(1)}, s32[1,4]{1,0:T(1,128)}, u32[]{:S(2)}) copy-start(s32[1,4]{1,0:T(1,128)} %param.13) | copy-start | bytes 52
  54.1 8.7 %all-to-all-start.1 = ((bf16[4,1,64]{2,1,0:T(2,128)(2,1)}), bf16[4,1,64]{2,1,0:T(2,128)(2,1)S(1)}, u32[]{:S(2)}, u32[]{:S(2)}) async-start(bf16[4,1,64]{2,1,0:T(2,128)(2,1)} %all_to_all.16), calls=%async_computation.1 | async-start | bytes 4096 | tf_op jit(solution)/shard_map/all_to_all | solution.py:61
  57.4 113.8 %all-reduce.3.cloned.1.call-start = ((), (), s32[]{:S(2)}) async-start(), calls=%async_computation.5 | async-start | bytes 262144 | tf_op jit(solution)/shard_map/psum | solution.py:77
  118.1 157.9 %reduce-scatter.2.cloned.1.call-start = ((), (), s32[]{:S(2)}) async-start(), calls=%async_computation.6 | async-start | bytes 10616832 | tf_op jit(solution)/shard_map/reduce_scatter | solution.py:94
  172.1 3.7 %copy-start.2 = (bf16[1,2,1024,720]{2,3,1,0:T(8,128)(2,1)S(1)}, bf16[1,2,1024,720]{2,3,1,0:T(8,128)(2,1)}, u32[]{:S(2)}) copy-start(bf16[1,2,1024,720]{2,3,1,0:T(8,128)(2,1)} %param.17) | copy-start | bytes 8847364
  199.9 109.3 %copy-start.1 = (f32[96,2]{0,1:T(2,128)S(1)}, f32[96,2]{0,1:T(2,128)}, u32[]{:S(2)}) copy-start(f32[96,2]{0,1:T(2,128)} %param.11) | copy-start | bytes 2308
  276.0 33.2 %all-to-all-start.2 = ((bf16[4,64,2304]{2,1,0:T(8,128)(2,1)}), bf16[4,64,2304]{2,1,0:T(8,128)(2,1)}, u32[]{:S(2)}, u32[]{:S(2)}) async-start(bf16[4,64,2304]{2,1,0:T(8,128)(2,1)} %bitcast.63), calls=%async_computation.3 | async-start | bytes 2359296 | tf_op jit(solution)/shard_map/all_to_all | solution.py:103
Sparse Core Ops, SparseCore 0:
  52.8 57.9 all-gather.2
  118.2 52.9 all-reduce.2
  200.1 75.8 reduce-scatter.1
where the time goes:
time: 320 us; the launch traced here: 319 us
  waiting for transfers between devices  174 us (54%)
  matrix products  59.4 us (19%)
  blocking collectives  43.7 us (14%)
  between operations  13.3 us (4%)
  other arithmetic  10.7 us (3%)
  local copies, waits for them, and re-layouts  10.3 us (3%)
  starting transfers between devices  8.09 us (3%)
    reduce_scatter x1, waiting for transfers between devices, body(): lax.psum_scatter(jnp.dot(hidden_activations, expert_down[0], preferred_el...  76 us
    all_gather x1, waiting for transfers between devices, body(): lax.all_gather(arrived.reshape(-1, width), 'dp', axis=0, tiled=True)  38.1 us
    all_to_all x1, blocking collectives, body(): lax.all_to_all(outgoing, 'expert', split_axis=0, concat_axis=0, tiled=True)  34.8 us
    all_to_all x1, waiting for transfers between devices, body(): lax.all_to_all(mine, 'expert', split_axis=0, concat_axis=0, tiled=True)  28.5 us
    psum x1, waiting for transfers between devices, body(): lowrank = lax.psum(lowrank_part.astype(jnp.bfloat16), 'dp')  28.4 us
    dot_general x1, matrix products, body(): jnp.dot(hidden_activations, expert_down[0], preferred_element_type=jnp.fl...  18.9 us
    dot_general x1, matrix products, body(): jnp.dot(rows, expert_weights[0, 0], preferred_element_type=jnp.float32)  12.2 us
    dot_general x1, matrix products, body(): jnp.dot(rows, expert_weights[0, 1], preferred_element_type=jnp.float32)  12.2 us
  transfers between devices with their start and end apart: 5, of which 5 were waited for; matrix products, arithmetic and copies ran while one was open for 9% of the time, Pallas kernels for 0%

commit v1 on v0

v1 whole, which is shorter than its diff:
```python
import functools

import jax
import jax.numpy as jnp
from jax import lax
from jax.experimental import pallas as pl
from jax.experimental.pallas import tpu as pltpu
from jax.sharding import PartitionSpec as P

TOP = 2
RANK = 16
LANES = 128
BF = jnp.bfloat16
F32 = jnp.float32
I32 = jnp.int32
VM = pl.BlockSpec(memory_space=pltpu.VMEM)
SM = pl.BlockSpec(memory_space=pltpu.SMEM)


def swap(x, axis, bit):
    n = lax.axis_size(axis)
    return lax.ppermute(x, axis, [(i, i ^ bit) for i in range(n)])


def call(fn, outs, args, specs, flops, name):
    size = sum(a.size * a.dtype.itemsize for a in args) + sum(
        o.size * o.dtype.itemsize for o in outs
    )
    return pl.pallas_call(
        fn,
        out_shape=tuple(outs),
        in_specs=specs,
        out_specs=tuple(VM for _ in outs),
        compiler_params=pltpu.CompilerParams(vmem_limit_bytes=16 << 20),
        cost_estimate=pl.CostEstimate(flops=flops, bytes_accessed=size, transcendentals=0),
        name=name,
    )(*args)


def shape(rows, cols, dtype=BF):
    return jax.ShapeDtypeStruct((rows, cols), dtype)


def one_hots(ids_ref, z, experts, capacity, local_tokens):
    first = ids_ref[0:1, :]
    second = ids_ref[1:2, :]
    member = jnp.concatenate(
        [((first == (z ^ d)) | (second == (z ^ d))).astype(F32) for d in range(experts)], axis=0
    )
    before = (
        lax.broadcasted_iota(I32, (local_tokens, local_tokens), 0)
        < lax.broadcasted_iota(I32, (local_tokens, local_tokens), 1)
    ).astype(F32)
    slot = jnp.dot(member.astype(BF), before.astype(BF), preferred_element_type=F32)
    rank = lax.broadcasted_iota(I32, (capacity, local_tokens), 0).astype(F32)
    return [
        jnp.where((rank == slot[d : d + 1, :]) & (member[d : d + 1, :] > 0.0), 1.0, 0.0)
        for d in range(experts)
    ]


def front_kernel(experts, capacity, z_ref, len_ref, ada_ref, ids_ref, tok_ref, *outs):
    local_tokens, width = tok_ref.shape
    values = tok_ref[...].astype(F32)
    normed = (
        values * lax.rsqrt(jnp.mean(values * values, axis=1, keepdims=True) + 1e-05)
    ).astype(BF)
    place = lax.broadcasted_iota(I32, (local_tokens, LANES), 0)
    lane = lax.broadcasted_iota(I32, (local_tokens, LANES), 1)
    tag = jnp.zeros((local_tokens, LANES), F32) + ada_ref[0, 0].astype(F32)
    end = len_ref[0, 0]
    for r in range(1, len_ref.shape[1]):
        tag = jnp.where(place >= end, ada_ref[0, r].astype(F32), tag)
        end = end + len_ref[0, r]
    tag = jnp.where(lane == 0, tag, 0.0).astype(BF)
    puts = one_hots(ids_ref, z_ref[0], experts, capacity, local_tokens)
    for d in range(experts):
        put = puts[d].astype(BF)
        outs[d][:, :width] = jnp.dot(put, normed, preferred_element_type=F32).astype(BF)
        outs[d][:, width:] = jnp.dot(put, tag, preferred_element_type=F32).astype(BF)


def proj_kernel(counts, held, me_ref, fold_ref, *refs):
    n = sum(counts)
    piece_refs = refs[:n]
    ld_refs = refs[n : n + 2]
    rows_ref, tag_ref = refs[n + 2], refs[n + 3]
    packs = refs[n + 4 :]
    width = rows_ref.shape[1]
    start = 0
    for ref in piece_refs:
        size = ref.shape[0]
        rows_ref[start : start + size, :] = ref[:, :width]
        tag_ref[start : start + size, :] = ref[:, width:]
        start += size
    spots = len(counts)
    group = start // spots
    labels = tag_ref[:, 0:1].astype(F32)
    cols = held * 2 * RANK
    column = lax.broadcasted_iota(I32, (1, cols), 1) // (2 * RANK)
    kept = []
    for side in range(2):
        base = (me_ref[0] ^ side) * held
        prod = jnp.dot(rows_ref[...], ld_refs[side][...], preferred_element_type=F32)
        kept.append(jnp.where(labels == (column + base).astype(F32), prod, 0.0).astype(BF))
    folded = jnp.dot(kept[0] + kept[1], fold_ref[...], preferred_element_type=F32)
    lanes = packs[0].shape[1]
    spot = lax.broadcasted_iota(I32, (1, lanes), 1) // (2 * RANK)
    for s in range(spots):
        total = jnp.zeros((group, lanes), F32)
        for p in range(spots):
            total = total + jnp.where(
                spot == (p ^ s), folded[p * group : (p + 1) * group, :], 0.0
            )
        packs[s][...] = total.astype(BF)


def nt(a, b):
    return lax.dot_general(a, b, (((1,), (1,)), ((), ())), preferred_element_type=F32)


def main_kernel(rows_ref, own_ref, par_ref, raw_ref):
    for side, ref in enumerate((own_ref, par_ref)):
        for g in range(2):
            raw_ref[2 * side + g, :, :] = nt(rows_ref[...], ref[g, :, :])


def down_kernel(spots, adapters, tile_ref, *refs):
    packs = refs[:spots]
    tag_ref, raw_ref = refs[spots], refs[spots + 1]
    lu_refs = refs[spots + 2 : spots + 4]
    dn_refs = refs[spots + 4 : spots + 6]
    outs = refs[spots + 6 :]
    lanes = packs[0].shape[1]
    low = packs[0][...].astype(F32)
    for s in range(1, spots):
        low = low + packs[s][...].astype(F32)
    spot = lax.broadcasted_iota(I32, (1, lanes), 1) // (2 * RANK)
    low = jnp.concatenate(
        [jnp.where(spot == p, low, 0.0).astype(BF) for p in range(spots)], axis=0
    )
    labels = tag_ref[:, 0:1].astype(F32)
    wide = adapters * RANK
    owner = (lax.broadcasted_iota(I32, (1, wide), 1) // RANK).astype(F32)
    mark = labels == owner
    spread = [
        jnp.where(
            mark, jnp.dot(low, tile_ref[g, :, :], preferred_element_type=F32), 0.0
        ).astype(BF)
        for g in range(2)
    ]
    total = None
    for side in range(2):
        act = [
            raw_ref[2 * side + g, :, :] + nt(spread[g], lu_refs[side][g, :, :])
            for g in range(2)
        ]
        hidden = (act[0] / (1.0 + jnp.exp(-act[0])) * act[1]).astype(BF)
        term = jnp.dot(hidden, dn_refs[side][...], preferred_element_type=F32)
        total = term if total is None else total + term
    start = 0
    for ref in outs:
        ref[...] = total[start : start + ref.shape[0], :].astype(BF)
        start += ref.shape[0]


def add_kernel(a_ref, b_ref, o_ref):
    o_ref[...] = (a_ref[...].astype(F32) + b_ref[...].astype(F32)).astype(BF)


def add_rows(a, b):
    return call(add_kernel, [shape(*a.shape)], (a, b), [VM, VM], a.size, "add_rows")[0]


def sum_kernel(s_ref, xl_ref, xh_ref, yl_ref, yh_ref, o_ref):
    half = xl_ref.shape[0]
    o_ref[:half, :] = (
        s_ref[:half, :].astype(F32) + xl_ref[...].astype(F32) + yl_ref[...].astype(F32)
    ).astype(BF)
    o_ref[half:, :] = (
        s_ref[half:, :].astype(F32) + xh_ref[...].astype(F32) + yh_ref[...].astype(F32)
    ).astype(BF)


def back_kernel(experts, capacity, z_ref, ids_ref, idc_ref, gw_ref, tok_ref, *refs):
    backs = refs[:-1]
    out_ref = refs[-1]
    local_tokens = tok_ref.shape[0]
    puts = one_hots(ids_ref, z_ref[0], experts, capacity, local_tokens)
    total = None
    for d in range(experts):
        scale = jnp.sum(
            jnp.where(idc_ref[...] == (z_ref[0] ^ d), gw_ref[...], 0.0), axis=1, keepdims=True
        )
        got = lax.dot_general(
            puts[d].astype(BF),
            backs[d][...],
            (((0,), (0,)), ((), ())),
            preferred_element_type=F32,
        )
        total = scale * got if total is None else total + scale * got
    out_ref[...] = (tok_ref[...].astype(F32) + total).astype(BF)


def positions(bits):
    out = [0]
    for b in bits:
        out = out + [p ^ b for p in out]
    return out


def after(values, deps):
    return lax.optimization_barrier((values, deps))[0]


def gather_first(own, bits):
    if len(bits) == 2:
        return own, swap(own, "dp", bits[0]), swap(own, "dp", bits[1])
    return (own,)


def gather_second(have, bits):
    if len(bits) == 2:
        own, px, py = have
        half = own.shape[0] // 2
        low = swap(px[:half], "dp", bits[1])
        high = swap(py[half:], "dp", bits[0])
        return (own, px, py, low, high), [1, 1, 1, 2]
    pieces = {0: have[0]}
    for b in bits:
        for p in list(pieces):
            pieces[p ^ b] = swap(pieces[p], "dp", b)
    return tuple(pieces[p] for p in positions(bits)), [1] * (2 ** len(bits))


def split_sizes(group, bits):
    if len(bits) == 2:
        half = group // 2
        return [group] + [half] * 6
    return [group] * (2 ** len(bits))


def reduce_first(parts, bits):
    if len(bits) == 2:
        bx, by = bits
        s0, xl, xh, yl, yh, dl, dh = parts
        gl = swap(dl, "dp", bx)
        gh = swap(dh, "dp", by)
        rxl = swap(xl, "dp", bx)
        ryh = swap(yh, "dp", by)
        return s0, rxl, add_rows(xh, gh), add_rows(yl, gl), ryh
    return tuple(parts)


def reduce_second(parts, bits):
    if len(bits) == 2:
        bx, by = bits
        s0, rxl, xh, yl, ryh = parts
        rxh = swap(xh, "dp", bx)
        ryl = swap(yl, "dp", by)
        return call(
            sum_kernel, [shape(*s0.shape)], (s0, rxl, rxh, ryl, ryh), [VM] * 5, s0.size, "sum_rows"
        )[0]
    table = dict(zip(positions(bits), parts))
    for b in reversed(bits):
        keep = [p for p in table if not p & b]
        table = {p: add_rows(table[p], swap(table[p ^ b], "dp", b)) for p in keep}
    return table[0]


def body(
    tokens,
    expert_ids,
    gate_weights,
    request_lengths,
    request_adapter,
    expert_weights,
    expert_down,
    low_down,
    low_up,
):
    experts = lax.axis_size("expert")
    n_dp = lax.axis_size("dp")
    local_tokens, width = tokens.shape
    capacity = local_tokens * TOP * 4 // (3 * experts)
    held = low_down.shape[2] // (2 * RANK)
    adapters = low_up.shape[2] // RANK
    units = expert_down.shape[1]
    bits = []
    b = 2
    while b < n_dp:
        bits.append(b)
        b *= 2
    pos = positions(bits)
    spots = len(pos)
    z = lax.axis_index("expert").astype(I32).reshape(1)
    me = lax.axis_index("dp").astype(I32).reshape(1)
    ids_t = expert_ids.T

    outgoing = call(
        functools.partial(front_kernel, experts, capacity),
        [shape(capacity, width + LANES)] * experts,
        (z, request_lengths, request_adapter, ids_t, tokens),
        [SM, SM, SM, VM, VM],
        2 * experts * capacity * local_tokens * width,
        "front",
    )
    arrived = [outgoing[0]] + [swap(outgoing[d], "expert", d) for d in range(1, experts)]

    wt_t = jnp.swapaxes(expert_weights[0], 1, 2)
    lu_t = jnp.swapaxes(low_up[0], 1, 2)
    ld = (low_down[0], swap(low_down[0], "dp", 1))
    wt = (wt_t, swap(wt_t, "dp", 1))
    lu = (lu_t, swap(lu_t, "dp", 1))
    dn = (expert_down[0], swap(expert_down[0], "dp", 1))
    lanes = 2 * RANK * spots
    fold = (
        jnp.arange(held * 2 * RANK)[:, None] % (2 * RANK) == jnp.arange(lanes)[None, :] % (2 * RANK)
    ).astype(BF)
    tile = jnp.stack(
        [
            (
                jnp.arange(lanes)[:, None] % (2 * RANK)
                == jnp.arange(adapters * RANK)[None, :] % RANK + g * RANK
            ).astype(BF)
            for g in range(2)
        ]
    )

    order = list(range(experts))
    first, second = {}, {}
    parts, done, adds = {}, {}, {}
    first[0] = gather_first(arrived[order[0]], bits)
    second[0] = gather_second(first[0], bits)
    first[1] = gather_first(arrived[order[1]], bits)
    raw = None
    for i, d in enumerate(order):
        pieces, counts = second[i]
        group = capacity
        count = group * spots
        if i == 0:
            pieces, ld, wt = after((pieces, ld, wt), ())
        else:
            pieces = after(pieces, parts[i - 1][0])
        got = call(
            functools.partial(proj_kernel, counts, held),
            [shape(count, width), shape(count, LANES)] + [shape(group, lanes)] * spots,
            (me, fold, *pieces, *ld),
            [SM] + [VM] * (len(pieces) + 3),
            4 * count * width * held * 2 * RANK,
            "project",
        )
        rows, tags, packs = got[0], got[1], got[2:]
        packs = [packs[0]] + [swap(packs[s], "dp", pos[s]) for s in range(1, spots)]
        if i == 0:
            rows, lu, dn = after((rows, lu, dn), ())
        raw = call(
            main_kernel,
            [jax.ShapeDtypeStruct((4, count, units), F32)],
            (rows, *wt),
            [VM] * 3,
            8 * count * width * units,
            "gate_up",
        )[0]
        deps = []
        if i + 1 < experts:
            second[i + 1] = gather_second(first[i + 1], bits)
            deps.append(first[i + 1])
        if i + 2 < experts:
            first[i + 2] = gather_first(arrived[order[i + 2]], bits)
        if i >= 1:
            adds[i - 1] = reduce_first(parts[i - 1], bits)
            deps.append(adds[i - 1])
        if i >= 2:
            done[i - 2] = reduce_second(adds[i - 2], bits)
            deps.append(done[i - 2])
        raw = after(raw, deps)
        parts[i] = call(
            functools.partial(down_kernel, spots, adapters),
            [shape(size, width) for size in split_sizes(group, bits)],
            (tile, *packs, tags, raw, *lu, *dn),
            [VM] * (spots + 7),
            8 * count * adapters * RANK * units + 4 * count * units * width,
            "down",
        )
    for i in range(experts):
        if i not in adds:
            adds[i] = reduce_first(parts[i], bits)
        if i not in done:
            done[i] = reduce_second(adds[i], bits)
    backs = [None] * experts
    for i, d in enumerate(order):
        backs[d] = done[i] if d == 0 else swap(done[i], "expert", d)

    return call(
        functools.partial(back_kernel, experts, capacity),
        [shape(local_tokens, width)],
        (z, ids_t, expert_ids, gate_weights, tokens, *backs),
        [SM] + [VM] * (4 + experts),
        2 * experts * capacity * local_tokens * width,
        "combine",
    )[0]


def solution(mesh):
    return jax.shard_map(
        body,
        mesh=mesh,
        in_specs=(
            P(("expert", "dp"), None),
            P(("expert", "dp"), None),
            P(("expert", "dp"), None),
            P(("expert", "dp"), None),
            P(("expert", "dp"), None),
            P("expert", None, None, "dp"),
            P("expert", "dp", None),
            P("expert", None, "dp"),
            P("expert", None, None, "dp"),
        ),
        out_specs=P(("expert", "dp"), None),
        check_vma=False,
    )
```

time: 320 us -> 188 us (0.59)
  waiting for transfers between devices: 174 us -> 36 us
  Pallas kernels: 0 us -> 66 us
  starting transfers between devices: 8.09 us -> 68.1 us
  matrix products: 59.4 us -> 0 us
  blocking collectives: 43.7 us -> 0 us
  between operations: 13.3 us -> 0.51 us
  other arithmetic: 10.7 us -> 1.08 us
  local copies, waits for them, and re-layouts: 10.3 us -> 15.1 us
    reduce_scatter x1 -> x0, waiting for transfers between devices: 76 us -> none  [body(): lax.psum_scatter(jnp.dot(hidden_activations, expert_down[0], preferred_el...]
    ppermute x0 -> x62, starting transfers between devices: none -> 68.1 us  [swap(): return lax.ppermute(x, axis, [(i, i ^ bit) for i in range(n)])]
    pallas_call x0 -> x26, Pallas kernels: none -> 66 us  [call(): pl.pallas_call(fn, out_shape=tuple(outs), in_specs=specs, out_specs=tuple...]
    dot_general x8 -> x0, matrix products: 59.4 us -> none  [the longest x1 18.9 us: body(): jnp.dot(hidden_activations, expert_down[0], preferred_element_type=jnp.fl...]
    all_gather x1 -> x0, waiting for transfers between devices: 38.1 us -> none  [body(): lax.all_gather(arrived.reshape(-1, width), 'dp', axis=0, tiled=True)]
    ppermute x0 -> x62, waiting for transfers between devices: none -> 36 us  [swap(): return lax.ppermute(x, axis, [(i, i ^ bit) for i in range(n)])]
    all_to_all x1 -> x0, blocking collectives: 34.8 us -> none  [body(): lax.all_to_all(outgoing, 'expert', split_axis=0, concat_axis=0, tiled=True)]
    all_to_all x2 -> x0, waiting for transfers between devices: 31.4 us -> none  [the longest x1 28.5 us: body(): lax.all_to_all(mine, 'expert', split_axis=0, concat_axis=0, tiled=True)]
  transfers between devices with their start and end apart: 5 -> 62, of which waited for: 5 -> 14; matrix products, arithmetic and copies ran while one was open for 9% -> 1% of each run, Pallas kernels for 0% -> 31%
where the time goes in v1:
time: 188 us; the launch traced here: 187 us
  starting transfers between devices  68.1 us (36%)
  Pallas kernels  66 us (35%)
  waiting for transfers between devices  36 us (19%)
  local copies, waits for them, and re-layouts  15.1 us (8%)
    ppermute x62, starting transfers between devices, swap(): return lax.ppermute(x, axis, [(i, i ^ bit) for i in range(n)])  68.1 us
    pallas_call x26, Pallas kernels, call(): pl.pallas_call(fn, out_shape=tuple(outs), in_specs=specs, out_specs=tuple...  66 us
    ppermute x62, waiting for transfers between devices, swap(): return lax.ppermute(x, axis, [(i, i ^ bit) for i in range(n)])  36 us
    unnamed x60, local copies, waits for them, and re-layouts  14.1 us
  transfers between devices with their start and end apart: 62, of which 14 were waited for; matrix products, arithmetic and copies ran while one was open for 1% of the time, Pallas kernels for 31%

profile of v1, /device:TPU:0, one launch (start us, length us, event | category | flops | bytes accessed | tf_op | source)
XLA Modules:
  0.0 186.7 jit_solution(936521548875739465)
XLA Ops:
  5.9 2.5 %collective-permute-start = (bf16[64,2432]{1,0:T(8,128)(2,1)S(1)}, bf16[64,2432]{1,0:T(8,128)(2,1)S(1)}, u32[]{:S(2)}, u32[]{:S(2)}) collective-permute-start(bf16[64,2432]{1,0:T(8,128)(2,1)S(1)} %get-tuple-element.95.refs_0_), channel_id=1, source_target_pairs={{0,2},{1,3},{2,0},{3,1},{4,6},{5,7},{6,4},{7,5},{8,10},{9,11},{10,... | collective-permute-start | bytes 933896 | tf_op jit(solution)/shard_map/ppermute | solution.py:22
  10.6 5.8 %collective-permute-done.refs_1_ = bf16[64,2432]{1,0:T(8,128)(2,1)S(1)} collective-permute-done((bf16[64,2432]{1,0:T(8,128)(2,1)S(1)}, bf16[64,2432]{1,0:T(8,128)(2,1)S(1)}, u32[]{:S(2)}, u32[]{:S(2)}) %collective-permute-start) | collective-permute-done | bytes 311328 | tf_op jit(solution)/shard_map/ppermute | solution.py:22
  20.2 6.5 %collective-permute-done.11.refs_0_ = bf16[64,2432]{1,0:T(8,128)(2,1)} collective-permute-done((bf16[64,2432]{1,0:T(8,128)(2,1)S(1)}, bf16[64,2432]{1,0:T(8,128)(2,1)}, u32[]{:S(2)}, u32[]{:S(2)}) %collective-permute-start.11) | collective-permute-done | bytes 311328 | tf_op jit(solution)/shard_map/ppermute | solution.py:22
  28.2 3.7 %collective-permute-done.2.refs_3_ = bf16[32,2432]{1,0:T(8,128)(2,1)S(1)} collective-permute-done((bf16[32,2432]{1,0:T(8,128)(2,1)S(1)}, bf16[32,2432]{1,0:T(8,128)(2,1)S(1)}, u32[]{:S(2)}, u32[]{:S(2)}) %collective-permute-start.2) | collective-permute-done | bytes 155680 | tf_op jit(solution)/shard_map/ppermute | solution.py:22
  31.9 1.7 collective-permute-start.3
  34.6 2.6 %collective-permute-done.3.refs_4_ = bf16[32,2432]{1,0:T(8,128)(2,1)S(1)} collective-permute-done((bf16[32,2432]{1,0:T(8,128)(2,1)S(1)}, bf16[32,2432]{1,0:T(8,128)(2,1)S(1)}, u32[]{:S(2)}, u32[]{:S(2)}) %collective-permute-start.3) | collective-permute-done | bytes 155680 | tf_op jit(solution)/shard_map/ppermute | solution.py:22
  37.8 1.7 collective-permute-start.12
  39.5 2.4 %collective-permute-start.25 = (bf16[64,2432]{1,0:T(8,128)(2,1)}, bf16[64,2432]{1,0:T(8,128)(2,1)S(1)}, u32[]{:S(2)}, u32[]{:S(2)}) collective-permute-start(bf16[64,2432]{1,0:T(8,128)(2,1)} %copy-done.23), channel_id=1, source_target_pairs={{0,16},{8,24},{16,0},{24,8},{1,17},{9,25},{17,1},{25,9},{2,18},{10... | collective-permute-start | bytes 933896 | tf_op jit(solution)/shard_map/ppermute | solution.py:22
  48.7 2.3 %project.4 = (bf16[256,2304]{1,0:T(8,128)(2,1)S(1)}, bf16[256,128]{1,0:T(8,128)(2,1)S(1)}, bf16[64,128]{1,0:T(8,128)(2,1)S(1)}, bf16[64,128]{1,0:T(8,128)(2,1)S(...) custom-call(s32[1]{0:T(128)} %bitcast.2.me_ref, bf16[256,128]{1,0:T(8,128)(2,1)S(1)} %compare_convert_fusion.fold_ref, ...), custom_call_target="tpu_custom_call" | custom-call | flops 603979776 | bytes 4980740 | tf_op jit(solution)/shard_map/project/pallas_call | solution.py:29
  53.9 3.1 %collective-permute-start.40 = (bf16[64,2432]{1,0:T(8,128)(2,1)S(1)}, bf16[64,2432]{1,0:T(8,128)(2,1)S(1)}, u32[]{:S(2)}, u32[]{:S(2)}) collective-permute-start(bf16[64,2432]{1,0:T(8,128)(2,1)S(1)} %copy-done.22), channel_id=1, source_target_pairs={{0,24},{8,16},{16,8},{24,0},{1,25},{9,17},{17,9},{25,1},{2,26},{10... | collective-permute-start | bytes 933896 | tf_op jit(solution)/shard_map/ppermute | solution.py:22
  57.5 1.6 collective-permute-start.27
  59.6 2.5 %collective-permute-start.8 = (bf16[64,128]{1,0:T(8,128)(2,1)S(1)}, bf16[64,128]{1,0:T(8,128)(2,1)S(1)}, u32[]{:S(2)}, u32[]{:S(2)}) collective-permute-start(bf16[64,128]{1,0:T(8,128)(2,1)S(1)} %get-tuple-element.105), channel_id=1, source_target_pairs={{0,6},{1,7},{2,4},{3,5},{4,2},{5,3},{6,0},{7,1},{8,14},{9,15},{10,... | collective-permute-start | bytes 49160 | tf_op jit(solution)/shard_map/ppermute | solution.py:22
  62.1 2.9 %copy-done = bf16[1,2,2304,720]{2,3,1,0:T(8,128)(2,1)S(1)} copy-done((bf16[1,2,2304,720]{2,3,1,0:T(8,128)(2,1)S(1)}, bf16[1,2,2304,720]{2,3,1,0:T(8,128)(2,1)}, u32[]{:S(2)}) %copy-start) | copy-done | bytes 6635544
  65.0 6.9 %gate_up.4.refs_5_ = f32[4,256,720]{2,1,0:T(8,128)S(1)} custom-call(bf16[256,2304]{1,0:T(8,128)(2,1)S(1)} %get-tuple-element.108.rows_ref, bf16[2,720,2304]{2,1,0:T(8,128)(2,1)S(1)} %bitcast.12, bf16[2,720,2304]{2,1,0:T(8,128)(2,1)} %collective-permute-done.5.par_ref), custom_call_target="tpu_custom_call" | custom-call | flops 3397386240 | bytes 17399808 | tf_op jit(solution)/shard_map/gate_up/pallas_call | solution.py:29
  73.0 6.4 %down.4 = (bf16[64,2304]{1,0:T(8,128)(2,1)S(1)}, bf16[32,2304]{1,0:T(8,128)(2,1)S(1)}, bf16[32,2304]{1,0:T(8,128)(2,1)S(1)}, bf16[32,2304]{1,0:T(8,128)(2,1)S(1)...) custom-call(bf16[2,128,1024]{2,1,0:T(8,128)(2,1)S(1)} %add_convert_fusion.tile_ref, ...), custom_call_target="tpu_custom_call" | custom-call | flops 3208642560 | bytes 17317888 | tf_op jit(solution)/shard_map/down/pallas_call | solution.py:29
  79.4 1.6 collective-permute-start.14
  83.6 1.6 collective-permute-start.41
  85.2 2.5 %project.5 = (bf16[256,2304]{1,0:T(8,128)(2,1)S(1)}, bf16[256,128]{1,0:T(8,128)(2,1)S(1)}, bf16[64,128]{1,0:T(8,128)(2,1)S(1)}, bf16[64,128]{1,0:T(8,128)(2,1)S(...) custom-call(s32[1]{0:T(128)} %bitcast.2.me_ref, bf16[256,128]{1,0:T(8,128)(2,1)S(1)} %compare_convert_fusion.fold_ref, ...), custom_call_target="tpu_custom_call" | custom-call | flops 603979776 | bytes 4980740 | tf_op jit(solution)/shard_map/project/pallas_call | solution.py:29
  90.9 1.8 collective-permute-start.24
  92.7 6.9 %gate_up.5.refs_5_ = f32[4,256,720]{2,1,0:T(8,128)S(1)} custom-call(bf16[256,2304]{1,0:T(8,128)(2,1)S(1)} %get-tuple-element.134.rows_ref, bf16[2,720,2304]{2,1,0:T(8,128)(2,1)S(1)} %bitcast.15, bf16[2,720,2304]{2,1,0:T(8,128)(2,1)} %collective-permute-done.5.par_ref), custom_call_target="tpu_custom_call" | custom-call | flops 3397386240 | bytes 17399808 | tf_op jit(solution)/shard_map/gate_up/pallas_call | solution.py:29
  103.0 6.2 %down.5 = (bf16[64,2304]{1,0:T(8,128)(2,1)S(1)}, bf16[32,2304]{1,0:T(8,128)(2,1)S(1)}, bf16[32,2304]{1,0:T(8,128)(2,1)S(1)}, bf16[32,2304]{1,0:T(8,128)(2,1)S(1)...) custom-call(bf16[2,128,1024]{2,1,0:T(8,128)(2,1)S(1)} %add_convert_fusion.tile_ref, ...), custom_call_target="tpu_custom_call" | custom-call | flops 3208642560 | bytes 17317888 | tf_op jit(solution)/shard_map/down/pallas_call | solution.py:29
  111.9 1.6 collective-permute-start.28
  113.5 2.3 %project.6 = (bf16[256,2304]{1,0:T(8,128)(2,1)S(1)}, bf16[256,128]{1,0:T(8,128)(2,1)S(1)}, bf16[64,128]{1,0:T(8,128)(2,1)S(1)}, bf16[64,128]{1,0:T(8,128)(2,1)S(...) custom-call(s32[1]{0:T(128)} %bitcast.2.me_ref, bf16[256,128]{1,0:T(8,128)(2,1)S(1)} %compare_convert_fusion.fold_ref, ...), custom_call_target="tpu_custom_call" | custom-call | flops 603979776 | bytes 4980740 | tf_op jit(solution)/shard_map/project/pallas_call | solution.py:29
  118.4 1.8 collective-permute-start.39
  120.2 6.7 %gate_up.6.refs_5_ = f32[4,256,720]{2,1,0:T(8,128)S(1)} custom-call(bf16[256,2304]{1,0:T(8,128)(2,1)S(1)} %get-tuple-element.154.rows_ref, bf16[2,720,2304]{2,1,0:T(8,128)(2,1)S(1)} %bitcast.16, bf16[2,720,2304]{2,1,0:T(8,128)(2,1)} %collective-permute-done.5.par_ref), custom_call_target="tpu_custom_call" | custom-call | flops 3397386240 | bytes 17399808 | tf_op jit(solution)/shard_map/gate_up/pallas_call | solution.py:29
  131.3 6.4 %down.6 = (bf16[64,2304]{1,0:T(8,128)(2,1)S(1)}, bf16[32,2304]{1,0:T(8,128)(2,1)S(1)}, bf16[32,2304]{1,0:T(8,128)(2,1)S(1)}, bf16[32,2304]{1,0:T(8,128)(2,1)S(1)...) custom-call(bf16[2,128,1024]{2,1,0:T(8,128)(2,1)S(1)} %add_convert_fusion.tile_ref, ...), custom_call_target="tpu_custom_call" | custom-call | flops 3208642560 | bytes 17317888 | tf_op jit(solution)/shard_map/down/pallas_call | solution.py:29
  141.0 2.3 %project.7 = (bf16[256,2304]{1,0:T(8,128)(2,1)S(1)}, bf16[256,128]{1,0:T(8,128)(2,1)S(1)}, bf16[64,128]{1,0:T(8,128)(2,1)S(1)}, bf16[64,128]{1,0:T(8,128)(2,1)S(...) custom-call(s32[1]{0:T(128)} %bitcast.2.me_ref, bf16[256,128]{1,0:T(8,128)(2,1)S(1)} %compare_convert_fusion.fold_ref, ...), custom_call_target="tpu_custom_call" | custom-call | flops 603979776 | bytes 4980740 | tf_op jit(solution)/shard_map/project/pallas_call | solution.py:29
  145.9 1.8 collective-permute-start.54
  147.7 6.7 %gate_up.7.refs_5_ = f32[4,256,720]{2,1,0:T(8,128)S(1)} custom-call(bf16[256,2304]{1,0:T(8,128)(2,1)S(1)} %get-tuple-element.174.rows_ref, bf16[2,720,2304]{2,1,0:T(8,128)(2,1)S(1)} %bitcast.17, bf16[2,720,2304]{2,1,0:T(8,128)(2,1)} %collective-permute-done.5.par_ref), custom_call_target="tpu_custom_call" | custom-call | flops 3397386240 | bytes 17399808 | tf_op jit(solution)/shard_map/gate_up/pallas_call | solution.py:29
  155.4 6.2 %down.7 = (bf16[64,2304]{1,0:T(8,128)(2,1)S(1)}, bf16[32,2304]{1,0:T(8,128)(2,1)S(1)}, bf16[32,2304]{1,0:T(8,128)(2,1)S(1)}, bf16[32,2304]{1,0:T(8,128)(2,1)S(1)...) custom-call(bf16[2,128,1024]{2,1,0:T(8,128)(2,1)S(1)} %add_convert_fusion.tile_ref, ...), custom_call_target="tpu_custom_call" | custom-call | flops 3208642560 | bytes 17317888 | tf_op jit(solution)/shard_map/down/pallas_call | solution.py:29
  175.5 2.9 %collective-permute-done.34.refs_1_ = bf16[64,2304]{1,0:T(8,128)(2,1)S(1)} collective-permute-done((bf16[64,2304]{1,0:T(8,128)(2,1)}, bf16[64,2304]{1,0:T(8,128)(2,1)S(1)}, u32[]{:S(2)}, u32[]{:S(2)}) %collective-permute-start.34) | collective-permute-done | bytes 294944 | tf_op jit(solution)/shard_map/ppermute | solution.py:22
  178.4 6.8 %collective-permute-done.49.refs_2_ = bf16[64,2304]{1,0:T(8,128)(2,1)S(1)} collective-permute-done((bf16[64,2304]{1,0:T(8,128)(2,1)S(1)}, bf16[64,2304]{1,0:T(8,128)(2,1)S(1)}, u32[]{:S(2)}, u32[]{:S(2)}) %collective-permute-start.49) | collective-permute-done | bytes 294944 | tf_op jit(solution)/shard_map/ppermute | solution.py:22
  (193 shorter events, 67.7 us)
Async XLA Ops:
  0.0 41.9 %collective-permute-start.5 = (bf16[2,720,2304]{2,1,0:T(8,128)(2,1)}, bf16[2,720,2304]{2,1,0:T(8,128)(2,1)}, u32[]{:S(2)}, u32[]{:S(2)}) collective-permute-start(bf16[2,720,2304]{2,1,0:T(8,128)(2,1)} %bitcast.11), channel_id=1, source_target_pairs={{0,1},{1,0},{2,3},{3,2},{4,5},{5,4},{6,7},{7,6},{8,9},{9,8},{10,11... | collective-permute-start | bytes 19906568 | tf_op jit(solution)/shard_map/ppermute | solution.py:22
  0.5 58.6 %collective-permute-start.10 = (bf16[720,2304]{1,0:T(8,128)(2,1)}, bf16[720,2304]{1,0:T(8,128)(2,1)S(1)}, u32[]{:S(2)}, u32[]{:S(2)}) collective-permute-start(bf16[720,2304]{1,0:T(8,128)(2,1)} %bitcast.18), channel_id=1, source_target_pairs={{0,1},{1,0},{2,3},{3,2},{4,5},{5,4},{6,7},{7,6},{8,9},{9,8},{10,11... | collective-permute-start | bytes 9953288 | tf_op jit(solution)/shard_map/ppermute | solution.py:22
  0.5 57.0 %collective-permute-start.9 = (bf16[2,720,1024]{2,1,0:T(8,128)(2,1)}, bf16[2,720,1024]{2,1,0:T(8,128)(2,1)}, u32[]{:S(2)}, u32[]{:S(2)}) collective-permute-start(bf16[2,720,1024]{2,1,0:T(8,128)(2,1)} %bitcast.23), channel_id=1, source_target_pairs={{0,1},{1,0},{2,3},{3,2},{4,5},{5,4},{6,7},{7,6},{8,9},{9,8},{10,11... | collective-permute-start | bytes 8847368 | tf_op jit(solution)/shard_map/ppermute | solution.py:22
  16.4 23.1 %collective-permute-start.4 = (bf16[2304,256]{1,0:T(8,128)(2,1)}, bf16[2304,256]{1,0:T(8,128)(2,1)}, u32[]{:S(2)}, u32[]{:S(2)}) collective-permute-start(bf16[2304,256]{1,0:T(8,128)(2,1)} %bitcast.28), channel_id=1, source_target_pairs={{0,1},{1,0},{2,3},{3,2},{4,5},{5,4},{6,7},{7,6},{8,9},{9,8},{10,11... | collective-permute-start | bytes 3538952 | tf_op jit(solution)/shard_map/ppermute | solution.py:22
  37.8 13.2 %collective-permute-start.12 = (bf16[64,2432]{1,0:T(8,128)(2,1)}, bf16[64,2432]{1,0:T(8,128)(2,1)}, u32[]{:S(2)}, u32[]{:S(2)}) collective-permute-start(bf16[64,2432]{1,0:T(8,128)(2,1)} %collective-permute-done.11.refs_0_), channel_id=1, source_target_pairs={{0,2},{1,3},{2,0},{3,1},{4,6},{5,7},{6,4},{7,5},{8,10},{9,11},{10,... | collective-permute-start | bytes 933896 | tf_op jit(solution)/shard_map/ppermute | solution.py:22
  39.5 14.4 %collective-permute-start.25 = (bf16[64,2432]{1,0:T(8,128)(2,1)}, bf16[64,2432]{1,0:T(8,128)(2,1)S(1)}, u32[]{:S(2)}, u32[]{:S(2)}) collective-permute-start(bf16[64,2432]{1,0:T(8,128)(2,1)} %copy-done.23), channel_id=1, source_target_pairs={{0,16},{8,24},{16,0},{24,8},{1,17},{9,25},{17,1},{25,9},{2,18},{10... | collective-permute-start | bytes 933896 | tf_op jit(solution)/shard_map/ppermute | solution.py:22
  41.9 15.0 %collective-permute-start.13 = (bf16[64,2432]{1,0:T(8,128)(2,1)}, bf16[64,2432]{1,0:T(8,128)(2,1)S(1)}, u32[]{:S(2)}, u32[]{:S(2)}) collective-permute-start(bf16[64,2432]{1,0:T(8,128)(2,1)} %collective-permute-done.11.refs_0_), channel_id=1, source_target_pairs={{0,4},{1,5},{2,6},{3,7},{4,0},{5,1},{6,2},{7,3},{8,12},{9,13},{10,... | collective-permute-start | bytes 933896 | tf_op jit(solution)/shard_map/ppermute | solution.py:22
  53.9 25.5 %collective-permute-start.40 = (bf16[64,2432]{1,0:T(8,128)(2,1)S(1)}, bf16[64,2432]{1,0:T(8,128)(2,1)S(1)}, u32[]{:S(2)}, u32[]{:S(2)}) collective-permute-start(bf16[64,2432]{1,0:T(8,128)(2,1)S(1)} %copy-done.22), channel_id=1, source_target_pairs={{0,24},{8,16},{16,8},{24,0},{1,25},{9,17},{17,9},{25,1},{2,26},{10... | collective-permute-start | bytes 933896 | tf_op jit(solution)/shard_map/ppermute | solution.py:22
  57.0 24.0 %collective-permute-start.26 = (bf16[64,2432]{1,0:T(8,128)(2,1)S(1)}, bf16[64,2432]{1,0:T(8,128)(2,1)S(1)}, u32[]{:S(2)}, u32[]{:S(2)}) collective-permute-start(bf16[64,2432]{1,0:T(8,128)(2,1)S(1)} %collective-permute-done.25.refs_0_), channel_id=1, source_target_pairs={{0,2},{1,3},{2,0},{3,1},{4,6},{5,7},{6,4},{7,5},{8,10},{9,11},{10,... | collective-permute-start | bytes 933896 | tf_op jit(solution)/shard_map/ppermute | solution.py:22
  57.5 25.0 %collective-permute-start.27 = (bf16[64,2432]{1,0:T(8,128)(2,1)S(1)}, bf16[64,2432]{1,0:T(8,128)(2,1)S(1)}, u32[]{:S(2)}, u32[]{:S(2)}) collective-permute-start(bf16[64,2432]{1,0:T(8,128)(2,1)S(1)} %collective-permute-done.25.refs_0_), channel_id=1, source_target_pairs={{0,4},{1,5},{2,6},{3,7},{4,0},{5,1},{6,2},{7,3},{8,12},{9,13},{10,... | collective-permute-start | bytes 933896 | tf_op jit(solution)/shard_map/ppermute | solution.py:22
  59.1 12.8 %collective-permute-start.7 = (bf16[64,128]{1,0:T(8,128)(2,1)S(1)}, bf16[64,128]{1,0:T(8,128)(2,1)S(1)}, u32[]{:S(2)}, u32[]{:S(2)}) collective-permute-start(bf16[64,128]{1,0:T(8,128)(2,1)S(1)} %get-tuple-element.104), channel_id=1, source_target_pairs={{0,4},{1,5},{2,6},{3,7},{4,0},{5,1},{6,2},{7,3},{8,12},{9,13},{10,... | collective-permute-start | bytes 49160 | tf_op jit(solution)/shard_map/ppermute | solution.py:22
  59.6 12.8 %collective-permute-start.8 = (bf16[64,128]{1,0:T(8,128)(2,1)S(1)}, bf16[64,128]{1,0:T(8,128)(2,1)S(1)}, u32[]{:S(2)}, u32[]{:S(2)}) collective-permute-start(bf16[64,128]{1,0:T(8,128)(2,1)S(1)} %get-tuple-element.105), channel_id=1, source_target_pairs={{0,6},{1,7},{2,4},{3,5},{4,2},{5,3},{6,0},{7,1},{8,14},{9,15},{10,... | collective-permute-start | bytes 49160 | tf_op jit(solution)/shard_map/ppermute | solution.py:22
  71.9 11.1 %collective-permute-start.20 = (bf16[32,2432]{1,0:T(8,128)(2,1)S(1)}, bf16[32,2432]{1,0:T(8,128)(2,1)S(1)}, u32[]{:S(2)}, u32[]{:S(2)}) collective-permute-start(bf16[32,2432]{1,0:T(8,128)(2,1)S(1)} %slice.34), channel_id=1, source_target_pairs={{0,4},{1,5},{2,6},{3,7},{4,0},{5,1},{6,2},{7,3},{8,12},{9,13},{10,... | collective-permute-start | bytes 466952 | tf_op jit(solution)/shard_map/ppermute | solution.py:22
  72.4 11.1 %collective-permute-start.21 = (bf16[32,2432]{1,0:T(8,128)(2,1)S(1)}, bf16[32,2432]{1,0:T(8,128)(2,1)S(1)}, u32[]{:S(2)}, u32[]{:S(2)}) collective-permute-start(bf16[32,2432]{1,0:T(8,128)(2,1)S(1)} %slice.35), channel_id=1, source_target_pairs={{0,2},{1,3},{2,0},{3,1},{4,6},{5,7},{6,4},{7,5},{8,10},{9,11},{10,... | collective-permute-start | bytes 466952 | tf_op jit(solution)/shard_map/ppermute | solution.py:22
  83.6 25.7 %collective-permute-start.41 = (bf16[64,2432]{1,0:T(8,128)(2,1)S(1)}, bf16[64,2432]{1,0:T(8,128)(2,1)S(1)}, u32[]{:S(2)}, u32[]{:S(2)}) collective-permute-start(bf16[64,2432]{1,0:T(8,128)(2,1)S(1)} %collective-permute-done.40.refs_0_), channel_id=1, source_target_pairs={{0,2},{1,3},{2,0},{3,1},{4,6},{5,7},{6,4},{7,5},{8,10},{9,11},{10,... | collective-permute-start | bytes 933896 | tf_op jit(solution)/shard_map/ppermute | solution.py:22
  87.6 22.5 %collective-permute-start.42 = (bf16[64,2432]{1,0:T(8,128)(2,1)S(1)}, bf16[64,2432]{1,0:T(8,128)(2,1)S(1)}, u32[]{:S(2)}, u32[]{:S(2)}) collective-permute-start(bf16[64,2432]{1,0:T(8,128)(2,1)S(1)} %collective-permute-done.40.refs_0_), channel_id=1, source_target_pairs={{0,4},{1,5},{2,6},{3,7},{4,0},{5,1},{6,2},{7,3},{8,12},{9,13},{10,... | collective-permute-start | bytes 933896 | tf_op jit(solution)/shard_map/ppermute | solution.py:22
  89.7 11.3 %collective-permute-start.23 = (bf16[64,128]{1,0:T(8,128)(2,1)S(1)}, bf16[64,128]{1,0:T(8,128)(2,1)S(1)}, u32[]{:S(2)}, u32[]{:S(2)}) collective-permute-start(bf16[64,128]{1,0:T(8,128)(2,1)S(1)} %get-tuple-element.131), channel_id=1, source_target_pairs={{0,4},{1,5},{2,6},{3,7},{4,0},{5,1},{6,2},{7,3},{8,12},{9,13},{10,... | collective-permute-start | bytes 49160 | tf_op jit(solution)/shard_map/ppermute | solution.py:22
  99.7 11.6 %collective-permute-start.35 = (bf16[32,2432]{1,0:T(8,128)(2,1)S(1)}, bf16[32,2432]{1,0:T(8,128)(2,1)S(1)}, u32[]{:S(2)}, u32[]{:S(2)}) collective-permute-start(bf16[32,2432]{1,0:T(8,128)(2,1)S(1)} %slice.36), channel_id=1, source_target_pairs={{0,4},{1,5},{2,6},{3,7},{4,0},{5,1},{6,2},{7,3},{8,12},{9,13},{10,... | collective-permute-start | bytes 466952 | tf_op jit(solution)/shard_map/ppermute | solution.py:22
  101.5 14.3 %collective-permute-start.16 = (bf16[32,2304]{1,0:T(8,128)(2,1)S(1)}, bf16[32,2304]{1,0:T(8,128)(2,1)S(1)}, u32[]{:S(2)}, u32[]{:S(2)}) collective-permute-start(bf16[32,2304]{1,0:T(8,128)(2,1)S(1)} %add_rows.8), channel_id=1, source_target_pairs={{0,2},{1,3},{2,0},{3,1},{4,6},{5,7},{6,4},{7,5},{8,10},{9,11},{10,... | collective-permute-start | bytes 442376 | tf_op jit(solution)/shard_map/ppermute | solution.py:22
  111.9 15.2 %collective-permute-start.28 = (bf16[32,2304]{1,0:T(8,128)(2,1)S(1)}, bf16[32,2304]{1,0:T(8,128)(2,1)S(1)}, u32[]{:S(2)}, u32[]{:S(2)}) collective-permute-start(bf16[32,2304]{1,0:T(8,128)(2,1)S(1)} %get-tuple-element.138), channel_id=1, source_target_pairs={{0,2},{1,3},{2,0},{3,1},{4,6},{5,7},{6,4},{7,5},{8,10},{9,11},{10,... | collective-permute-start | bytes 442376 | tf_op jit(solution)/shard_map/ppermute | solution.py:22
  115.8 12.6 %collective-permute-start.33 = (bf16[32,2304]{1,0:T(8,128)(2,1)S(1)}, bf16[32,2304]{1,0:T(8,128)(2,1)S(1)}, u32[]{:S(2)}, u32[]{:S(2)}) collective-permute-start(bf16[32,2304]{1,0:T(8,128)(2,1)S(1)} %get-tuple-element.143), channel_id=1, source_target_pairs={{0,4},{1,5},{2,6},{3,7},{4,0},{5,1},{6,2},{7,3},{8,12},{9,13},{10,... | collective-permute-start | bytes 442376 | tf_op jit(solution)/shard_map/ppermute | solution.py:22
  116.7 12.2 %collective-permute-start.37 = (bf16[64,128]{1,0:T(8,128)(2,1)S(1)}, bf16[64,128]{1,0:T(8,128)(2,1)S(1)}, u32[]{:S(2)}, u32[]{:S(2)}) collective-permute-start(bf16[64,128]{1,0:T(8,128)(2,1)S(1)} %get-tuple-element.150), channel_id=1, source_target_pairs={{0,2},{1,3},{2,0},{3,1},{4,6},{5,7},{6,4},{7,5},{8,10},{9,11},{10,... | collective-permute-start | bytes 49160 | tf_op jit(solution)/shard_map/ppermute | solution.py:22
  117.2 13.3 %collective-permute-start.38 = (bf16[64,128]{1,0:T(8,128)(2,1)S(1)}, bf16[64,128]{1,0:T(8,128)(2,1)S(1)}, u32[]{:S(2)}, u32[]{:S(2)}) collective-permute-start(bf16[64,128]{1,0:T(8,128)(2,1)S(1)} %get-tuple-element.151), channel_id=1, source_target_pairs={{0,4},{1,5},{2,6},{3,7},{4,0},{5,1},{6,2},{7,3},{8,12},{9,13},{10,... | collective-permute-start | bytes 49160 | tf_op jit(solution)/shard_map/ppermute | solution.py:22
  118.4 12.9 %collective-permute-start.39 = (bf16[64,128]{1,0:T(8,128)(2,1)S(1)}, bf16[64,128]{1,0:T(8,128)(2,1)S(1)}, u32[]{:S(2)}, u32[]{:S(2)}) collective-permute-start(bf16[64,128]{1,0:T(8,128)(2,1)S(1)} %get-tuple-element.152), channel_id=1, source_target_pairs={{0,6},{1,7},{2,4},{3,5},{4,2},{5,3},{6,0},{7,1},{8,14},{9,15},{10,... | collective-permute-start | bytes 49160 | tf_op jit(solution)/shard_map/ppermute | solution.py:22
  127.1 11.9 %collective-permute-start.50 = (bf16[32,2432]{1,0:T(8,128)(2,1)S(1)}, bf16[32,2432]{1,0:T(8,128)(2,1)S(1)}, u32[]{:S(2)}, u32[]{:S(2)}) collective-permute-start(bf16[32,2432]{1,0:T(8,128)(2,1)S(1)} %slice.38), channel_id=1, source_target_pairs={{0,4},{1,5},{2,6},{3,7},{4,0},{5,1},{6,2},{7,3},{8,12},{9,13},{10,... | collective-permute-start | bytes 466952 | tf_op jit(solution)/shard_map/ppermute | solution.py:22
  128.4 11.1 %collective-permute-start.51 = (bf16[32,2432]{1,0:T(8,128)(2,1)S(1)}, bf16[32,2432]{1,0:T(8,128)(2,1)S(1)}, u32[]{:S(2)}, u32[]{:S(2)}) collective-permute-start(bf16[32,2432]{1,0:T(8,128)(2,1)S(1)} %slice.39), channel_id=1, source_target_pairs={{0,2},{1,3},{2,0},{3,1},{4,6},{5,7},{6,4},{7,5},{8,10},{9,11},{10,... | collective-permute-start | bytes 466952 | tf_op jit(solution)/shard_map/ppermute | solution.py:22
  128.9 14.4 %collective-permute-start.30 = (bf16[32,2304]{1,0:T(8,128)(2,1)S(1)}, bf16[32,2304]{1,0:T(8,128)(2,1)S(1)}, u32[]{:S(2)}, u32[]{:S(2)}) collective-permute-start(bf16[32,2304]{1,0:T(8,128)(2,1)S(1)} %add_rows.10), channel_id=1, source_target_pairs={{0,2},{1,3},{2,0},{3,1},{4,6},{5,7},{6,4},{7,5},{8,10},{9,11},{10,... | collective-permute-start | bytes 442376 | tf_op jit(solution)/shard_map/ppermute | solution.py:22
  130.4 13.8 %collective-permute-start.32 = (bf16[32,2304]{1,0:T(8,128)(2,1)S(1)}, bf16[32,2304]{1,0:T(8,128)(2,1)S(1)}, u32[]{:S(2)}, u32[]{:S(2)}) collective-permute-start(bf16[32,2304]{1,0:T(8,128)(2,1)S(1)} %add_rows.11), channel_id=1, source_target_pairs={{0,4},{1,5},{2,6},{3,7},{4,0},{5,1},{6,2},{7,3},{8,12},{9,13},{10,... | collective-permute-start | bytes 442376 | tf_op jit(solution)/shard_map/ppermute | solution.py:22
  139.5 15.8 %collective-permute-start.43 = (bf16[32,2304]{1,0:T(8,128)(2,1)S(1)}, bf16[32,2304]{1,0:T(8,128)(2,1)S(1)}, u32[]{:S(2)}, u32[]{:S(2)}) collective-permute-start(bf16[32,2304]{1,0:T(8,128)(2,1)S(1)} %get-tuple-element.158), channel_id=1, source_target_pairs={{0,2},{1,3},{2,0},{3,1},{4,6},{5,7},{6,4},{7,5},{8,10},{9,11},{10,... | collective-permute-start | bytes 442376 | tf_op jit(solution)/shard_map/ppermute | solution.py:22
  143.3 12.0 %collective-permute-start.48 = (bf16[32,2304]{1,0:T(8,128)(2,1)S(1)}, bf16[32,2304]{1,0:T(8,128)(2,1)S(1)}, u32[]{:S(2)}, u32[]{:S(2)}) collective-permute-start(bf16[32,2304]{1,0:T(8,128)(2,1)S(1)} %get-tuple-element.163), channel_id=1, source_target_pairs={{0,4},{1,5},{2,6},{3,7},{4,0},{5,1},{6,2},{7,3},{8,12},{9,13},{10,... | collective-permute-start | bytes 442376 | tf_op jit(solution)/shard_map/ppermute | solution.py:22
  144.2 11.1 %collective-permute-start.52 = (bf16[64,128]{1,0:T(8,128)(2,1)S(1)}, bf16[64,128]{1,0:T(8,128)(2,1)S(1)}, u32[]{:S(2)}, u32[]{:S(2)}) collective-permute-start(bf16[64,128]{1,0:T(8,128)(2,1)S(1)} %get-tuple-element.170), channel_id=1, source_target_pairs={{0,2},{1,3},{2,0},{3,1},{4,6},{5,7},{6,4},{7,5},{8,10},{9,11},{10,... | collective-permute-start | bytes 49160 | tf_op jit(solution)/shard_map/ppermute | solution.py:22
  171.2 13.9 %collective-permute-start.49 = (bf16[64,2304]{1,0:T(8,128)(2,1)S(1)}, bf16[64,2304]{1,0:T(8,128)(2,1)S(1)}, u32[]{:S(2)}, u32[]{:S(2)}) collective-permute-start(bf16[64,2304]{1,0:T(8,128)(2,1)S(1)} %sum_rows.6), channel_id=1, source_target_pairs={{0,16},{8,24},{16,0},{24,8},{1,17},{9,25},{17,1},{25,9},{2,18},{10... | collective-permute-start | bytes 884744 | tf_op jit(solution)/shard_map/ppermute | solution.py:22
  (59 other events, 447.4 us)

commit v2 on v1

v2 whole, which is shorter than its diff:
```python
import functools

import jax
import jax.numpy as jnp
from jax import lax
from jax.experimental import pallas as pl
from jax.experimental.pallas import tpu as pltpu
from jax.sharding import PartitionSpec as P

TOP = 2
RANK = 16
LANES = 128
COST = 16
BF = jnp.bfloat16
F32 = jnp.float32
I32 = jnp.int32
VM = pl.BlockSpec(memory_space=pltpu.VMEM)
SM = pl.BlockSpec(memory_space=pltpu.SMEM)
ANY = pl.BlockSpec(memory_space=pltpu.HBM)


def swap(x, axis, bit):
    n = lax.axis_size(axis)
    return lax.ppermute(x, axis, [(i, i ^ bit) for i in range(n)])


def spot_mask(index, spot, bits):
    turn = index & 1 if len(bits) == 2 else 0
    mask = 0
    for j in range(len(bits)):
        if spot >> j & 1:
            mask ^= bits[j ^ turn]
    return mask


def hop(x, spot, bits):
    n = lax.axis_size("dp")
    return lax.ppermute(x, "dp", [(i, i ^ spot_mask(i, spot, bits)) for i in range(n)])


def call(fn, outs, args, specs, flops, name, scratch=(), out_spec=VM):
    size = sum(a.size * a.dtype.itemsize for a in args)
    return pl.pallas_call(
        fn,
        out_shape=tuple(outs),
        in_specs=specs,
        out_specs=tuple(out_spec for _ in outs),
        scratch_shapes=scratch,
        compiler_params=pltpu.CompilerParams(vmem_limit_bytes=16 << 20),
        cost_estimate=pl.CostEstimate(
            flops=flops // COST, bytes_accessed=size // COST, transcendentals=0
        ),
        name=name,
    )(*args)


def pin(arrays):
    return [pltpu.with_memory_space_constraint(a, pltpu.HBM) for a in arrays]


def shape(rows, cols, dtype=BF):
    return jax.ShapeDtypeStruct((rows, cols), dtype)


def one_hots(ids_ref, z, experts, capacity, local_tokens):
    first = ids_ref[0:1, :]
    second = ids_ref[1:2, :]
    member = jnp.concatenate(
        [((first == (z ^ d)) | (second == (z ^ d))).astype(F32) for d in range(experts)], axis=0
    )
    before = (
        lax.broadcasted_iota(I32, (local_tokens, local_tokens), 0)
        < lax.broadcasted_iota(I32, (local_tokens, local_tokens), 1)
    ).astype(F32)
    slot = jnp.dot(member.astype(BF), before.astype(BF), preferred_element_type=F32)
    rank = lax.broadcasted_iota(I32, (capacity, local_tokens), 0).astype(F32)
    return [
        jnp.where((rank == slot[d : d + 1, :]) & (member[d : d + 1, :] > 0.0), 1.0, 0.0)
        for d in range(experts)
    ]


def front_kernel(experts, capacity, z_ref, len_hbm, ada_hbm, ids_hbm, tok_hbm, *refs):
    outs = refs[:experts]
    len_ref, ada_ref, ids_ref, tok_ref, put_ref, sems, out_sems = refs[experts:]
    copies = [
        pltpu.make_async_copy(src, dst, sems.at[i])
        for i, (src, dst) in enumerate(
            [(tok_hbm, tok_ref), (ids_hbm, ids_ref), (len_hbm, len_ref), (ada_hbm, ada_ref)]
        )
    ]
    for copy in copies:
        copy.start()
    for copy in copies:
        copy.wait()
    local_tokens, width = tok_ref.shape
    values = tok_ref[...].astype(F32)
    normed = (
        values * lax.rsqrt(jnp.mean(values * values, axis=1, keepdims=True) + 1e-05)
    ).astype(BF)
    place = lax.broadcasted_iota(I32, (local_tokens, LANES), 0)
    lane = lax.broadcasted_iota(I32, (local_tokens, LANES), 1)
    tag = jnp.zeros((local_tokens, LANES), F32) + ada_ref[0, 0].astype(F32)
    end = len_ref[0, 0]
    for r in range(1, len_ref.shape[1]):
        tag = jnp.where(place >= end, ada_ref[0, r].astype(F32), tag)
        end = end + len_ref[0, r]
    tag = jnp.where(lane == 0, tag, 0.0).astype(BF)
    puts = one_hots(ids_ref, z_ref[0], experts, capacity, local_tokens)
    sends = []
    for d in range(experts):
        put = puts[d].astype(BF)
        put_ref[d, :, :width] = jnp.dot(put, normed, preferred_element_type=F32).astype(BF)
        put_ref[d, :, width:] = jnp.dot(put, tag, preferred_element_type=F32).astype(BF)
        sends.append(pltpu.make_async_copy(put_ref.at[d], outs[d], out_sems.at[d]))
        sends[d].start()
    for send in sends:
        send.wait()


def stage_kernel(axis, *refs):
    out_ref, sems = refs[-2:]
    copies = []
    start = 0
    for i, ref in enumerate(refs[:-2]):
        size = ref.shape[axis]
        where = tuple([slice(None)] * axis + [pl.ds(start, size)])
        copies.append(pltpu.make_async_copy(ref, out_ref.at[where], sems.at[i]))
        start += size
    for copy in copies:
        copy.start()
    for copy in copies:
        copy.wait()


def stage(arrays, axis, name):
    dims = list(arrays[0].shape)
    dims[axis] = sum(a.shape[axis] for a in arrays)
    return pl.pallas_call(
        functools.partial(stage_kernel, axis),
        out_shape=pltpu.VMEM(tuple(dims), BF),
        in_specs=[ANY] * len(arrays),
        out_specs=VM,
        scratch_shapes=[pltpu.SemaphoreType.DMA((len(arrays),))],
        compiler_params=pltpu.CompilerParams(vmem_limit_bytes=1 << 20),
        name=name,
    )(*pin(arrays))


def proj_kernel(spots, held, me_ref, fold_ref, *refs):
    piece_refs = refs[:spots]
    ld_ref = refs[spots]
    rows_ref, tag_ref = refs[spots + 1], refs[spots + 2]
    packs = refs[spots + 3 : spots + 5]
    all_ref, sems = refs[spots + 5 :]
    width = rows_ref.shape[0]
    group = piece_refs[0].shape[0]
    copies = [
        pltpu.make_async_copy(
            piece_refs[p], all_ref.at[pl.ds(p * group, group), :], sems.at[p]
        )
        for p in range(spots)
    ]
    for copy in copies:
        copy.start()
    for copy in copies:
        copy.wait()
    rows = all_ref[:, :width]
    rows_ref[...] = rows.T
    tags = all_ref[:, width:].astype(F32)
    tag_ref[...] = tags.T[0:8, :]
    labels = tags[:, 0:1]
    column = lax.broadcasted_iota(I32, (1, ld_ref.shape[1]), 1) // (2 * RANK)
    mine = me_ref[0] * held
    other = (me_ref[0] ^ 1) * held - held
    holder = jnp.where(column < held, column + mine, column + other).astype(F32)
    prod = jnp.dot(rows, ld_ref[...], preferred_element_type=F32)
    kept = jnp.where(labels == holder, prod, 0.0).astype(BF)
    folded = jnp.dot(kept, fold_ref[...], preferred_element_type=F32)
    lanes = packs[0].shape[1]
    spot = lax.broadcasted_iota(I32, (1, lanes), 1) // (2 * RANK)
    for s in range(2):
        total = jnp.zeros((group, lanes), F32)
        for p in range(spots):
            total = total + jnp.where(
                spot == (p ^ s), folded[p * group : (p + 1) * group, :], 0.0
            )
        packs[s][...] = total.astype(BF)


def nt(a, b):
    return lax.dot_general(a, b, (((1,), (1,)), ((), ())), preferred_element_type=F32)


def main_kernel(side, rows_ref, w_ref, raw_ref):
    for g in range(2):
        raw_ref[g, :, :] = jnp.dot(
            w_ref[2 * side + g, :, :], rows_ref[...], preferred_element_type=F32
        )


def mix_kernel(mask, own_ref, got_ref, sum_ref, out_ref):
    total = own_ref[...].astype(F32) + got_ref[...].astype(F32)
    sum_ref[...] = total.astype(BF)
    lanes = total.shape[1]
    step = mask * 2 * RANK
    spot = lax.broadcasted_iota(I32, total.shape, 1) // (2 * RANK)
    up = pltpu.roll(total, step, 1)
    down = pltpu.roll(total, lanes - step, 1)
    out_ref[...] = jnp.where(spot & mask == 0, down, up).astype(BF)


def down_kernel(spots, tile_ref, *refs):
    own_ref, got_ref, tag_ref = refs[:3]
    raw_refs, (lu_ref, dn_ref), outs = refs[3:5], refs[5:7], refs[7:]
    lanes = own_ref.shape[1]
    low = own_ref[...].astype(F32) + got_ref[...].astype(F32)
    spot = lax.broadcasted_iota(I32, (1, lanes), 1) // (2 * RANK)
    low = jnp.concatenate(
        [jnp.where(spot == p, low, 0.0).astype(BF) for p in range(spots)], axis=0
    )
    labels = tag_ref[0:1, :]
    wide = tile_ref.shape[1]
    owner = (lax.broadcasted_iota(I32, (wide, 1), 0) // RANK).astype(F32)
    mark = labels == owner
    spread = [jnp.where(mark, nt(tile_ref[g, :, :], low), 0.0).astype(BF) for g in range(2)]
    hidden = []
    for side in range(2):
        act = [
            raw_refs[side][g, :, :]
            + jnp.dot(lu_ref[2 * side + g, :, :], spread[g], preferred_element_type=F32)
            for g in range(2)
        ]
        hidden.append((act[0] / (1.0 + jnp.exp(-act[0])) * act[1]).astype(BF))
    total = lax.dot_general(
        jnp.concatenate(hidden, axis=0),
        dn_ref[...],
        (((0,), (0,)), ((), ())),
        preferred_element_type=F32,
    )
    start = 0
    for ref in outs:
        ref[...] = total[start : start + ref.shape[0], :].astype(BF)
        start += ref.shape[0]


def add_kernel(a_ref, b_ref, o_ref):
    o_ref[...] = (a_ref[...].astype(F32) + b_ref[...].astype(F32)).astype(BF)


def sum_kernel(*refs):
    size = refs[0].shape[0]
    total = refs[0][...].astype(F32)
    for ref in refs[1:-1]:
        total = total + ref[:size, :].astype(F32)
    refs[-1][...] = total.astype(BF)


def back_kernel(experts, capacity, z_ref, ids_ref, idc_ref, gw_ref, tok_ref, *refs):
    backs = refs[:-1]
    out_ref = refs[-1]
    local_tokens = tok_ref.shape[0]
    puts = one_hots(ids_ref, z_ref[0], experts, capacity, local_tokens)
    total = None
    for d in range(experts):
        scale = jnp.sum(
            jnp.where(idc_ref[...] == (z_ref[0] ^ d), gw_ref[...], 0.0), axis=1, keepdims=True
        )
        got = lax.dot_general(
            puts[d].astype(BF),
            backs[d][...],
            (((0,), (0,)), ((), ())),
            preferred_element_type=F32,
        )
        total = scale * got if total is None else total + scale * got
    out_ref[...] = (tok_ref[...].astype(F32) + total).astype(BF)


def after(values, deps):
    return lax.optimization_barrier((values, deps))[0]


def gather_first(own, bits):
    out = {0: own}
    for j in range(len(bits)):
        out[1 << j] = hop(own, 1 << j, bits)
    return out


def gather_second(have, bits):
    out = dict(have)
    for j in range(1, len(bits)):
        for p in range(1, 1 << j):
            out[p | 1 << j] = hop(out[p], 1 << j, bits)
    return [out[p] for p in range(1 << len(bits))]


def reduce_first(parts, bits, wait=()):
    table, gots = list(parts), []
    for j in reversed(range(1, len(bits))):
        for q in reversed(range(1 << j)):
            got = hop(table[q | 1 << j], 1 << j, bits)
            if q:
                table[q] = call(
                    add_kernel, [shape(*got.shape)], (after(table[q], wait), got), [VM] * 2, got.size, "add_rows"
                )[0]
            else:
                gots.append(got)
    return table[0], table[1], gots


def reduce_second(state, bits):
    own, last, gots = state
    return call(
        sum_kernel,
        [shape(*own.shape)],
        (own, *gots, hop(last, 1, bits)),
        [VM] * (2 + len(gots)),
        own.size,
        "sum_rows",
    )[0]


def body(
    tokens,
    expert_ids,
    gate_weights,
    request_lengths,
    request_adapter,
    expert_weights,
    expert_down,
    low_down,
    low_up,
):
    experts = lax.axis_size("expert")
    n_dp = lax.axis_size("dp")
    local_tokens, width = tokens.shape
    capacity = local_tokens * TOP * 4 // (3 * experts)
    held = low_down.shape[2] // (2 * RANK)
    adapters = low_up.shape[2] // RANK
    units = expert_down.shape[1]
    bits = []
    b = 2
    while b < n_dp:
        bits.append(b)
        b *= 2
    spots = 1 << len(bits)
    z = lax.axis_index("expert").astype(I32).reshape(1)
    me = lax.axis_index("dp").astype(I32).reshape(1)
    ids_t = expert_ids.T

    outgoing = call(
        functools.partial(front_kernel, experts, capacity),
        [pltpu.HBM((capacity, width + LANES), BF)] * experts,
        (z, *pin([request_lengths, request_adapter, ids_t, tokens])),
        [SM, ANY, ANY, ANY, ANY],
        2 * experts * capacity * local_tokens * width,
        "front",
        [
            pltpu.SMEM(request_lengths.shape, I32),
            pltpu.SMEM(request_adapter.shape, I32),
            pltpu.VMEM(ids_t.shape, I32),
            pltpu.VMEM(tokens.shape, BF),
            pltpu.VMEM((experts, capacity, width + LANES), BF),
            pltpu.SemaphoreType.DMA((4,)),
            pltpu.SemaphoreType.DMA((experts,)),
        ],
        ANY,
    )
    wt_t = jnp.swapaxes(expert_weights[0], 1, 2)
    lu_t = jnp.swapaxes(low_up[0], 1, 2)
    ld_o = swap(low_down[0], "dp", 1)
    wt_o = swap(after(wt_t, outgoing), "dp", 1)
    ld = stage([low_down[0], ld_o], 1, "stage_low_down")
    wt = stage([wt_t, wt_o], 0, "stage_gate_up")
    lanes = 2 * RANK * spots
    fold = (
        jnp.arange(4 * held * RANK)[:, None] % (2 * RANK) == jnp.arange(lanes)[None, :] % (2 * RANK)
    ).astype(BF)
    tile = jnp.stack(
        [
            (
                jnp.arange(lanes)[None, :] % (2 * RANK)
                == jnp.arange(adapters * RANK)[:, None] % RANK + g * RANK
            ).astype(BF)
            for g in range(2)
        ]
    )

    order = list(range(experts))
    first, second = {}, {}
    first[0] = gather_first(outgoing[0], bits)
    arrived = [outgoing[0]] + [swap(outgoing[order[i]], "expert", order[i]) for i in (1, 2)]

    group = capacity
    count = group * spots
    parts, done, adds = {}, {}, {}
    first[0] = after(first[0], (arrived[1], ld_o))
    second[0] = gather_second(first[0], bits)
    lu_o = swap(after(lu_t, (wt_o, first[0])), "dp", 1)
    dn_o = swap(after(expert_down[0], (lu_o, second[0])), "dp", 1)
    lu = stage([lu_t, lu_o], 0, "stage_low_up")
    dn = stage([expert_down[0], dn_o], 0, "stage_down")
    first[1] = gather_first(after(arrived[1], second[0]), bits)
    last = experts - 1
    backs = [None] * experts

    def give(j):
        backs[order[j]] = done[j] if order[j] == 0 else swap(done[j], "expert", order[j])

    for i, d in enumerate(order):
        deps = [first[2]] if i == 1 else [wt] if i == 0 else []
        if i >= 1:
            deps.append(parts[i - 1][0])
        if i >= 2:
            done[i - 2] = reduce_second(adds[i - 2], bits)
            deps.append(done[i - 2])
            give(i - 2)
        pieces = after(second[i], deps)
        got = call(
            functools.partial(proj_kernel, spots, held),
            [shape(width, count), shape(8, count, F32)] + [shape(group, lanes)] * 2,
            (me, fold, *pin(pieces), ld),
            [SM, VM] + [ANY] * spots + [VM],
            4 * count * width * held * 2 * RANK,
            "project",
            [pltpu.VMEM((count, width + LANES), BF), pltpu.SemaphoreType.DMA((spots,))],
        )
        rows, tags, low, send = got
        deps = [first[1]] if i == 0 else [second[3]] if i == 2 else []
        if i == 0:
            second[1] = gather_second(after(first[1], low), bits)
            first[2] = gather_first(after(arrived[2], low), bits)
            second[2] = gather_second(first[2], bits)
        rows = after(rows, deps)
        raw = []
        for side in range(2):
            raw.append(
                call(
                    functools.partial(main_kernel, side),
                    [jax.ShapeDtypeStruct((2, units, count), F32)],
                    (rows, wt),
                    [VM] * 2,
                    4 * count * width * units,
                    "gate_up",
                )[0]
            )
            if side == 0:
                recv = hop(send, 1, bits)
                early = raw[0]
                low = after(low, early)
                if i >= 1:
                    adds[i - 1] = reduce_first(parts[i - 1], bits, raw)
                    low = after(low, adds[i - 1][1])
                for j in range(1, len(bits)):
                    low, send = call(
                        functools.partial(mix_kernel, 1 << j),
                        [shape(group, lanes)] * 2,
                        (low, recv),
                        [VM] * 2,
                        group * lanes,
                        "mix",
                    )
                    recv = hop(send, 1 << j, bits)
                rows = after(rows, low)
        if i == 0:
            for j in range(3, experts):
                piece = after(outgoing[order[j]], (arrived[j - 1], early))
                arrived.append(swap(piece, "expert", order[j]))
                first[j] = gather_first(after(arrived[j], raw), bits)
                second[j] = gather_second(first[j], bits)
        deps = [second[1]] if i == 0 else [second[2], first[3]] if i == 1 else []
        raw = after(raw, deps)
        parts[i] = call(
            functools.partial(down_kernel, spots),
            [shape(group, width)] * spots,
            (tile, low, recv, tags, *raw, lu, dn),
            [VM] * 8,
            8 * count * adapters * RANK * units + 4 * count * units * width,
            "down",
        )
    done[last - 1] = reduce_second(adds[last - 1], bits)
    give(last - 1)
    own, left, gots = reduce_first(parts[last], bits)
    own = after(own, [backs[order[i]] for i in range(last)])
    done[last] = reduce_second((own, left, gots), bits)
    give(last)

    return call(
        functools.partial(back_kernel, experts, capacity),
        [shape(local_tokens, width)],
        (z, ids_t, expert_ids, gate_weights, tokens, *backs),
        [SM] + [VM] * (4 + experts),
        2 * experts * capacity * local_tokens * width,
        "combine",
    )[0]


def solution(mesh):
    return jax.shard_map(
        body,
        mesh=mesh,
        in_specs=(
            P(("expert", "dp"), None),
            P(("expert", "dp"), None),
            P(("expert", "dp"), None),
            P(("expert", "dp"), None),
            P(("expert", "dp"), None),
            P("expert", None, None, "dp"),
            P("expert", "dp", None),
            P("expert", None, "dp"),
            P("expert", None, None, "dp"),
        ),
        out_specs=P(("expert", "dp"), None),
        check_vma=False,
    )
```

time: 188 us -> 157 us (0.84)
  starting transfers between devices: 68.1 us -> 50.2 us
  local copies, waits for them, and re-layouts: 15.1 us -> 3.96 us
  Pallas kernels: 66 us -> 58.4 us
  waiting for transfers between devices: 36 us -> 43.2 us
    ppermute x62 -> x10, starting transfers between devices: 68.1 us -> 15 us  [swap(): return lax.ppermute(x, axis, [(i, i ^ bit) for i in range(n)])]
    ppermute x0 -> x32, starting transfers between devices: none -> 35.2 us  [hop(): lax.ppermute(x, 'dp', [(i, i ^ spot_mask(i, spot, bits)) for i in range(n)])]
    pallas_call x26 -> x30, Pallas kernels: 66 us -> 46.2 us  [call(): pl.pallas_call(fn, out_shape=tuple(outs), in_specs=specs, out_specs=tuple...]
    ppermute x0 -> x32, waiting for transfers between devices: none -> 16.3 us  [hop(): lax.ppermute(x, 'dp', [(i, i ^ spot_mask(i, spot, bits)) for i in range(n)])]
    pallas_call x0 -> x4, Pallas kernels: none -> 12.2 us  [stage(): pl.pallas_call(functools.partial(stage_kernel, axis), out_shape=pltpu.VME...]
    unnamed x60 -> x44, local copies, waits for them, and re-layouts: 14.1 us -> 3.96 us
    ppermute x62 -> x10, waiting for transfers between devices: 36 us -> 26.9 us  [swap(): return lax.ppermute(x, axis, [(i, i ^ bit) for i in range(n)])]
  transfers between devices with their start and end apart: 62 -> 42, of which waited for: 14 -> 16; matrix products, arithmetic and copies ran while one was open for 1% -> 1% of each run, Pallas kernels for 31% -> 34%
where the time goes in v2:
time: 157 us
  Pallas kernels  58.4 us (37%)
  starting transfers between devices  50.2 us (32%)
  waiting for transfers between devices  43.2 us (28%)
  local copies, waits for them, and re-layouts  3.96 us (3%)
    pallas_call x30, Pallas kernels, call(): pl.pallas_call(fn, out_shape=tuple(outs), in_specs=specs, out_specs=tuple...  46.2 us
    ppermute x32, starting transfers between devices, hop(): lax.ppermute(x, 'dp', [(i, i ^ spot_mask(i, spot, bits)) for i in range(n)])  35.2 us
    ppermute x10, waiting for transfers between devices, swap(): return lax.ppermute(x, axis, [(i, i ^ bit) for i in range(n)])  26.9 us
    ppermute x32, waiting for transfers between devices, hop(): lax.ppermute(x, 'dp', [(i, i ^ spot_mask(i, spot, bits)) for i in range(n)])  16.3 us
    ppermute x10, starting transfers between devices, swap(): return lax.ppermute(x, axis, [(i, i ^ bit) for i in range(n)])  15 us
    pallas_call x4, Pallas kernels, stage(): pl.pallas_call(functools.partial(stage_kernel, axis), out_shape=pltpu.VME...  12.2 us
    unnamed x44, local copies, waits for them, and re-layouts  3.96 us
  transfers between devices with their start and end apart: 42, of which 16 were waited for; matrix products, arithmetic and copies ran while one was open for 1% of the time, Pallas kernels for 34%

profile of v2, /device:TPU:0, one launch (start us, length us, event | category | flops | bytes accessed | tf_op | source)
XLA Modules:
  0.0 156.8 jit_solution(7825407070146022210)
XLA Ops:
  0.0 2.5 %front.1 = (bf16[64,2432]{1,0:T(8,128)(2,1)}, bf16[64,2432]{1,0:T(8,128)(2,1)}, bf16[64,2432]{1,0:T(8,128)(2,1)}, bf16[64,2432]{1,0:T(8,128)(2,1)}) custom-call(s32[1]{0:T(128)} %bitcast.z_ref, s32[1,4]{1,0:T(1,128)} %len_hbm.1, s32[1,4]{1,0:T(1,128)} %ada_hbm.1, s32[2,96]{1,0:T(2,128)} %bitcast.11, bf16[96,2304]{1,0:T(8,128)(2,1)} %tok_ref.1), custom_call_target="tpu_custom_call" | custom-call | flops 7077888 | bytes 27698 | tf_op jit(solution)/shard_map/front/pallas_call | solution.py:43
  3.2 2.9 %collective-permute-start = (bf16[64,2432]{1,0:T(8,128)(2,1)}, bf16[64,2432]{1,0:T(8,128)(2,1)S(1)}, u32[]{:S(2)}, u32[]{:S(2)}) collective-permute-start(bf16[64,2432]{1,0:T(8,128)(2,1)} %get-tuple-element.111.refs_0_), channel_id=1, source_target_pairs={{0,2},{1,5},{2,0},{3,7},{4,6},{5,1},{6,4},{7,3},{8,10},{9,13},{10,... | collective-permute-start | bytes 933896 | tf_op jit(solution)/shard_map/ppermute | solution.py:38
  9.2 4.7 %collective-permute-done.refs_1_ = bf16[64,2432]{1,0:T(8,128)(2,1)S(1)} collective-permute-done((bf16[64,2432]{1,0:T(8,128)(2,1)}, bf16[64,2432]{1,0:T(8,128)(2,1)S(1)}, u32[]{:S(2)}, u32[]{:S(2)}) %collective-permute-start) | collective-permute-done | bytes 311328 | tf_op jit(solution)/shard_map/ppermute | solution.py:38
  13.9 2.7 %collective-permute-done.2.refs_0_ = bf16[64,2432]{1,0:T(8,128)(2,1)S(1)} collective-permute-done((bf16[64,2432]{1,0:T(8,128)(2,1)}, bf16[64,2432]{1,0:T(8,128)(2,1)S(1)}, u32[]{:S(2)}, u32[]{:S(2)}) %collective-permute-start.2) | collective-permute-done | bytes 311328 | tf_op jit(solution)/shard_map/ppermute | solution.py:24
  18.4 6.2 %collective-permute-done.4.refs_3_ = bf16[64,2432]{1,0:T(8,128)(2,1)S(1)} collective-permute-done((bf16[64,2432]{1,0:T(8,128)(2,1)S(1)}, bf16[64,2432]{1,0:T(8,128)(2,1)S(1)}, u32[]{:S(2)}, u32[]{:S(2)}) %collective-permute-start.4) | collective-permute-done | bytes 311328 | tf_op jit(solution)/shard_map/ppermute | solution.py:38
  26.4 2.6 %collective-permute-start.14 = (bf16[64,2432]{1,0:T(8,128)(2,1)}, bf16[64,2432]{1,0:T(8,128)(2,1)}, u32[]{:S(2)}, u32[]{:S(2)}) collective-permute-start(bf16[64,2432]{1,0:T(8,128)(2,1)} %get-tuple-element.108), channel_id=1, source_target_pairs={{0,16},{8,24},{16,0},{24,8},{1,17},{9,25},{17,1},{25,9},{2,18},{10... | collective-permute-start | bytes 933896 | tf_op jit(solution)/shard_map/ppermute | solution.py:24
  33.0 4.8 %stage_gate_up.1.w_ref = bf16[4,720,2304]{2,1,0:T(8,128)(2,1)S(1)} custom-call(bf16[2,720,2304]{2,1,0:T(8,128)(2,1)} %bitcast.14, bf16[2,720,2304]{2,1,0:T(8,128)(2,1)} %collective-permute-done.5.refs_1_), custom_call_target="tpu_custom_call" | custom-call | tf_op jit(solution)/shard_map/stage_gate_up/pallas_call | solution.py:139
  37.8 2.2 %project.4 = (bf16[2304,256]{1,0:T(8,128)(2,1)S(1)}, f32[8,256]{1,0:T(8,128)S(1)}, bf16[64,128]{1,0:T(8,128)(2,1)S(1)}, bf16[64,128]{1,0:T(8,128)(2,1)S(1)}) custom-call(s32[1]{0:T(128)} %bitcast.2.me_ref, bf16[512,128]{1,0:T(8,128)(2,1)S(1)} %compare_convert_fusion.fold_ref, bf16[64,2432]{1,0:T(8,128)(2,1)} %get-tuple-element.111.refs_0_, ...), custom_call_target="tpu_custom_call" | custom-call | flops 37748736 | bytes 233472 | tf_op jit(solution)/shard_map/project/pallas_call | solution.py:43
  40.1 1.9 %gate_up.8.refs_3_ = f32[2,720,256]{2,1,0:T(8,128)S(1)} custom-call(bf16[2304,256]{1,0:T(8,128)(2,1)S(1)} %get-tuple-element.124.rows_ref, bf16[4,720,2304]{2,1,0:T(8,128)(2,1)S(1)} %stage_gate_up.1.w_ref), custom_call_target="tpu_custom_call" | custom-call | flops 106168320 | bytes 903168 | tf_op jit(solution)/shard_map/gate_up/pallas_call | solution.py:43
  42.0 2.0 %collective-permute-done.14.refs_0_ = bf16[64,2432]{1,0:T(8,128)(2,1)} collective-permute-done((bf16[64,2432]{1,0:T(8,128)(2,1)}, bf16[64,2432]{1,0:T(8,128)(2,1)}, u32[]{:S(2)}, u32[]{:S(2)}) %collective-permute-start.14) | collective-permute-done | bytes 311328 | tf_op jit(solution)/shard_map/ppermute | solution.py:24
  44.0 3.5 %collective-permute-start.22 = (bf16[64,2432]{1,0:T(8,128)(2,1)S(1)}, bf16[64,2432]{1,0:T(8,128)(2,1)S(1)}, u32[]{:S(2)}, u32[]{:S(2)}) collective-permute-start(bf16[64,2432]{1,0:T(8,128)(2,1)S(1)} %copy-done.20), channel_id=1, source_target_pairs={{0,24},{8,16},{16,8},{24,0},{1,25},{9,17},{17,9},{25,1},{2,26},{10... | collective-permute-start | bytes 933896 | tf_op jit(solution)/shard_map/ppermute | solution.py:24
  52.2 3.0 %collective-permute-done.22.refs_0_ = bf16[64,2432]{1,0:T(8,128)(2,1)S(1)} collective-permute-done((bf16[64,2432]{1,0:T(8,128)(2,1)S(1)}, bf16[64,2432]{1,0:T(8,128)(2,1)S(1)}, u32[]{:S(2)}, u32[]{:S(2)}) %collective-permute-start.22) | collective-permute-done | bytes 311328 | tf_op jit(solution)/shard_map/ppermute | solution.py:24
  59.5 2.7 %stage_low_up.1.refs_5_ = bf16[4,720,1024]{2,1,0:T(8,128)(2,1)S(1)} custom-call(bf16[2,720,1024]{2,1,0:T(8,128)(2,1)} %bitcast.18, bf16[2,720,1024]{2,1,0:T(8,128)(2,1)} %copy-done.3), custom_call_target="tpu_custom_call" | custom-call | tf_op jit(solution)/shard_map/stage_low_up/pallas_call | solution.py:139
  63.9 3.0 %stage_down.1.refs_6_ = bf16[1440,2304]{1,0:T(8,128)(2,1)S(1)} custom-call(bf16[720,2304]{1,0:T(8,128)(2,1)} %bitcast.16, bf16[720,2304]{1,0:T(8,128)(2,1)} %copy-done.2), custom_call_target="tpu_custom_call" | custom-call | tf_op jit(solution)/shard_map/stage_down/pallas_call | solution.py:139
  66.9 4.2 %down.4 = (bf16[64,2304]{1,0:T(8,128)(2,1)S(1)}, bf16[64,2304]{1,0:T(8,128)(2,1)S(1)}, bf16[64,2304]{1,0:T(8,128)(2,1)S(1)}, bf16[64,2304]{1,0:T(8,128)(2,1)S(1)}) custom-call(bf16[2,1024,128]{2,1,0:T(8,128)(2,1)S(1)} %add_convert_fusion.tile_ref, bf16[64,128]{1,0:T(8,128)(2,1)S(1)} %get-tuple-element.121.refs_0_, ...), custom_call_target="tpu_custom_call" | custom-call | flops 200540160 | bytes 1003008 | tf_op jit(solution)/shard_map/down/pallas_call | solution.py:43
  73.2 2.3 %project.5 = (bf16[2304,256]{1,0:T(8,128)(2,1)S(1)}, f32[8,256]{1,0:T(8,128)S(1)}, bf16[64,128]{1,0:T(8,128)(2,1)S(1)}, bf16[64,128]{1,0:T(8,128)(2,1)S(1)}) custom-call(s32[1]{0:T(128)} %bitcast.2.me_ref, bf16[512,128]{1,0:T(8,128)(2,1)S(1)} %compare_convert_fusion.fold_ref, bf16[64,2432]{1,0:T(8,128)(2,1)} %copy-done.8, bf16[64,2432]{1,0:T(8,128)(2,1)} %copy-done.12, ...), custom_call_target="tpu_custom_call" | custom-call | flops 37748736 | bytes 233472 | tf_op jit(solution)/shard_map/project/pallas_call | solution.py:43
  76.6 1.9 %gate_up.10.refs_3_ = f32[2,720,256]{2,1,0:T(8,128)S(1)} custom-call(bf16[2304,256]{1,0:T(8,128)(2,1)S(1)} %get-tuple-element.150.rows_ref, bf16[4,720,2304]{2,1,0:T(8,128)(2,1)S(1)} %stage_gate_up.1.w_ref), custom_call_target="tpu_custom_call" | custom-call | flops 106168320 | bytes 903168 | tf_op jit(solution)/shard_map/gate_up/pallas_call | solution.py:43
  83.3 1.9 %gate_up.11.refs_4_ = f32[2,720,256]{2,1,0:T(8,128)S(1)} custom-call(bf16[2304,256]{1,0:T(8,128)(2,1)S(1)} %get-tuple-element.150.rows_ref, bf16[4,720,2304]{2,1,0:T(8,128)(2,1)S(1)} %stage_gate_up.1.w_ref), custom_call_target="tpu_custom_call" | custom-call | flops 106168320 | bytes 903168 | tf_op jit(solution)/shard_map/gate_up/pallas_call | solution.py:43
  85.3 4.4 %down.5 = (bf16[64,2304]{1,0:T(8,128)(2,1)S(1)}, bf16[64,2304]{1,0:T(8,128)(2,1)S(1)}, bf16[64,2304]{1,0:T(8,128)(2,1)S(1)}, bf16[64,2304]{1,0:T(8,128)(2,1)S(1)}) custom-call(bf16[2,1024,128]{2,1,0:T(8,128)(2,1)S(1)} %add_convert_fusion.tile_ref, bf16[64,128]{1,0:T(8,128)(2,1)S(1)} %get-tuple-element.147.refs_0_, ...), custom_call_target="tpu_custom_call" | custom-call | flops 200540160 | bytes 1003008 | tf_op jit(solution)/shard_map/down/pallas_call | solution.py:43
  91.4 2.2 %project.6 = (bf16[2304,256]{1,0:T(8,128)(2,1)S(1)}, f32[8,256]{1,0:T(8,128)S(1)}, bf16[64,128]{1,0:T(8,128)(2,1)S(1)}, bf16[64,128]{1,0:T(8,128)(2,1)S(1)}) custom-call(s32[1]{0:T(128)} %bitcast.2.me_ref, bf16[512,128]{1,0:T(8,128)(2,1)S(1)} %compare_convert_fusion.fold_ref, bf16[64,2432]{1,0:T(8,128)(2,1)} %collective-permute-done.14.refs_0_, ...), custom_call_target="tpu_custom_call" | custom-call | flops 37748736 | bytes 233472 | tf_op jit(solution)/shard_map/project/pallas_call | solution.py:43
  94.9 1.9 %gate_up.12.refs_3_ = f32[2,720,256]{2,1,0:T(8,128)S(1)} custom-call(bf16[2304,256]{1,0:T(8,128)(2,1)S(1)} %get-tuple-element.173.rows_ref, bf16[4,720,2304]{2,1,0:T(8,128)(2,1)S(1)} %stage_gate_up.1.w_ref), custom_call_target="tpu_custom_call" | custom-call | flops 106168320 | bytes 903168 | tf_op jit(solution)/shard_map/gate_up/pallas_call | solution.py:43
  101.0 1.9 %gate_up.13.refs_4_ = f32[2,720,256]{2,1,0:T(8,128)S(1)} custom-call(bf16[2304,256]{1,0:T(8,128)(2,1)S(1)} %get-tuple-element.173.rows_ref, bf16[4,720,2304]{2,1,0:T(8,128)(2,1)S(1)} %stage_gate_up.1.w_ref), custom_call_target="tpu_custom_call" | custom-call | flops 106168320 | bytes 903168 | tf_op jit(solution)/shard_map/gate_up/pallas_call | solution.py:43
  102.8 4.2 %down.6 = (bf16[64,2304]{1,0:T(8,128)(2,1)S(1)}, bf16[64,2304]{1,0:T(8,128)(2,1)S(1)}, bf16[64,2304]{1,0:T(8,128)(2,1)S(1)}, bf16[64,2304]{1,0:T(8,128)(2,1)S(1)}) custom-call(bf16[2,1024,128]{2,1,0:T(8,128)(2,1)S(1)} %add_convert_fusion.tile_ref, bf16[64,128]{1,0:T(8,128)(2,1)S(1)} %get-tuple-element.170.refs_0_, ...), custom_call_target="tpu_custom_call" | custom-call | flops 200540160 | bytes 1003008 | tf_op jit(solution)/shard_map/down/pallas_call | solution.py:43
  109.2 2.2 %project.7 = (bf16[2304,256]{1,0:T(8,128)(2,1)S(1)}, f32[8,256]{1,0:T(8,128)S(1)}, bf16[64,128]{1,0:T(8,128)(2,1)S(1)}, bf16[64,128]{1,0:T(8,128)(2,1)S(1)}) custom-call(s32[1]{0:T(128)} %bitcast.2.me_ref, bf16[512,128]{1,0:T(8,128)(2,1)S(1)} %compare_convert_fusion.fold_ref, bf16[64,2432]{1,0:T(8,128)(2,1)} %copy-done.5, bf16[64,2432]{1,0:T(8,128)(2,1)} %copy-done.6, ...), custom_call_target="tpu_custom_call" | custom-call | flops 37748736 | bytes 233472 | tf_op jit(solution)/shard_map/project/pallas_call | solution.py:43
  113.1 1.9 %gate_up.14.refs_3_ = f32[2,720,256]{2,1,0:T(8,128)S(1)} custom-call(bf16[2304,256]{1,0:T(8,128)(2,1)S(1)} %get-tuple-element.193.rows_ref, bf16[4,720,2304]{2,1,0:T(8,128)(2,1)S(1)} %stage_gate_up.1.w_ref), custom_call_target="tpu_custom_call" | custom-call | flops 106168320 | bytes 903168 | tf_op jit(solution)/shard_map/gate_up/pallas_call | solution.py:43
  119.2 1.9 %gate_up.15.refs_4_ = f32[2,720,256]{2,1,0:T(8,128)S(1)} custom-call(bf16[2304,256]{1,0:T(8,128)(2,1)S(1)} %get-tuple-element.193.rows_ref, bf16[4,720,2304]{2,1,0:T(8,128)(2,1)S(1)} %stage_gate_up.1.w_ref), custom_call_target="tpu_custom_call" | custom-call | flops 106168320 | bytes 903168 | tf_op jit(solution)/shard_map/gate_up/pallas_call | solution.py:43
  121.1 4.4 %down.7 = (bf16[64,2304]{1,0:T(8,128)(2,1)S(1)}, bf16[64,2304]{1,0:T(8,128)(2,1)S(1)}, bf16[64,2304]{1,0:T(8,128)(2,1)S(1)}, bf16[64,2304]{1,0:T(8,128)(2,1)S(1)}) custom-call(bf16[2,1024,128]{2,1,0:T(8,128)(2,1)S(1)} %add_convert_fusion.tile_ref, bf16[64,128]{1,0:T(8,128)(2,1)S(1)} %get-tuple-element.190.refs_0_, ...), custom_call_target="tpu_custom_call" | custom-call | flops 200540160 | bytes 1003008 | tf_op jit(solution)/shard_map/down/pallas_call | solution.py:43
  125.6 5.5 %collective-permute-start.29 = (bf16[64,2304]{1,0:T(8,128)(2,1)S(1)}, bf16[64,2304]{1,0:T(8,128)(2,1)S(1)}, u32[]{:S(2)}, u32[]{:S(2)}) collective-permute-start(bf16[64,2304]{1,0:T(8,128)(2,1)S(1)} %sum_rows.5), channel_id=1, source_target_pairs={{0,8},{8,0},{16,24},{24,16},{1,9},{9,1},{17,25},{25,17},{2,10},{10... | collective-permute-start | bytes 884744 | tf_op jit(solution)/shard_map/ppermute | solution.py:24
  132.4 1.9 %collective-permute-start.38 = (bf16[64,2304]{1,0:T(8,128)(2,1)S(1)}, bf16[64,2304]{1,0:T(8,128)(2,1)S(1)}, u32[]{:S(2)}, u32[]{:S(2)}) collective-permute-start(bf16[64,2304]{1,0:T(8,128)(2,1)S(1)} %get-tuple-element.198), channel_id=1, source_target_pairs={{0,4},{1,3},{2,6},{3,1},{4,0},{5,7},{6,2},{7,5},{8,12},{9,11},{10,... | collective-permute-start | bytes 884744 | tf_op jit(solution)/shard_map/ppermute | solution.py:38
  135.6 3.0 %collective-permute-done.29.refs_1_ = bf16[64,2304]{1,0:T(8,128)(2,1)S(1)} collective-permute-done((bf16[64,2304]{1,0:T(8,128)(2,1)S(1)}, bf16[64,2304]{1,0:T(8,128)(2,1)S(1)}, u32[]{:S(2)}, u32[]{:S(2)}) %collective-permute-start.29) | collective-permute-done | bytes 294944 | tf_op jit(solution)/shard_map/ppermute | solution.py:24
  138.5 7.9 %collective-permute-done.35.refs_2_ = bf16[64,2304]{1,0:T(8,128)(2,1)S(1)} collective-permute-done((bf16[64,2304]{1,0:T(8,128)(2,1)S(1)}, bf16[64,2304]{1,0:T(8,128)(2,1)S(1)}, u32[]{:S(2)}, u32[]{:S(2)}) %collective-permute-start.35) | collective-permute-done | bytes 294944 | tf_op jit(solution)/shard_map/ppermute | solution.py:24
  146.9 8.4 %collective-permute-done.41.refs_3_ = bf16[64,2304]{1,0:T(8,128)(2,1)S(1)} collective-permute-done((bf16[64,2304]{1,0:T(8,128)(2,1)S(1)}, bf16[64,2304]{1,0:T(8,128)(2,1)S(1)}, u32[]{:S(2)}, u32[]{:S(2)}) %collective-permute-start.41) | collective-permute-done | bytes 294944 | tf_op jit(solution)/shard_map/ppermute | solution.py:24
  (136 shorter events, 49.9 us)
Async XLA Ops:
  2.6 14.0 %collective-permute-start.5 = (bf16[2,720,2304]{2,1,0:T(8,128)(2,1)}, bf16[2,720,2304]{2,1,0:T(8,128)(2,1)}, u32[]{:S(2)}, u32[]{:S(2)}) collective-permute-start(bf16[2,720,2304]{2,1,0:T(8,128)(2,1)} %bitcast.13), channel_id=1, source_target_pairs={{0,1},{1,0},{2,3},{3,2},{4,5},{5,4},{6,7},{7,6},{8,9},{9,8},{10,11... | collective-permute-start | bytes 19906568 | tf_op jit(solution)/shard_map/ppermute | solution.py:24
  3.1 13.5 %collective-permute-start.3 = (bf16[2304,256]{1,0:T(8,128)(2,1)}, bf16[2304,256]{1,0:T(8,128)(2,1)S(1)}, u32[]{:S(2)}, u32[]{:S(2)}) collective-permute-start(bf16[2304,256]{1,0:T(8,128)(2,1)} %bitcast.19), channel_id=1, source_target_pairs={{0,1},{1,0},{2,3},{3,2},{4,5},{5,4},{6,7},{7,6},{8,9},{9,8},{10,11... | collective-permute-start | bytes 3538952 | tf_op jit(solution)/shard_map/ppermute | solution.py:24
  3.2 10.7 %collective-permute-start = (bf16[64,2432]{1,0:T(8,128)(2,1)}, bf16[64,2432]{1,0:T(8,128)(2,1)S(1)}, u32[]{:S(2)}, u32[]{:S(2)}) collective-permute-start(bf16[64,2432]{1,0:T(8,128)(2,1)} %get-tuple-element.111.refs_0_), channel_id=1, source_target_pairs={{0,2},{1,5},{2,0},{3,7},{4,6},{5,1},{6,4},{7,3},{8,10},{9,13},{10,... | collective-permute-start | bytes 933896 | tf_op jit(solution)/shard_map/ppermute | solution.py:38
  6.1 7.8 %collective-permute-start.1 = (bf16[64,2432]{1,0:T(8,128)(2,1)}, bf16[64,2432]{1,0:T(8,128)(2,1)S(1)}, u32[]{:S(2)}, u32[]{:S(2)}) collective-permute-start(bf16[64,2432]{1,0:T(8,128)(2,1)} %get-tuple-element.111.refs_0_), channel_id=1, source_target_pairs={{0,4},{1,3},{2,6},{3,1},{4,0},{5,7},{6,2},{7,5},{8,12},{9,11},{10,... | collective-permute-start | bytes 933896 | tf_op jit(solution)/shard_map/ppermute | solution.py:38
  7.6 9.0 %collective-permute-start.2 = (bf16[64,2432]{1,0:T(8,128)(2,1)}, bf16[64,2432]{1,0:T(8,128)(2,1)S(1)}, u32[]{:S(2)}, u32[]{:S(2)}) collective-permute-start(bf16[64,2432]{1,0:T(8,128)(2,1)} %get-tuple-element.104), channel_id=1, source_target_pairs={{0,8},{8,0},{16,24},{24,16},{1,9},{9,1},{17,25},{25,17},{2,10},{10... | collective-permute-start | bytes 933896 | tf_op jit(solution)/shard_map/ppermute | solution.py:24
  26.3 35.9 %collective-permute-start.12 = (bf16[720,2304]{1,0:T(8,128)(2,1)}, bf16[720,2304]{1,0:T(8,128)(2,1)S(1)}, u32[]{:S(2)}, u32[]{:S(2)}) collective-permute-start(bf16[720,2304]{1,0:T(8,128)(2,1)} %bitcast.15), channel_id=1, source_target_pairs={{0,1},{1,0},{2,3},{3,2},{4,5},{5,4},{6,7},{7,6},{8,9},{9,8},{10,11... | collective-permute-start | bytes 9953288 | tf_op jit(solution)/shard_map/ppermute | solution.py:24
  26.4 17.6 %collective-permute-start.14 = (bf16[64,2432]{1,0:T(8,128)(2,1)}, bf16[64,2432]{1,0:T(8,128)(2,1)}, u32[]{:S(2)}, u32[]{:S(2)}) collective-permute-start(bf16[64,2432]{1,0:T(8,128)(2,1)} %get-tuple-element.108), channel_id=1, source_target_pairs={{0,16},{8,24},{16,0},{24,8},{1,17},{9,25},{17,1},{25,9},{2,18},{10... | collective-permute-start | bytes 933896 | tf_op jit(solution)/shard_map/ppermute | solution.py:24
  29.0 11.1 %collective-permute-start.6 = (bf16[64,2432]{1,0:T(8,128)(2,1)}, bf16[64,2432]{1,0:T(8,128)(2,1)S(1)}, u32[]{:S(2)}, u32[]{:S(2)}) collective-permute-start(bf16[64,2432]{1,0:T(8,128)(2,1)} %copy-done.8), channel_id=1, source_target_pairs={{0,2},{1,5},{2,0},{3,7},{4,6},{5,1},{6,4},{7,3},{8,10},{9,13},{10,... | collective-permute-start | bytes 933896 | tf_op jit(solution)/shard_map/ppermute | solution.py:38
  29.7 10.4 %collective-permute-start.7 = (bf16[64,2432]{1,0:T(8,128)(2,1)}, bf16[64,2432]{1,0:T(8,128)(2,1)S(1)}, u32[]{:S(2)}, u32[]{:S(2)}) collective-permute-start(bf16[64,2432]{1,0:T(8,128)(2,1)} %copy-done.8), channel_id=1, source_target_pairs={{0,4},{1,3},{2,6},{3,1},{4,0},{5,7},{6,2},{7,5},{8,12},{9,11},{10,... | collective-permute-start | bytes 933896 | tf_op jit(solution)/shard_map/ppermute | solution.py:38
  44.0 11.2 %collective-permute-start.22 = (bf16[64,2432]{1,0:T(8,128)(2,1)S(1)}, bf16[64,2432]{1,0:T(8,128)(2,1)S(1)}, u32[]{:S(2)}, u32[]{:S(2)}) collective-permute-start(bf16[64,2432]{1,0:T(8,128)(2,1)S(1)} %copy-done.20), channel_id=1, source_target_pairs={{0,24},{8,16},{16,8},{24,0},{1,25},{9,17},{17,9},{25,1},{2,26},{10... | collective-permute-start | bytes 933896 | tf_op jit(solution)/shard_map/ppermute | solution.py:24
  48.2 10.2 %collective-permute-start.10 = (bf16[64,2432]{1,0:T(8,128)(2,1)S(1)}, bf16[64,2432]{1,0:T(8,128)(2,1)S(1)}, u32[]{:S(2)}, u32[]{:S(2)}) collective-permute-start(bf16[64,2432]{1,0:T(8,128)(2,1)S(1)} %collective-permute-done.6.refs_1_), channel_id=1, source_target_pairs={{0,4},{1,3},{2,6},{3,1},{4,0},{5,7},{6,2},{7,5},{8,12},{9,11},{10,... | collective-permute-start | bytes 933896 | tf_op jit(solution)/shard_map/ppermute | solution.py:38
  49.7 22.3 %collective-permute-start.15 = (bf16[64,2432]{1,0:T(8,128)(2,1)}, bf16[64,2432]{1,0:T(8,128)(2,1)S(1)}, u32[]{:S(2)}, u32[]{:S(2)}) collective-permute-start(bf16[64,2432]{1,0:T(8,128)(2,1)} %collective-permute-done.14.refs_0_), channel_id=1, source_target_pairs={{0,2},{1,5},{2,0},{3,7},{4,6},{5,1},{6,4},{7,3},{8,10},{9,13},{10,... | collective-permute-start | bytes 933896 | tf_op jit(solution)/shard_map/ppermute | solution.py:38
  51.4 21.9 %collective-permute-start.16 = (bf16[64,2432]{1,0:T(8,128)(2,1)}, bf16[64,2432]{1,0:T(8,128)(2,1)S(1)}, u32[]{:S(2)}, u32[]{:S(2)}) collective-permute-start(bf16[64,2432]{1,0:T(8,128)(2,1)} %collective-permute-done.14.refs_0_), channel_id=1, source_target_pairs={{0,4},{1,3},{2,6},{3,1},{4,0},{5,7},{6,2},{7,5},{8,12},{9,11},{10,... | collective-permute-start | bytes 933896 | tf_op jit(solution)/shard_map/ppermute | solution.py:38
  55.2 11.7 %collective-permute-start.9 = (bf16[64,128]{1,0:T(8,128)(2,1)S(1)}, bf16[64,128]{1,0:T(8,128)(2,1)S(1)}, u32[]{:S(2)}, u32[]{:S(2)}) collective-permute-start(bf16[64,128]{1,0:T(8,128)(2,1)S(1)} %get-tuple-element.122), channel_id=1, source_target_pairs={{0,4},{1,3},{2,6},{3,1},{4,0},{5,7},{6,2},{7,5},{8,12},{9,11},{10,... | collective-permute-start | bytes 49160 | tf_op jit(solution)/shard_map/ppermute | solution.py:38
  58.4 22.0 %collective-permute-start.23 = (bf16[64,2432]{1,0:T(8,128)(2,1)S(1)}, bf16[64,2432]{1,0:T(8,128)(2,1)S(1)}, u32[]{:S(2)}, u32[]{:S(2)}) collective-permute-start(bf16[64,2432]{1,0:T(8,128)(2,1)S(1)} %collective-permute-done.22.refs_0_), channel_id=1, source_target_pairs={{0,2},{1,5},{2,0},{3,7},{4,6},{5,1},{6,4},{7,3},{8,10},{9,13},{10,... | collective-permute-start | bytes 933896 | tf_op jit(solution)/shard_map/ppermute | solution.py:38
  62.3 20.2 %collective-permute-start.24 = (bf16[64,2432]{1,0:T(8,128)(2,1)S(1)}, bf16[64,2432]{1,0:T(8,128)(2,1)S(1)}, u32[]{:S(2)}, u32[]{:S(2)}) collective-permute-start(bf16[64,2432]{1,0:T(8,128)(2,1)S(1)} %collective-permute-done.22.refs_0_), channel_id=1, source_target_pairs={{0,4},{1,3},{2,6},{3,1},{4,0},{5,7},{6,2},{7,5},{8,12},{9,11},{10,... | collective-permute-start | bytes 933896 | tf_op jit(solution)/shard_map/ppermute | solution.py:38
  71.1 7.4 %collective-permute-start.17 = (bf16[64,2304]{1,0:T(8,128)(2,1)S(1)}, bf16[64,2304]{1,0:T(8,128)(2,1)S(1)}, u32[]{:S(2)}, u32[]{:S(2)}) collective-permute-start(bf16[64,2304]{1,0:T(8,128)(2,1)S(1)} %get-tuple-element.142), channel_id=1, source_target_pairs={{0,4},{1,3},{2,6},{3,1},{4,0},{5,7},{6,2},{7,5},{8,12},{9,11},{10,... | collective-permute-start | bytes 884744 | tf_op jit(solution)/shard_map/ppermute | solution.py:38
  72.0 13.2 %collective-permute-start.21 = (bf16[64,2432]{1,0:T(8,128)(2,1)S(1)}, bf16[64,2432]{1,0:T(8,128)(2,1)S(1)}, u32[]{:S(2)}, u32[]{:S(2)}) collective-permute-start(bf16[64,2432]{1,0:T(8,128)(2,1)S(1)} %collective-permute-done.15.refs_1_), channel_id=1, source_target_pairs={{0,4},{1,3},{2,6},{3,1},{4,0},{5,7},{6,2},{7,5},{8,12},{9,11},{10,... | collective-permute-start | bytes 933896 | tf_op jit(solution)/shard_map/ppermute | solution.py:38
  80.4 14.5 %collective-permute-start.26 = (bf16[64,2432]{1,0:T(8,128)(2,1)S(1)}, bf16[64,2432]{1,0:T(8,128)(2,1)S(1)}, u32[]{:S(2)}, u32[]{:S(2)}) collective-permute-start(bf16[64,2432]{1,0:T(8,128)(2,1)S(1)} %collective-permute-done.23.refs_1_), channel_id=1, source_target_pairs={{0,4},{1,3},{2,6},{3,1},{4,0},{5,7},{6,2},{7,5},{8,12},{9,11},{10,... | collective-permute-start | bytes 933896 | tf_op jit(solution)/shard_map/ppermute | solution.py:38
  81.5 9.8 %collective-permute-start.13 = (bf16[64,2304]{1,0:T(8,128)(2,1)S(1)}, bf16[64,2304]{1,0:T(8,128)(2,1)S(1)}, u32[]{:S(2)}, u32[]{:S(2)}) collective-permute-start(bf16[64,2304]{1,0:T(8,128)(2,1)S(1)} %get-tuple-element.133), channel_id=1, source_target_pairs={{0,4},{1,3},{2,6},{3,1},{4,0},{5,7},{6,2},{7,5},{8,12},{9,11},{10,... | collective-permute-start | bytes 884744 | tf_op jit(solution)/shard_map/ppermute | solution.py:38
  82.4 8.8 %collective-permute-start.18 = (bf16[64,2304]{1,0:T(8,128)(2,1)S(1)}, bf16[64,2304]{1,0:T(8,128)(2,1)S(1)}, u32[]{:S(2)}, u32[]{:S(2)}) collective-permute-start(bf16[64,2304]{1,0:T(8,128)(2,1)S(1)} %add_rows.4), channel_id=1, source_target_pairs={{0,2},{1,5},{2,0},{3,7},{4,6},{5,1},{6,4},{7,3},{8,10},{9,13},{10,... | collective-permute-start | bytes 884744 | tf_op jit(solution)/shard_map/ppermute | solution.py:38
  98.7 9.0 %collective-permute-start.25 = (bf16[64,2304]{1,0:T(8,128)(2,1)S(1)}, bf16[64,2304]{1,0:T(8,128)(2,1)S(1)}, u32[]{:S(2)}, u32[]{:S(2)}) collective-permute-start(bf16[64,2304]{1,0:T(8,128)(2,1)S(1)} %get-tuple-element.156), channel_id=1, source_target_pairs={{0,4},{1,3},{2,6},{3,1},{4,0},{5,7},{6,2},{7,5},{8,12},{9,11},{10,... | collective-permute-start | bytes 884744 | tf_op jit(solution)/shard_map/ppermute | solution.py:38
  99.7 9.4 %collective-permute-start.28 = (bf16[64,2304]{1,0:T(8,128)(2,1)S(1)}, bf16[64,2304]{1,0:T(8,128)(2,1)S(1)}, u32[]{:S(2)}, u32[]{:S(2)}) collective-permute-start(bf16[64,2304]{1,0:T(8,128)(2,1)S(1)} %add_rows.5), channel_id=1, source_target_pairs={{0,2},{1,5},{2,0},{3,7},{4,6},{5,1},{6,4},{7,3},{8,10},{9,13},{10,... | collective-permute-start | bytes 884744 | tf_op jit(solution)/shard_map/ppermute | solution.py:38
  107.1 7.9 %collective-permute-start.33 = (bf16[64,2304]{1,0:T(8,128)(2,1)S(1)}, bf16[64,2304]{1,0:T(8,128)(2,1)S(1)}, u32[]{:S(2)}, u32[]{:S(2)}) collective-permute-start(bf16[64,2304]{1,0:T(8,128)(2,1)S(1)} %get-tuple-element.185), channel_id=1, source_target_pairs={{0,4},{1,3},{2,6},{3,1},{4,0},{5,7},{6,2},{7,5},{8,12},{9,11},{10,... | collective-permute-start | bytes 884744 | tf_op jit(solution)/shard_map/ppermute | solution.py:38
  116.9 14.2 %collective-permute-start.32 = (bf16[64,2304]{1,0:T(8,128)(2,1)S(1)}, bf16[64,2304]{1,0:T(8,128)(2,1)S(1)}, u32[]{:S(2)}, u32[]{:S(2)}) collective-permute-start(bf16[64,2304]{1,0:T(8,128)(2,1)S(1)} %get-tuple-element.177), channel_id=1, source_target_pairs={{0,4},{1,3},{2,6},{3,1},{4,0},{5,7},{6,2},{7,5},{8,12},{9,11},{10,... | collective-permute-start | bytes 884744 | tf_op jit(solution)/shard_map/ppermute | solution.py:38
  117.6 13.5 %collective-permute-start.34 = (bf16[64,2304]{1,0:T(8,128)(2,1)S(1)}, bf16[64,2304]{1,0:T(8,128)(2,1)S(1)}, u32[]{:S(2)}, u32[]{:S(2)}) collective-permute-start(bf16[64,2304]{1,0:T(8,128)(2,1)S(1)} %add_rows.6), channel_id=1, source_target_pairs={{0,2},{1,5},{2,0},{3,7},{4,6},{5,1},{6,4},{7,3},{8,10},{9,13},{10,... | collective-permute-start | bytes 884744 | tf_op jit(solution)/shard_map/ppermute | solution.py:38
  125.5 9.3 %collective-permute-start.39 = (bf16[64,2304]{1,0:T(8,128)(2,1)S(1)}, bf16[64,2304]{1,0:T(8,128)(2,1)S(1)}, u32[]{:S(2)}, u32[]{:S(2)}) collective-permute-start(bf16[64,2304]{1,0:T(8,128)(2,1)S(1)} %get-tuple-element.200), channel_id=1, source_target_pairs={{0,4},{1,3},{2,6},{3,1},{4,0},{5,7},{6,2},{7,5},{8,12},{9,11},{10,... | collective-permute-start | bytes 884744 | tf_op jit(solution)/shard_map/ppermute | solution.py:38
  125.6 12.9 %collective-permute-start.29 = (bf16[64,2304]{1,0:T(8,128)(2,1)S(1)}, bf16[64,2304]{1,0:T(8,128)(2,1)S(1)}, u32[]{:S(2)}, u32[]{:S(2)}) collective-permute-start(bf16[64,2304]{1,0:T(8,128)(2,1)S(1)} %sum_rows.5), channel_id=1, source_target_pairs={{0,8},{8,0},{16,24},{24,16},{1,9},{9,1},{17,25},{25,17},{2,10},{10... | collective-permute-start | bytes 884744 | tf_op jit(solution)/shard_map/ppermute | solution.py:24
  131.2 15.2 %collective-permute-start.35 = (bf16[64,2304]{1,0:T(8,128)(2,1)S(1)}, bf16[64,2304]{1,0:T(8,128)(2,1)S(1)}, u32[]{:S(2)}, u32[]{:S(2)}) collective-permute-start(bf16[64,2304]{1,0:T(8,128)(2,1)S(1)} %sum_rows.6), channel_id=1, source_target_pairs={{0,16},{8,24},{16,0},{24,8},{1,17},{9,25},{17,1},{25,9},{2,18},{10... | collective-permute-start | bytes 884744 | tf_op jit(solution)/shard_map/ppermute | solution.py:24
  132.4 14.1 %collective-permute-start.38 = (bf16[64,2304]{1,0:T(8,128)(2,1)S(1)}, bf16[64,2304]{1,0:T(8,128)(2,1)S(1)}, u32[]{:S(2)}, u32[]{:S(2)}) collective-permute-start(bf16[64,2304]{1,0:T(8,128)(2,1)S(1)} %get-tuple-element.198), channel_id=1, source_target_pairs={{0,4},{1,3},{2,6},{3,1},{4,0},{5,7},{6,2},{7,5},{8,12},{9,11},{10,... | collective-permute-start | bytes 884744 | tf_op jit(solution)/shard_map/ppermute | solution.py:38
  134.8 11.6 %collective-permute-start.40 = (bf16[64,2304]{1,0:T(8,128)(2,1)S(1)}, bf16[64,2304]{1,0:T(8,128)(2,1)S(1)}, u32[]{:S(2)}, u32[]{:S(2)}) collective-permute-start(bf16[64,2304]{1,0:T(8,128)(2,1)S(1)} %add_rows.7), channel_id=1, source_target_pairs={{0,2},{1,5},{2,0},{3,7},{4,6},{5,1},{6,4},{7,3},{8,10},{9,13},{10,... | collective-permute-start | bytes 884744 | tf_op jit(solution)/shard_map/ppermute | solution.py:38
  146.6 8.7 %collective-permute-start.41 = (bf16[64,2304]{1,0:T(8,128)(2,1)S(1)}, bf16[64,2304]{1,0:T(8,128)(2,1)S(1)}, u32[]{:S(2)}, u32[]{:S(2)}) collective-permute-start(bf16[64,2304]{1,0:T(8,128)(2,1)S(1)} %sum_rows.7), channel_id=1, source_target_pairs={{0,24},{8,16},{16,8},{24,0},{1,25},{9,17},{17,9},{25,1},{2,26},{10... | collective-permute-start | bytes 884744 | tf_op jit(solution)/shard_map/ppermute | solution.py:24
  (31 other events, 175.3 us)

commit v3 on v2

--- a/solution.py
+++ b/solution.py
@@ -401,7 +401,7 @@
     dn_o = swap(after(expert_down[0], (lu_o, second[0])), "dp", 1)
     lu = stage([lu_t, lu_o], 0, "stage_low_up")
     dn = stage([expert_down[0], dn_o], 0, "stage_down")
-    first[1] = gather_first(after(arrived[1], second[0]), bits)
+    first[1] = gather_first(after(arrived[1], (second[0], wt, ld)), bits)
     last = experts - 1
     backs = [None] * experts
 
@@ -427,7 +427,7 @@
             [pltpu.VMEM((count, width + LANES), BF), pltpu.SemaphoreType.DMA((spots,))],
         )
         rows, tags, low, send = got
-        deps = [first[1]] if i == 0 else [second[3]] if i == 2 else []
+        deps = [first[1], dn_o] if i == 0 else [second[3]] if i == 2 else []
         if i == 0:
             second[1] = gather_second(after(first[1], low), bits)
             first[2] = gather_first(after(arrived[2], low), bits)

time: 157 us -> 149 us (0.949)
  waiting for transfers between devices: 43.2 us -> 35.2 us
    ppermute x10, waiting for transfers between devices: 26.9 us -> 14.4 us  [swap(): return lax.ppermute(x, axis, [(i, i ^ bit) for i in range(n)])]
    ppermute x32, waiting for transfers between devices: 16.3 us -> 20.8 us  [hop(): lax.ppermute(x, 'dp', [(i, i ^ spot_mask(i, spot, bits)) for i in range(n)])]
    unnamed x44 -> x46, local copies, waits for them, and re-layouts: 3.96 us -> 3.13 us
  transfers between devices with their start and end apart: 42 -> 42, of which waited for: 16 -> 17; matrix products, arithmetic and copies ran while one was open for 1% -> 1% of each run, Pallas kernels for 34% -> 36%
where the time goes in v3:
time: 149 us
  Pallas kernels  58 us (39%)
  starting transfers between devices  51.2 us (34%)
  waiting for transfers between devices  35.2 us (24%)
  local copies, waits for them, and re-layouts  3.13 us (2%)
    pallas_call x30, Pallas kernels, call(): pl.pallas_call(fn, out_shape=tuple(outs), in_specs=specs, out_specs=tuple...  45.7 us
    ppermute x32, starting transfers between devices, hop(): lax.ppermute(x, 'dp', [(i, i ^ spot_mask(i, spot, bits)) for i in range(n)])  34.8 us
    ppermute x32, waiting for transfers between devices, hop(): lax.ppermute(x, 'dp', [(i, i ^ spot_mask(i, spot, bits)) for i in range(n)])  20.8 us
    ppermute x10, starting transfers between devices, swap(): return lax.ppermute(x, axis, [(i, i ^ bit) for i in range(n)])  16.4 us
    ppermute x10, waiting for transfers between devices, swap(): return lax.ppermute(x, axis, [(i, i ^ bit) for i in range(n)])  14.4 us
    pallas_call x4, Pallas kernels, stage(): pl.pallas_call(functools.partial(stage_kernel, axis), out_shape=pltpu.VME...  12.3 us
    unnamed x46, local copies, waits for them, and re-layouts  3.13 us
  transfers between devices with their start and end apart: 42, of which 17 were waited for; matrix products, arithmetic and copies ran while one was open for 1% of the time, Pallas kernels for 36%

profile of v3, /device:TPU:0, one launch (start us, length us, event | category | flops | bytes accessed | tf_op | source)
XLA Modules:
  0.0 148.6 jit_solution(10756810467582535752)
XLA Ops:
  0.0 2.6 %front.1 = (bf16[64,2432]{1,0:T(8,128)(2,1)}, bf16[64,2432]{1,0:T(8,128)(2,1)}, bf16[64,2432]{1,0:T(8,128)(2,1)}, bf16[64,2432]{1,0:T(8,128)(2,1)}) custom-call(s32[1]{0:T(128)} %bitcast.z_ref, s32[1,4]{1,0:T(1,128)} %len_hbm.1, s32[1,4]{1,0:T(1,128)} %ada_hbm.1, s32[2,96]{1,0:T(2,128)} %bitcast.11, bf16[96,2304]{1,0:T(8,128)(2,1)} %tok_ref.1), custom_call_target="tpu_custom_call" | custom-call | flops 7077888 | bytes 27698 | tf_op jit(solution)/shard_map/front/pallas_call | solution.py:43
  3.2 2.9 %collective-permute-start = (bf16[64,2432]{1,0:T(8,128)(2,1)}, bf16[64,2432]{1,0:T(8,128)(2,1)S(1)}, u32[]{:S(2)}, u32[]{:S(2)}) collective-permute-start(bf16[64,2432]{1,0:T(8,128)(2,1)} %get-tuple-element.111.refs_0_), channel_id=1, source_target_pairs={{0,2},{1,5},{2,0},{3,7},{4,6},{5,1},{6,4},{7,3},{8,10},{9,13},{10,... | collective-permute-start | bytes 933896 | tf_op jit(solution)/shard_map/ppermute | solution.py:38
  9.2 4.7 %collective-permute-done.refs_1_ = bf16[64,2432]{1,0:T(8,128)(2,1)S(1)} collective-permute-done((bf16[64,2432]{1,0:T(8,128)(2,1)}, bf16[64,2432]{1,0:T(8,128)(2,1)S(1)}, u32[]{:S(2)}, u32[]{:S(2)}) %collective-permute-start) | collective-permute-done | bytes 311328 | tf_op jit(solution)/shard_map/ppermute | solution.py:38
  13.9 2.7 %collective-permute-done.2.refs_0_ = bf16[64,2432]{1,0:T(8,128)(2,1)S(1)} collective-permute-done((bf16[64,2432]{1,0:T(8,128)(2,1)}, bf16[64,2432]{1,0:T(8,128)(2,1)S(1)}, u32[]{:S(2)}, u32[]{:S(2)}) %collective-permute-start.2) | collective-permute-done | bytes 311328 | tf_op jit(solution)/shard_map/ppermute | solution.py:24
  18.4 6.2 %collective-permute-done.4.refs_3_ = bf16[64,2432]{1,0:T(8,128)(2,1)S(1)} collective-permute-done((bf16[64,2432]{1,0:T(8,128)(2,1)S(1)}, bf16[64,2432]{1,0:T(8,128)(2,1)S(1)}, u32[]{:S(2)}, u32[]{:S(2)}) %collective-permute-start.4) | collective-permute-done | bytes 311328 | tf_op jit(solution)/shard_map/ppermute | solution.py:38
  26.4 2.6 %collective-permute-start.14 = (bf16[64,2432]{1,0:T(8,128)(2,1)}, bf16[64,2432]{1,0:T(8,128)(2,1)}, u32[]{:S(2)}, u32[]{:S(2)}) collective-permute-start(bf16[64,2432]{1,0:T(8,128)(2,1)} %get-tuple-element.108), channel_id=1, source_target_pairs={{0,16},{8,24},{16,0},{24,8},{1,17},{9,25},{17,1},{25,9},{2,18},{10... | collective-permute-start | bytes 933896 | tf_op jit(solution)/shard_map/ppermute | solution.py:24
  30.7 4.8 %stage_gate_up.1.w_ref = bf16[4,720,2304]{2,1,0:T(8,128)(2,1)S(1)} custom-call(bf16[2,720,2304]{2,1,0:T(8,128)(2,1)} %bitcast.14, bf16[2,720,2304]{2,1,0:T(8,128)(2,1)} %collective-permute-done.5.refs_1_), custom_call_target="tpu_custom_call" | custom-call | tf_op jit(solution)/shard_map/stage_gate_up/pallas_call | solution.py:139
  38.0 2.2 %project.4 = (bf16[2304,256]{1,0:T(8,128)(2,1)S(1)}, f32[8,256]{1,0:T(8,128)S(1)}, bf16[64,128]{1,0:T(8,128)(2,1)S(1)}, bf16[64,128]{1,0:T(8,128)(2,1)S(1)}) custom-call(s32[1]{0:T(128)} %bitcast.2.me_ref, bf16[512,128]{1,0:T(8,128)(2,1)S(1)} %compare_convert_fusion.fold_ref, bf16[64,2432]{1,0:T(8,128)(2,1)} %get-tuple-element.111.refs_0_, ...), custom_call_target="tpu_custom_call" | custom-call | flops 37748736 | bytes 233472 | tf_op jit(solution)/shard_map/project/pallas_call | solution.py:43
  40.8 3.2 %collective-permute-done.14.refs_0_ = bf16[64,2432]{1,0:T(8,128)(2,1)} collective-permute-done((bf16[64,2432]{1,0:T(8,128)(2,1)}, bf16[64,2432]{1,0:T(8,128)(2,1)}, u32[]{:S(2)}, u32[]{:S(2)}) %collective-permute-start.14) | collective-permute-done | bytes 311328 | tf_op jit(solution)/shard_map/ppermute | solution.py:24
  46.5 1.9 %gate_up.8.refs_3_ = f32[2,720,256]{2,1,0:T(8,128)S(1)} custom-call(bf16[2304,256]{1,0:T(8,128)(2,1)S(1)} %get-tuple-element.126.rows_ref, bf16[4,720,2304]{2,1,0:T(8,128)(2,1)S(1)} %stage_gate_up.1.w_ref), custom_call_target="tpu_custom_call" | custom-call | flops 106168320 | bytes 903168 | tf_op jit(solution)/shard_map/gate_up/pallas_call | solution.py:43
  48.4 3.4 %collective-permute-start.22 = (bf16[64,2432]{1,0:T(8,128)(2,1)S(1)}, bf16[64,2432]{1,0:T(8,128)(2,1)S(1)}, u32[]{:S(2)}, u32[]{:S(2)}) collective-permute-start(bf16[64,2432]{1,0:T(8,128)(2,1)S(1)} %copy-done.21), channel_id=1, source_target_pairs={{0,24},{8,16},{16,8},{24,0},{1,25},{9,17},{17,9},{25,1},{2,26},{10... | collective-permute-start | bytes 933896 | tf_op jit(solution)/shard_map/ppermute | solution.py:24
  55.0 2.7 %stage_low_up.1.refs_5_ = bf16[4,720,1024]{2,1,0:T(8,128)(2,1)S(1)} custom-call(bf16[2,720,1024]{2,1,0:T(8,128)(2,1)} %bitcast.18, bf16[2,720,1024]{2,1,0:T(8,128)(2,1)} %copy-done.3), custom_call_target="tpu_custom_call" | custom-call | tf_op jit(solution)/shard_map/stage_low_up/pallas_call | solution.py:139
  57.8 1.9 %gate_up.9.refs_4_ = f32[2,720,256]{2,1,0:T(8,128)S(1)} custom-call(bf16[2304,256]{1,0:T(8,128)(2,1)S(1)} %get-tuple-element.126.rows_ref, bf16[4,720,2304]{2,1,0:T(8,128)(2,1)S(1)} %stage_gate_up.1.w_ref), custom_call_target="tpu_custom_call" | custom-call | flops 106168320 | bytes 903168 | tf_op jit(solution)/shard_map/gate_up/pallas_call | solution.py:43
  59.7 3.1 %stage_down.1.refs_6_ = bf16[1440,2304]{1,0:T(8,128)(2,1)S(1)} custom-call(bf16[720,2304]{1,0:T(8,128)(2,1)} %bitcast.16, bf16[720,2304]{1,0:T(8,128)(2,1)} %copy-done.2), custom_call_target="tpu_custom_call" | custom-call | tf_op jit(solution)/shard_map/stage_down/pallas_call | solution.py:139
  64.5 4.1 %down.4 = (bf16[64,2304]{1,0:T(8,128)(2,1)S(1)}, bf16[64,2304]{1,0:T(8,128)(2,1)S(1)}, bf16[64,2304]{1,0:T(8,128)(2,1)S(1)}, bf16[64,2304]{1,0:T(8,128)(2,1)S(1)}) custom-call(bf16[2,1024,128]{2,1,0:T(8,128)(2,1)S(1)} %add_convert_fusion.tile_ref, bf16[64,128]{1,0:T(8,128)(2,1)S(1)} %get-tuple-element.123.refs_0_, ...), custom_call_target="tpu_custom_call" | custom-call | flops 200540160 | bytes 1003008 | tf_op jit(solution)/shard_map/down/pallas_call | solution.py:43
  70.7 2.3 %project.5 = (bf16[2304,256]{1,0:T(8,128)(2,1)S(1)}, f32[8,256]{1,0:T(8,128)S(1)}, bf16[64,128]{1,0:T(8,128)(2,1)S(1)}, bf16[64,128]{1,0:T(8,128)(2,1)S(1)}) custom-call(s32[1]{0:T(128)} %bitcast.2.me_ref, bf16[512,128]{1,0:T(8,128)(2,1)S(1)} %compare_convert_fusion.fold_ref, bf16[64,2432]{1,0:T(8,128)(2,1)} %copy-done.8, bf16[64,2432]{1,0:T(8,128)(2,1)} %copy-done.13, ...), custom_call_target="tpu_custom_call" | custom-call | flops 37748736 | bytes 233472 | tf_op jit(solution)/shard_map/project/pallas_call | solution.py:43
  73.4 1.9 %gate_up.10.refs_3_ = f32[2,720,256]{2,1,0:T(8,128)S(1)} custom-call(bf16[2304,256]{1,0:T(8,128)(2,1)S(1)} %get-tuple-element.150.rows_ref, bf16[4,720,2304]{2,1,0:T(8,128)(2,1)S(1)} %stage_gate_up.1.w_ref), custom_call_target="tpu_custom_call" | custom-call | flops 106168320 | bytes 903168 | tf_op jit(solution)/shard_map/gate_up/pallas_call | solution.py:43
  82.7 4.3 %down.5 = (bf16[64,2304]{1,0:T(8,128)(2,1)S(1)}, bf16[64,2304]{1,0:T(8,128)(2,1)S(1)}, bf16[64,2304]{1,0:T(8,128)(2,1)S(1)}, bf16[64,2304]{1,0:T(8,128)(2,1)S(1)}) custom-call(bf16[2,1024,128]{2,1,0:T(8,128)(2,1)S(1)} %add_convert_fusion.tile_ref, bf16[64,128]{1,0:T(8,128)(2,1)S(1)} %get-tuple-element.147.refs_0_, ...), custom_call_target="tpu_custom_call" | custom-call | flops 200540160 | bytes 1003008 | tf_op jit(solution)/shard_map/down/pallas_call | solution.py:43
  88.2 2.2 %project.6 = (bf16[2304,256]{1,0:T(8,128)(2,1)S(1)}, f32[8,256]{1,0:T(8,128)S(1)}, bf16[64,128]{1,0:T(8,128)(2,1)S(1)}, bf16[64,128]{1,0:T(8,128)(2,1)S(1)}) custom-call(s32[1]{0:T(128)} %bitcast.2.me_ref, bf16[512,128]{1,0:T(8,128)(2,1)S(1)} %compare_convert_fusion.fold_ref, bf16[64,2432]{1,0:T(8,128)(2,1)} %collective-permute-done.14.refs_0_, ...), custom_call_target="tpu_custom_call" | custom-call | flops 37748736 | bytes 233472 | tf_op jit(solution)/shard_map/project/pallas_call | solution.py:43
  91.7 1.9 %gate_up.12.refs_3_ = f32[2,720,256]{2,1,0:T(8,128)S(1)} custom-call(bf16[2304,256]{1,0:T(8,128)(2,1)S(1)} %get-tuple-element.173.rows_ref, bf16[4,720,2304]{2,1,0:T(8,128)(2,1)S(1)} %stage_gate_up.1.w_ref), custom_call_target="tpu_custom_call" | custom-call | flops 106168320 | bytes 903168 | tf_op jit(solution)/shard_map/gate_up/pallas_call | solution.py:43
  97.6 1.9 %gate_up.13.refs_4_ = f32[2,720,256]{2,1,0:T(8,128)S(1)} custom-call(bf16[2304,256]{1,0:T(8,128)(2,1)S(1)} %get-tuple-element.173.rows_ref, bf16[4,720,2304]{2,1,0:T(8,128)(2,1)S(1)} %stage_gate_up.1.w_ref), custom_call_target="tpu_custom_call" | custom-call | flops 106168320 | bytes 903168 | tf_op jit(solution)/shard_map/gate_up/pallas_call | solution.py:43
  99.5 4.1 %down.6 = (bf16[64,2304]{1,0:T(8,128)(2,1)S(1)}, bf16[64,2304]{1,0:T(8,128)(2,1)S(1)}, bf16[64,2304]{1,0:T(8,128)(2,1)S(1)}, bf16[64,2304]{1,0:T(8,128)(2,1)S(1)}) custom-call(bf16[2,1024,128]{2,1,0:T(8,128)(2,1)S(1)} %add_convert_fusion.tile_ref, bf16[64,128]{1,0:T(8,128)(2,1)S(1)} %get-tuple-element.170.refs_0_, ...), custom_call_target="tpu_custom_call" | custom-call | flops 200540160 | bytes 1003008 | tf_op jit(solution)/shard_map/down/pallas_call | solution.py:43
  105.9 2.2 %project.7 = (bf16[2304,256]{1,0:T(8,128)(2,1)S(1)}, f32[8,256]{1,0:T(8,128)S(1)}, bf16[64,128]{1,0:T(8,128)(2,1)S(1)}, bf16[64,128]{1,0:T(8,128)(2,1)S(1)}) custom-call(s32[1]{0:T(128)} %bitcast.2.me_ref, bf16[512,128]{1,0:T(8,128)(2,1)S(1)} %compare_convert_fusion.fold_ref, bf16[64,2432]{1,0:T(8,128)(2,1)} %copy-done.5, bf16[64,2432]{1,0:T(8,128)(2,1)} %copy-done.6, ...), custom_call_target="tpu_custom_call" | custom-call | flops 37748736 | bytes 233472 | tf_op jit(solution)/shard_map/project/pallas_call | solution.py:43
  115.6 1.9 %gate_up.15.refs_4_ = f32[2,720,256]{2,1,0:T(8,128)S(1)} custom-call(bf16[2304,256]{1,0:T(8,128)(2,1)S(1)} %get-tuple-element.193.rows_ref, bf16[4,720,2304]{2,1,0:T(8,128)(2,1)S(1)} %stage_gate_up.1.w_ref), custom_call_target="tpu_custom_call" | custom-call | flops 106168320 | bytes 903168 | tf_op jit(solution)/shard_map/gate_up/pallas_call | solution.py:43
  117.5 4.3 %down.7 = (bf16[64,2304]{1,0:T(8,128)(2,1)S(1)}, bf16[64,2304]{1,0:T(8,128)(2,1)S(1)}, bf16[64,2304]{1,0:T(8,128)(2,1)S(1)}, bf16[64,2304]{1,0:T(8,128)(2,1)S(1)}) custom-call(bf16[2,1024,128]{2,1,0:T(8,128)(2,1)S(1)} %add_convert_fusion.tile_ref, bf16[64,128]{1,0:T(8,128)(2,1)S(1)} %get-tuple-element.190.refs_0_, ...), custom_call_target="tpu_custom_call" | custom-call | flops 200540160 | bytes 1003008 | tf_op jit(solution)/shard_map/down/pallas_call | solution.py:43
  122.4 2.3 %collective-permute-start.29 = (bf16[64,2304]{1,0:T(8,128)(2,1)S(1)}, bf16[64,2304]{1,0:T(8,128)(2,1)S(1)}, u32[]{:S(2)}, u32[]{:S(2)}) collective-permute-start(bf16[64,2304]{1,0:T(8,128)(2,1)S(1)} %sum_rows.5), channel_id=1, source_target_pairs={{0,8},{8,0},{16,24},{24,16},{1,9},{9,1},{17,25},{25,17},{2,10},{10... | collective-permute-start | bytes 884744 | tf_op jit(solution)/shard_map/ppermute | solution.py:24
  126.5 2.0 %collective-permute-start.38 = (bf16[64,2304]{1,0:T(8,128)(2,1)S(1)}, bf16[64,2304]{1,0:T(8,128)(2,1)S(1)}, u32[]{:S(2)}, u32[]{:S(2)}) collective-permute-start(bf16[64,2304]{1,0:T(8,128)(2,1)S(1)} %get-tuple-element.198), channel_id=1, source_target_pairs={{0,4},{1,3},{2,6},{3,1},{4,0},{5,7},{6,2},{7,5},{8,12},{9,11},{10,... | collective-permute-start | bytes 884744 | tf_op jit(solution)/shard_map/ppermute | solution.py:38
  128.5 2.5 %collective-permute-done.39.b_ref = bf16[64,2304]{1,0:T(8,128)(2,1)S(1)} collective-permute-done((bf16[64,2304]{1,0:T(8,128)(2,1)S(1)}, bf16[64,2304]{1,0:T(8,128)(2,1)S(1)}, u32[]{:S(2)}, u32[]{:S(2)}) %collective-permute-start.39) | collective-permute-done | bytes 294944 | tf_op jit(solution)/shard_map/ppermute | solution.py:38
  132.5 3.3 %collective-permute-done.35.refs_2_ = bf16[64,2304]{1,0:T(8,128)(2,1)S(1)} collective-permute-done((bf16[64,2304]{1,0:T(8,128)(2,1)S(1)}, bf16[64,2304]{1,0:T(8,128)(2,1)S(1)}, u32[]{:S(2)}, u32[]{:S(2)}) %collective-permute-start.35) | collective-permute-done | bytes 294944 | tf_op jit(solution)/shard_map/ppermute | solution.py:24
  135.7 2.1 %collective-permute-done.40.refs_2_ = bf16[64,2304]{1,0:T(8,128)(2,1)S(1)} collective-permute-done((bf16[64,2304]{1,0:T(8,128)(2,1)S(1)}, bf16[64,2304]{1,0:T(8,128)(2,1)S(1)}, u32[]{:S(2)}, u32[]{:S(2)}) %collective-permute-start.40) | collective-permute-done | bytes 294944 | tf_op jit(solution)/shard_map/ppermute | solution.py:38
  138.0 4.2 %collective-permute-start.41 = (bf16[64,2304]{1,0:T(8,128)(2,1)S(1)}, bf16[64,2304]{1,0:T(8,128)(2,1)S(1)}, u32[]{:S(2)}, u32[]{:S(2)}) collective-permute-start(bf16[64,2304]{1,0:T(8,128)(2,1)S(1)} %sum_rows.7), channel_id=1, source_target_pairs={{0,24},{8,16},{16,8},{24,0},{1,25},{9,17},{17,9},{25,1},{2,26},{10... | collective-permute-start | bytes 884744 | tf_op jit(solution)/shard_map/ppermute | solution.py:24
  142.4 4.6 %collective-permute-done.41.refs_3_ = bf16[64,2304]{1,0:T(8,128)(2,1)S(1)} collective-permute-done((bf16[64,2304]{1,0:T(8,128)(2,1)S(1)}, bf16[64,2304]{1,0:T(8,128)(2,1)S(1)}, u32[]{:S(2)}, u32[]{:S(2)}) %collective-permute-start.41) | collective-permute-done | bytes 294944 | tf_op jit(solution)/shard_map/ppermute | solution.py:24
  (138 shorter events, 51.4 us)
Async XLA Ops:
  2.6 14.0 %collective-permute-start.5 = (bf16[2,720,2304]{2,1,0:T(8,128)(2,1)}, bf16[2,720,2304]{2,1,0:T(8,128)(2,1)}, u32[]{:S(2)}, u32[]{:S(2)}) collective-permute-start(bf16[2,720,2304]{2,1,0:T(8,128)(2,1)} %bitcast.13), channel_id=1, source_target_pairs={{0,1},{1,0},{2,3},{3,2},{4,5},{5,4},{6,7},{7,6},{8,9},{9,8},{10,11... | collective-permute-start | bytes 19906568 | tf_op jit(solution)/shard_map/ppermute | solution.py:24
  3.1 13.5 %collective-permute-start.3 = (bf16[2304,256]{1,0:T(8,128)(2,1)}, bf16[2304,256]{1,0:T(8,128)(2,1)S(1)}, u32[]{:S(2)}, u32[]{:S(2)}) collective-permute-start(bf16[2304,256]{1,0:T(8,128)(2,1)} %bitcast.19), channel_id=1, source_target_pairs={{0,1},{1,0},{2,3},{3,2},{4,5},{5,4},{6,7},{7,6},{8,9},{9,8},{10,11... | collective-permute-start | bytes 3538952 | tf_op jit(solution)/shard_map/ppermute | solution.py:24
  3.2 10.7 %collective-permute-start = (bf16[64,2432]{1,0:T(8,128)(2,1)}, bf16[64,2432]{1,0:T(8,128)(2,1)S(1)}, u32[]{:S(2)}, u32[]{:S(2)}) collective-permute-start(bf16[64,2432]{1,0:T(8,128)(2,1)} %get-tuple-element.111.refs_0_), channel_id=1, source_target_pairs={{0,2},{1,5},{2,0},{3,7},{4,6},{5,1},{6,4},{7,3},{8,10},{9,13},{10,... | collective-permute-start | bytes 933896 | tf_op jit(solution)/shard_map/ppermute | solution.py:38
  6.1 7.8 %collective-permute-start.1 = (bf16[64,2432]{1,0:T(8,128)(2,1)}, bf16[64,2432]{1,0:T(8,128)(2,1)S(1)}, u32[]{:S(2)}, u32[]{:S(2)}) collective-permute-start(bf16[64,2432]{1,0:T(8,128)(2,1)} %get-tuple-element.111.refs_0_), channel_id=1, source_target_pairs={{0,4},{1,3},{2,6},{3,1},{4,0},{5,7},{6,2},{7,5},{8,12},{9,11},{10,... | collective-permute-start | bytes 933896 | tf_op jit(solution)/shard_map/ppermute | solution.py:38
  7.6 9.0 %collective-permute-start.2 = (bf16[64,2432]{1,0:T(8,128)(2,1)}, bf16[64,2432]{1,0:T(8,128)(2,1)S(1)}, u32[]{:S(2)}, u32[]{:S(2)}) collective-permute-start(bf16[64,2432]{1,0:T(8,128)(2,1)} %get-tuple-element.104), channel_id=1, source_target_pairs={{0,8},{8,0},{16,24},{24,16},{1,9},{9,1},{17,25},{25,17},{2,10},{10... | collective-permute-start | bytes 933896 | tf_op jit(solution)/shard_map/ppermute | solution.py:24
  26.3 20.1 %collective-permute-start.9 = (bf16[720,2304]{1,0:T(8,128)(2,1)}, bf16[720,2304]{1,0:T(8,128)(2,1)S(1)}, u32[]{:S(2)}, u32[]{:S(2)}) collective-permute-start(bf16[720,2304]{1,0:T(8,128)(2,1)} %bitcast.15), channel_id=1, source_target_pairs={{0,1},{1,0},{2,3},{3,2},{4,5},{5,4},{6,7},{7,6},{8,9},{9,8},{10,11... | collective-permute-start | bytes 9953288 | tf_op jit(solution)/shard_map/ppermute | solution.py:24
  26.4 17.6 %collective-permute-start.14 = (bf16[64,2432]{1,0:T(8,128)(2,1)}, bf16[64,2432]{1,0:T(8,128)(2,1)}, u32[]{:S(2)}, u32[]{:S(2)}) collective-permute-start(bf16[64,2432]{1,0:T(8,128)(2,1)} %get-tuple-element.108), channel_id=1, source_target_pairs={{0,16},{8,24},{16,0},{24,8},{1,17},{9,25},{17,1},{25,9},{2,18},{10... | collective-permute-start | bytes 933896 | tf_op jit(solution)/shard_map/ppermute | solution.py:24
  35.5 10.0 %collective-permute-start.6 = (bf16[64,2432]{1,0:T(8,128)(2,1)S(1)}, bf16[64,2432]{1,0:T(8,128)(2,1)S(1)}, u32[]{:S(2)}, u32[]{:S(2)}) collective-permute-start(bf16[64,2432]{1,0:T(8,128)(2,1)S(1)} %copy-done.9), channel_id=1, source_target_pairs={{0,2},{1,5},{2,0},{3,7},{4,6},{5,1},{6,4},{7,3},{8,10},{9,13},{10,... | collective-permute-start | bytes 933896 | tf_op jit(solution)/shard_map/ppermute | solution.py:38
  36.3 9.2 %collective-permute-start.7 = (bf16[64,2432]{1,0:T(8,128)(2,1)S(1)}, bf16[64,2432]{1,0:T(8,128)(2,1)S(1)}, u32[]{:S(2)}, u32[]{:S(2)}) collective-permute-start(bf16[64,2432]{1,0:T(8,128)(2,1)S(1)} %copy-done.9), channel_id=1, source_target_pairs={{0,4},{1,3},{2,6},{3,1},{4,0},{5,7},{6,2},{7,5},{8,12},{9,11},{10,... | collective-permute-start | bytes 933896 | tf_op jit(solution)/shard_map/ppermute | solution.py:38
  40.2 12.5 %collective-permute-start.10 = (bf16[64,128]{1,0:T(8,128)(2,1)S(1)}, bf16[64,128]{1,0:T(8,128)(2,1)S(1)}, u32[]{:S(2)}, u32[]{:S(2)}) collective-permute-start(bf16[64,128]{1,0:T(8,128)(2,1)S(1)} %get-tuple-element.122), channel_id=1, source_target_pairs={{0,2},{1,5},{2,0},{3,7},{4,6},{5,1},{6,4},{7,3},{8,10},{9,13},{10,... | collective-permute-start | bytes 49160 | tf_op jit(solution)/shard_map/ppermute | solution.py:38
  44.0 10.4 %collective-permute-start.15 = (bf16[64,2432]{1,0:T(8,128)(2,1)}, bf16[64,2432]{1,0:T(8,128)(2,1)S(1)}, u32[]{:S(2)}, u32[]{:S(2)}) collective-permute-start(bf16[64,2432]{1,0:T(8,128)(2,1)} %collective-permute-done.14.refs_0_), channel_id=1, source_target_pairs={{0,2},{1,5},{2,0},{3,7},{4,6},{5,1},{6,4},{7,3},{8,10},{9,13},{10,... | collective-permute-start | bytes 933896 | tf_op jit(solution)/shard_map/ppermute | solution.py:38
  45.5 14.1 %collective-permute-start.12 = (bf16[64,2432]{1,0:T(8,128)(2,1)S(1)}, bf16[64,2432]{1,0:T(8,128)(2,1)S(1)}, u32[]{:S(2)}, u32[]{:S(2)}) collective-permute-start(bf16[64,2432]{1,0:T(8,128)(2,1)S(1)} %collective-permute-done.6.refs_1_), channel_id=1, source_target_pairs={{0,4},{1,3},{2,6},{3,1},{4,0},{5,7},{6,2},{7,5},{8,12},{9,11},{10,... | collective-permute-start | bytes 933896 | tf_op jit(solution)/shard_map/ppermute | solution.py:38
  48.4 14.4 %collective-permute-start.22 = (bf16[64,2432]{1,0:T(8,128)(2,1)S(1)}, bf16[64,2432]{1,0:T(8,128)(2,1)S(1)}, u32[]{:S(2)}, u32[]{:S(2)}) collective-permute-start(bf16[64,2432]{1,0:T(8,128)(2,1)S(1)} %copy-done.21), channel_id=1, source_target_pairs={{0,24},{8,16},{16,8},{24,0},{1,25},{9,17},{17,9},{25,1},{2,26},{10... | collective-permute-start | bytes 933896 | tf_op jit(solution)/shard_map/ppermute | solution.py:24
  52.1 18.5 %collective-permute-start.16 = (bf16[64,2432]{1,0:T(8,128)(2,1)}, bf16[64,2432]{1,0:T(8,128)(2,1)S(1)}, u32[]{:S(2)}, u32[]{:S(2)}) collective-permute-start(bf16[64,2432]{1,0:T(8,128)(2,1)} %collective-permute-done.14.refs_0_), channel_id=1, source_target_pairs={{0,4},{1,3},{2,6},{3,1},{4,0},{5,7},{6,2},{7,5},{8,12},{9,11},{10,... | collective-permute-start | bytes 933896 | tf_op jit(solution)/shard_map/ppermute | solution.py:38
  52.8 11.7 %collective-permute-start.11 = (bf16[64,128]{1,0:T(8,128)(2,1)S(1)}, bf16[64,128]{1,0:T(8,128)(2,1)S(1)}, u32[]{:S(2)}, u32[]{:S(2)}) collective-permute-start(bf16[64,128]{1,0:T(8,128)(2,1)S(1)} %get-tuple-element.124), channel_id=1, source_target_pairs={{0,4},{1,3},{2,6},{3,1},{4,0},{5,7},{6,2},{7,5},{8,12},{9,11},{10,... | collective-permute-start | bytes 49160 | tf_op jit(solution)/shard_map/ppermute | solution.py:38
  54.4 24.5 %collective-permute-start.21 = (bf16[64,2432]{1,0:T(8,128)(2,1)S(1)}, bf16[64,2432]{1,0:T(8,128)(2,1)S(1)}, u32[]{:S(2)}, u32[]{:S(2)}) collective-permute-start(bf16[64,2432]{1,0:T(8,128)(2,1)S(1)} %collective-permute-done.15.refs_1_), channel_id=1, source_target_pairs={{0,4},{1,3},{2,6},{3,1},{4,0},{5,7},{6,2},{7,5},{8,12},{9,11},{10,... | collective-permute-start | bytes 933896 | tf_op jit(solution)/shard_map/ppermute | solution.py:38
  62.8 16.8 %collective-permute-start.23 = (bf16[64,2432]{1,0:T(8,128)(2,1)S(1)}, bf16[64,2432]{1,0:T(8,128)(2,1)S(1)}, u32[]{:S(2)}, u32[]{:S(2)}) collective-permute-start(bf16[64,2432]{1,0:T(8,128)(2,1)S(1)} %collective-permute-done.22.refs_0_), channel_id=1, source_target_pairs={{0,2},{1,5},{2,0},{3,7},{4,6},{5,1},{6,4},{7,3},{8,10},{9,13},{10,... | collective-permute-start | bytes 933896 | tf_op jit(solution)/shard_map/ppermute | solution.py:38
  68.6 7.0 %collective-permute-start.17 = (bf16[64,2304]{1,0:T(8,128)(2,1)S(1)}, bf16[64,2304]{1,0:T(8,128)(2,1)S(1)}, u32[]{:S(2)}, u32[]{:S(2)}) collective-permute-start(bf16[64,2304]{1,0:T(8,128)(2,1)S(1)} %get-tuple-element.142), channel_id=1, source_target_pairs={{0,4},{1,3},{2,6},{3,1},{4,0},{5,7},{6,2},{7,5},{8,12},{9,11},{10,... | collective-permute-start | bytes 884744 | tf_op jit(solution)/shard_map/ppermute | solution.py:38
  69.0 13.7 %collective-permute-start.24 = (bf16[64,2432]{1,0:T(8,128)(2,1)S(1)}, bf16[64,2432]{1,0:T(8,128)(2,1)S(1)}, u32[]{:S(2)}, u32[]{:S(2)}) collective-permute-start(bf16[64,2432]{1,0:T(8,128)(2,1)S(1)} %collective-permute-done.22.refs_0_), channel_id=1, source_target_pairs={{0,4},{1,3},{2,6},{3,1},{4,0},{5,7},{6,2},{7,5},{8,12},{9,11},{10,... | collective-permute-start | bytes 933896 | tf_op jit(solution)/shard_map/ppermute | solution.py:38
  77.5 10.3 %collective-permute-start.13 = (bf16[64,2304]{1,0:T(8,128)(2,1)S(1)}, bf16[64,2304]{1,0:T(8,128)(2,1)S(1)}, u32[]{:S(2)}, u32[]{:S(2)}) collective-permute-start(bf16[64,2304]{1,0:T(8,128)(2,1)S(1)} %get-tuple-element.133), channel_id=1, source_target_pairs={{0,4},{1,3},{2,6},{3,1},{4,0},{5,7},{6,2},{7,5},{8,12},{9,11},{10,... | collective-permute-start | bytes 884744 | tf_op jit(solution)/shard_map/ppermute | solution.py:38
  78.9 9.2 %collective-permute-start.18 = (bf16[64,2304]{1,0:T(8,128)(2,1)S(1)}, bf16[64,2304]{1,0:T(8,128)(2,1)S(1)}, u32[]{:S(2)}, u32[]{:S(2)}) collective-permute-start(bf16[64,2304]{1,0:T(8,128)(2,1)S(1)} %add_rows.4), channel_id=1, source_target_pairs={{0,2},{1,5},{2,0},{3,7},{4,6},{5,1},{6,4},{7,3},{8,10},{9,13},{10,... | collective-permute-start | bytes 884744 | tf_op jit(solution)/shard_map/ppermute | solution.py:38
  79.5 12.1 %collective-permute-start.26 = (bf16[64,2432]{1,0:T(8,128)(2,1)S(1)}, bf16[64,2432]{1,0:T(8,128)(2,1)S(1)}, u32[]{:S(2)}, u32[]{:S(2)}) collective-permute-start(bf16[64,2432]{1,0:T(8,128)(2,1)S(1)} %collective-permute-done.23.refs_1_), channel_id=1, source_target_pairs={{0,4},{1,3},{2,6},{3,1},{4,0},{5,7},{6,2},{7,5},{8,12},{9,11},{10,... | collective-permute-start | bytes 933896 | tf_op jit(solution)/shard_map/ppermute | solution.py:38
  95.5 9.1 %collective-permute-start.25 = (bf16[64,2304]{1,0:T(8,128)(2,1)S(1)}, bf16[64,2304]{1,0:T(8,128)(2,1)S(1)}, u32[]{:S(2)}, u32[]{:S(2)}) collective-permute-start(bf16[64,2304]{1,0:T(8,128)(2,1)S(1)} %get-tuple-element.156), channel_id=1, source_target_pairs={{0,4},{1,3},{2,6},{3,1},{4,0},{5,7},{6,2},{7,5},{8,12},{9,11},{10,... | collective-permute-start | bytes 884744 | tf_op jit(solution)/shard_map/ppermute | solution.py:38
  96.5 9.3 %collective-permute-start.28 = (bf16[64,2304]{1,0:T(8,128)(2,1)S(1)}, bf16[64,2304]{1,0:T(8,128)(2,1)S(1)}, u32[]{:S(2)}, u32[]{:S(2)}) collective-permute-start(bf16[64,2304]{1,0:T(8,128)(2,1)S(1)} %add_rows.5), channel_id=1, source_target_pairs={{0,2},{1,5},{2,0},{3,7},{4,6},{5,1},{6,4},{7,3},{8,10},{9,13},{10,... | collective-permute-start | bytes 884744 | tf_op jit(solution)/shard_map/ppermute | solution.py:38
  103.6 7.8 %collective-permute-start.33 = (bf16[64,2304]{1,0:T(8,128)(2,1)S(1)}, bf16[64,2304]{1,0:T(8,128)(2,1)S(1)}, u32[]{:S(2)}, u32[]{:S(2)}) collective-permute-start(bf16[64,2304]{1,0:T(8,128)(2,1)S(1)} %get-tuple-element.185), channel_id=1, source_target_pairs={{0,4},{1,3},{2,6},{3,1},{4,0},{5,7},{6,2},{7,5},{8,12},{9,11},{10,... | collective-permute-start | bytes 884744 | tf_op jit(solution)/shard_map/ppermute | solution.py:38
  113.2 11.5 %collective-permute-start.32 = (bf16[64,2304]{1,0:T(8,128)(2,1)S(1)}, bf16[64,2304]{1,0:T(8,128)(2,1)S(1)}, u32[]{:S(2)}, u32[]{:S(2)}) collective-permute-start(bf16[64,2304]{1,0:T(8,128)(2,1)S(1)} %get-tuple-element.177), channel_id=1, source_target_pairs={{0,4},{1,3},{2,6},{3,1},{4,0},{5,7},{6,2},{7,5},{8,12},{9,11},{10,... | collective-permute-start | bytes 884744 | tf_op jit(solution)/shard_map/ppermute | solution.py:38
  114.3 10.4 %collective-permute-start.34 = (bf16[64,2304]{1,0:T(8,128)(2,1)S(1)}, bf16[64,2304]{1,0:T(8,128)(2,1)S(1)}, u32[]{:S(2)}, u32[]{:S(2)}) collective-permute-start(bf16[64,2304]{1,0:T(8,128)(2,1)S(1)} %add_rows.6), channel_id=1, source_target_pairs={{0,2},{1,5},{2,0},{3,7},{4,6},{5,1},{6,4},{7,3},{8,10},{9,13},{10,... | collective-permute-start | bytes 884744 | tf_op jit(solution)/shard_map/ppermute | solution.py:38
  121.8 9.2 %collective-permute-start.39 = (bf16[64,2304]{1,0:T(8,128)(2,1)S(1)}, bf16[64,2304]{1,0:T(8,128)(2,1)S(1)}, u32[]{:S(2)}, u32[]{:S(2)}) collective-permute-start(bf16[64,2304]{1,0:T(8,128)(2,1)S(1)} %get-tuple-element.200), channel_id=1, source_target_pairs={{0,4},{1,3},{2,6},{3,1},{4,0},{5,7},{6,2},{7,5},{8,12},{9,11},{10,... | collective-permute-start | bytes 884744 | tf_op jit(solution)/shard_map/ppermute | solution.py:38
  122.4 10.0 %collective-permute-start.29 = (bf16[64,2304]{1,0:T(8,128)(2,1)S(1)}, bf16[64,2304]{1,0:T(8,128)(2,1)S(1)}, u32[]{:S(2)}, u32[]{:S(2)}) collective-permute-start(bf16[64,2304]{1,0:T(8,128)(2,1)S(1)} %sum_rows.5), channel_id=1, source_target_pairs={{0,8},{8,0},{16,24},{24,16},{1,9},{9,1},{17,25},{25,17},{2,10},{10... | collective-permute-start | bytes 884744 | tf_op jit(solution)/shard_map/ppermute | solution.py:24
  124.8 10.9 %collective-permute-start.35 = (bf16[64,2304]{1,0:T(8,128)(2,1)S(1)}, bf16[64,2304]{1,0:T(8,128)(2,1)S(1)}, u32[]{:S(2)}, u32[]{:S(2)}) collective-permute-start(bf16[64,2304]{1,0:T(8,128)(2,1)S(1)} %sum_rows.6), channel_id=1, source_target_pairs={{0,16},{8,24},{16,0},{24,8},{1,17},{9,25},{17,1},{25,9},{2,18},{10... | collective-permute-start | bytes 884744 | tf_op jit(solution)/shard_map/ppermute | solution.py:24
  126.5 9.2 %collective-permute-start.38 = (bf16[64,2304]{1,0:T(8,128)(2,1)S(1)}, bf16[64,2304]{1,0:T(8,128)(2,1)S(1)}, u32[]{:S(2)}, u32[]{:S(2)}) collective-permute-start(bf16[64,2304]{1,0:T(8,128)(2,1)S(1)} %get-tuple-element.198), channel_id=1, source_target_pairs={{0,4},{1,3},{2,6},{3,1},{4,0},{5,7},{6,2},{7,5},{8,12},{9,11},{10,... | collective-permute-start | bytes 884744 | tf_op jit(solution)/shard_map/ppermute | solution.py:38
  138.0 9.0 %collective-permute-start.41 = (bf16[64,2304]{1,0:T(8,128)(2,1)S(1)}, bf16[64,2304]{1,0:T(8,128)(2,1)S(1)}, u32[]{:S(2)}, u32[]{:S(2)}) collective-permute-start(bf16[64,2304]{1,0:T(8,128)(2,1)S(1)} %sum_rows.7), channel_id=1, source_target_pairs={{0,24},{8,16},{16,8},{24,0},{1,25},{9,17},{17,9},{25,1},{2,26},{10... | collective-permute-start | bytes 884744 | tf_op jit(solution)/shard_map/ppermute | solution.py:24
  (32 other events, 175.8 us)

commit v4 on v3

--- a/solution.py
+++ b/solution.py
@@ -163,10 +163,14 @@
     ]
     for copy in copies:
         copy.start()
-    for copy in copies:
-        copy.wait()
+    count = all_ref.shape[0]
+    half = count // 2
+    for part in range(2):
+        for copy in copies[part * spots // 2 : (part + 1) * spots // 2]:
+            copy.wait()
+        span = slice(part * half, (part + 1) * half)
+        rows_ref[:, span] = all_ref[span, :width].T
     rows = all_ref[:, :width]
-    rows_ref[...] = rows.T
     tags = all_ref[:, width:].astype(F32)
     tag_ref[...] = tags.T[0:8, :]
     labels = tags[:, 0:1]

time: 149 us -> 149 us (level)
  no operation moved by 1% of the time
where the time goes in v4:
time: 149 us
  Pallas kernels  58.1 us (39%)
  starting transfers between devices  50.7 us (34%)
  waiting for transfers between devices  35.6 us (24%)
  local copies, waits for them, and re-layouts  3.13 us (2%)
    pallas_call x30, Pallas kernels, call(): pl.pallas_call(fn, out_shape=tuple(outs), in_specs=specs, out_specs=tuple...  45.8 us
    ppermute x32, starting transfers between devices, hop(): lax.ppermute(x, 'dp', [(i, i ^ spot_mask(i, spot, bits)) for i in range(n)])  34.7 us
    ppermute x32, waiting for transfers between devices, hop(): lax.ppermute(x, 'dp', [(i, i ^ spot_mask(i, spot, bits)) for i in range(n)])  21.1 us
    ppermute x10, starting transfers between devices, swap(): return lax.ppermute(x, axis, [(i, i ^ bit) for i in range(n)])  16 us
    ppermute x10, waiting for transfers between devices, swap(): return lax.ppermute(x, axis, [(i, i ^ bit) for i in range(n)])  14.6 us
    pallas_call x4, Pallas kernels, stage(): pl.pallas_call(functools.partial(stage_kernel, axis), out_shape=pltpu.VME...  12.3 us
    unnamed x46, local copies, waits for them, and re-layouts  3.13 us
  transfers between devices with their start and end apart: 42, of which 17 were waited for; matrix products, arithmetic and copies ran while one was open for 1% of the time, Pallas kernels for 36%

profile of v4, /device:TPU:0, one launch (start us, length us, event | category | flops | bytes accessed | tf_op | source)
XLA Modules:
  0.0 148.5 jit_solution(1762496866311459103)
XLA Ops:
  0.0 2.6 %front.1 = (bf16[64,2432]{1,0:T(8,128)(2,1)}, bf16[64,2432]{1,0:T(8,128)(2,1)}, bf16[64,2432]{1,0:T(8,128)(2,1)}, bf16[64,2432]{1,0:T(8,128)(2,1)}) custom-call(s32[1]{0:T(128)} %bitcast.z_ref, s32[1,4]{1,0:T(1,128)} %len_hbm.1, s32[1,4]{1,0:T(1,128)} %ada_hbm.1, s32[2,96]{1,0:T(2,128)} %bitcast.11, bf16[96,2304]{1,0:T(8,128)(2,1)} %tok_ref.1), custom_call_target="tpu_custom_call" | custom-call | flops 7077888 | bytes 27698 | tf_op jit(solution)/shard_map/front/pallas_call | solution.py:43
  3.2 2.9 %collective-permute-start = (bf16[64,2432]{1,0:T(8,128)(2,1)}, bf16[64,2432]{1,0:T(8,128)(2,1)S(1)}, u32[]{:S(2)}, u32[]{:S(2)}) collective-permute-start(bf16[64,2432]{1,0:T(8,128)(2,1)} %get-tuple-element.111.refs_0_), channel_id=1, source_target_pairs={{0,2},{1,5},{2,0},{3,7},{4,6},{5,1},{6,4},{7,3},{8,10},{9,13},{10,... | collective-permute-start | bytes 933896 | tf_op jit(solution)/shard_map/ppermute | solution.py:38
  9.2 4.7 %collective-permute-done.refs_1_ = bf16[64,2432]{1,0:T(8,128)(2,1)S(1)} collective-permute-done((bf16[64,2432]{1,0:T(8,128)(2,1)}, bf16[64,2432]{1,0:T(8,128)(2,1)S(1)}, u32[]{:S(2)}, u32[]{:S(2)}) %collective-permute-start) | collective-permute-done | bytes 311328 | tf_op jit(solution)/shard_map/ppermute | solution.py:38
  13.9 2.7 %collective-permute-done.2.refs_0_ = bf16[64,2432]{1,0:T(8,128)(2,1)S(1)} collective-permute-done((bf16[64,2432]{1,0:T(8,128)(2,1)}, bf16[64,2432]{1,0:T(8,128)(2,1)S(1)}, u32[]{:S(2)}, u32[]{:S(2)}) %collective-permute-start.2) | collective-permute-done | bytes 311328 | tf_op jit(solution)/shard_map/ppermute | solution.py:24
  18.4 6.2 %collective-permute-done.4.refs_3_ = bf16[64,2432]{1,0:T(8,128)(2,1)S(1)} collective-permute-done((bf16[64,2432]{1,0:T(8,128)(2,1)S(1)}, bf16[64,2432]{1,0:T(8,128)(2,1)S(1)}, u32[]{:S(2)}, u32[]{:S(2)}) %collective-permute-start.4) | collective-permute-done | bytes 311328 | tf_op jit(solution)/shard_map/ppermute | solution.py:38
  26.4 2.6 %collective-permute-start.14 = (bf16[64,2432]{1,0:T(8,128)(2,1)}, bf16[64,2432]{1,0:T(8,128)(2,1)}, u32[]{:S(2)}, u32[]{:S(2)}) collective-permute-start(bf16[64,2432]{1,0:T(8,128)(2,1)} %get-tuple-element.108), channel_id=1, source_target_pairs={{0,16},{8,24},{16,0},{24,8},{1,17},{9,25},{17,1},{25,9},{2,18},{10... | collective-permute-start | bytes 933896 | tf_op jit(solution)/shard_map/ppermute | solution.py:24
  30.7 4.8 %stage_gate_up.1.w_ref = bf16[4,720,2304]{2,1,0:T(8,128)(2,1)S(1)} custom-call(bf16[2,720,2304]{2,1,0:T(8,128)(2,1)} %bitcast.14, bf16[2,720,2304]{2,1,0:T(8,128)(2,1)} %collective-permute-done.5.refs_1_), custom_call_target="tpu_custom_call" | custom-call | tf_op jit(solution)/shard_map/stage_gate_up/pallas_call | solution.py:139
  38.0 2.2 %project.4 = (bf16[2304,256]{1,0:T(8,128)(2,1)S(1)}, f32[8,256]{1,0:T(8,128)S(1)}, bf16[64,128]{1,0:T(8,128)(2,1)S(1)}, bf16[64,128]{1,0:T(8,128)(2,1)S(1)}) custom-call(s32[1]{0:T(128)} %bitcast.2.me_ref, bf16[512,128]{1,0:T(8,128)(2,1)S(1)} %compare_convert_fusion.fold_ref, bf16[64,2432]{1,0:T(8,128)(2,1)} %get-tuple-element.111.refs_0_, ...), custom_call_target="tpu_custom_call" | custom-call | flops 37748736 | bytes 233472 | tf_op jit(solution)/shard_map/project/pallas_call | solution.py:43
  40.8 3.2 %collective-permute-done.14.refs_0_ = bf16[64,2432]{1,0:T(8,128)(2,1)} collective-permute-done((bf16[64,2432]{1,0:T(8,128)(2,1)}, bf16[64,2432]{1,0:T(8,128)(2,1)}, u32[]{:S(2)}, u32[]{:S(2)}) %collective-permute-start.14) | collective-permute-done | bytes 311328 | tf_op jit(solution)/shard_map/ppermute | solution.py:24
  46.5 1.9 %gate_up.8.refs_3_ = f32[2,720,256]{2,1,0:T(8,128)S(1)} custom-call(bf16[2304,256]{1,0:T(8,128)(2,1)S(1)} %get-tuple-element.126.rows_ref, bf16[4,720,2304]{2,1,0:T(8,128)(2,1)S(1)} %stage_gate_up.1.w_ref), custom_call_target="tpu_custom_call" | custom-call | flops 106168320 | bytes 903168 | tf_op jit(solution)/shard_map/gate_up/pallas_call | solution.py:43
  48.4 3.4 %collective-permute-start.22 = (bf16[64,2432]{1,0:T(8,128)(2,1)S(1)}, bf16[64,2432]{1,0:T(8,128)(2,1)S(1)}, u32[]{:S(2)}, u32[]{:S(2)}) collective-permute-start(bf16[64,2432]{1,0:T(8,128)(2,1)S(1)} %copy-done.21), channel_id=1, source_target_pairs={{0,24},{8,16},{16,8},{24,0},{1,25},{9,17},{17,9},{25,1},{2,26},{10... | collective-permute-start | bytes 933896 | tf_op jit(solution)/shard_map/ppermute | solution.py:24
  55.0 2.7 %stage_low_up.1.refs_5_ = bf16[4,720,1024]{2,1,0:T(8,128)(2,1)S(1)} custom-call(bf16[2,720,1024]{2,1,0:T(8,128)(2,1)} %bitcast.18, bf16[2,720,1024]{2,1,0:T(8,128)(2,1)} %copy-done.3), custom_call_target="tpu_custom_call" | custom-call | tf_op jit(solution)/shard_map/stage_low_up/pallas_call | solution.py:139
  57.8 1.9 %gate_up.9.refs_4_ = f32[2,720,256]{2,1,0:T(8,128)S(1)} custom-call(bf16[2304,256]{1,0:T(8,128)(2,1)S(1)} %get-tuple-element.126.rows_ref, bf16[4,720,2304]{2,1,0:T(8,128)(2,1)S(1)} %stage_gate_up.1.w_ref), custom_call_target="tpu_custom_call" | custom-call | flops 106168320 | bytes 903168 | tf_op jit(solution)/shard_map/gate_up/pallas_call | solution.py:43
  59.7 3.1 %stage_down.1.refs_6_ = bf16[1440,2304]{1,0:T(8,128)(2,1)S(1)} custom-call(bf16[720,2304]{1,0:T(8,128)(2,1)} %bitcast.16, bf16[720,2304]{1,0:T(8,128)(2,1)} %copy-done.2), custom_call_target="tpu_custom_call" | custom-call | tf_op jit(solution)/shard_map/stage_down/pallas_call | solution.py:139
  64.5 4.1 %down.4 = (bf16[64,2304]{1,0:T(8,128)(2,1)S(1)}, bf16[64,2304]{1,0:T(8,128)(2,1)S(1)}, bf16[64,2304]{1,0:T(8,128)(2,1)S(1)}, bf16[64,2304]{1,0:T(8,128)(2,1)S(1)}) custom-call(bf16[2,1024,128]{2,1,0:T(8,128)(2,1)S(1)} %add_convert_fusion.tile_ref, bf16[64,128]{1,0:T(8,128)(2,1)S(1)} %get-tuple-element.123.refs_0_, ...), custom_call_target="tpu_custom_call" | custom-call | flops 200540160 | bytes 1003008 | tf_op jit(solution)/shard_map/down/pallas_call | solution.py:43
  70.7 2.3 %project.5 = (bf16[2304,256]{1,0:T(8,128)(2,1)S(1)}, f32[8,256]{1,0:T(8,128)S(1)}, bf16[64,128]{1,0:T(8,128)(2,1)S(1)}, bf16[64,128]{1,0:T(8,128)(2,1)S(1)}) custom-call(s32[1]{0:T(128)} %bitcast.2.me_ref, bf16[512,128]{1,0:T(8,128)(2,1)S(1)} %compare_convert_fusion.fold_ref, bf16[64,2432]{1,0:T(8,128)(2,1)} %copy-done.8, bf16[64,2432]{1,0:T(8,128)(2,1)} %copy-done.13, ...), custom_call_target="tpu_custom_call" | custom-call | flops 37748736 | bytes 233472 | tf_op jit(solution)/shard_map/project/pallas_call | solution.py:43
  73.5 1.9 %gate_up.10.refs_3_ = f32[2,720,256]{2,1,0:T(8,128)S(1)} custom-call(bf16[2304,256]{1,0:T(8,128)(2,1)S(1)} %get-tuple-element.150.rows_ref, bf16[4,720,2304]{2,1,0:T(8,128)(2,1)S(1)} %stage_gate_up.1.w_ref), custom_call_target="tpu_custom_call" | custom-call | flops 106168320 | bytes 903168 | tf_op jit(solution)/shard_map/gate_up/pallas_call | solution.py:43
  82.8 4.3 %down.5 = (bf16[64,2304]{1,0:T(8,128)(2,1)S(1)}, bf16[64,2304]{1,0:T(8,128)(2,1)S(1)}, bf16[64,2304]{1,0:T(8,128)(2,1)S(1)}, bf16[64,2304]{1,0:T(8,128)(2,1)S(1)}) custom-call(bf16[2,1024,128]{2,1,0:T(8,128)(2,1)S(1)} %add_convert_fusion.tile_ref, bf16[64,128]{1,0:T(8,128)(2,1)S(1)} %get-tuple-element.147.refs_0_, ...), custom_call_target="tpu_custom_call" | custom-call | flops 200540160 | bytes 1003008 | tf_op jit(solution)/shard_map/down/pallas_call | solution.py:43
  88.2 2.2 %project.6 = (bf16[2304,256]{1,0:T(8,128)(2,1)S(1)}, f32[8,256]{1,0:T(8,128)S(1)}, bf16[64,128]{1,0:T(8,128)(2,1)S(1)}, bf16[64,128]{1,0:T(8,128)(2,1)S(1)}) custom-call(s32[1]{0:T(128)} %bitcast.2.me_ref, bf16[512,128]{1,0:T(8,128)(2,1)S(1)} %compare_convert_fusion.fold_ref, bf16[64,2432]{1,0:T(8,128)(2,1)} %collective-permute-done.14.refs_0_, ...), custom_call_target="tpu_custom_call" | custom-call | flops 37748736 | bytes 233472 | tf_op jit(solution)/shard_map/project/pallas_call | solution.py:43
  91.7 1.9 %gate_up.12.refs_3_ = f32[2,720,256]{2,1,0:T(8,128)S(1)} custom-call(bf16[2304,256]{1,0:T(8,128)(2,1)S(1)} %get-tuple-element.173.rows_ref, bf16[4,720,2304]{2,1,0:T(8,128)(2,1)S(1)} %stage_gate_up.1.w_ref), custom_call_target="tpu_custom_call" | custom-call | flops 106168320 | bytes 903168 | tf_op jit(solution)/shard_map/gate_up/pallas_call | solution.py:43
  99.6 4.1 %down.6 = (bf16[64,2304]{1,0:T(8,128)(2,1)S(1)}, bf16[64,2304]{1,0:T(8,128)(2,1)S(1)}, bf16[64,2304]{1,0:T(8,128)(2,1)S(1)}, bf16[64,2304]{1,0:T(8,128)(2,1)S(1)}) custom-call(bf16[2,1024,128]{2,1,0:T(8,128)(2,1)S(1)} %add_convert_fusion.tile_ref, bf16[64,128]{1,0:T(8,128)(2,1)S(1)} %get-tuple-element.170.refs_0_, ...), custom_call_target="tpu_custom_call" | custom-call | flops 200540160 | bytes 1003008 | tf_op jit(solution)/shard_map/down/pallas_call | solution.py:43
  105.9 2.2 %project.7 = (bf16[2304,256]{1,0:T(8,128)(2,1)S(1)}, f32[8,256]{1,0:T(8,128)S(1)}, bf16[64,128]{1,0:T(8,128)(2,1)S(1)}, bf16[64,128]{1,0:T(8,128)(2,1)S(1)}) custom-call(s32[1]{0:T(128)} %bitcast.2.me_ref, bf16[512,128]{1,0:T(8,128)(2,1)S(1)} %compare_convert_fusion.fold_ref, bf16[64,2432]{1,0:T(8,128)(2,1)} %copy-done.5, bf16[64,2432]{1,0:T(8,128)(2,1)} %copy-done.6, ...), custom_call_target="tpu_custom_call" | custom-call | flops 37748736 | bytes 233472 | tf_op jit(solution)/shard_map/project/pallas_call | solution.py:43
  109.7 1.9 %gate_up.14.refs_3_ = f32[2,720,256]{2,1,0:T(8,128)S(1)} custom-call(bf16[2304,256]{1,0:T(8,128)(2,1)S(1)} %get-tuple-element.193.rows_ref, bf16[4,720,2304]{2,1,0:T(8,128)(2,1)S(1)} %stage_gate_up.1.w_ref), custom_call_target="tpu_custom_call" | custom-call | flops 106168320 | bytes 903168 | tf_op jit(solution)/shard_map/gate_up/pallas_call | solution.py:43
  115.8 2.1 %gate_up.15.refs_4_ = f32[2,720,256]{2,1,0:T(8,128)S(1)} custom-call(bf16[2304,256]{1,0:T(8,128)(2,1)S(1)} %get-tuple-element.193.rows_ref, bf16[4,720,2304]{2,1,0:T(8,128)(2,1)S(1)} %stage_gate_up.1.w_ref), custom_call_target="tpu_custom_call" | custom-call | flops 106168320 | bytes 903168 | tf_op jit(solution)/shard_map/gate_up/pallas_call | solution.py:43
  117.9 4.1 %down.7 = (bf16[64,2304]{1,0:T(8,128)(2,1)S(1)}, bf16[64,2304]{1,0:T(8,128)(2,1)S(1)}, bf16[64,2304]{1,0:T(8,128)(2,1)S(1)}, bf16[64,2304]{1,0:T(8,128)(2,1)S(1)}) custom-call(bf16[2,1024,128]{2,1,0:T(8,128)(2,1)S(1)} %add_convert_fusion.tile_ref, bf16[64,128]{1,0:T(8,128)(2,1)S(1)} %get-tuple-element.190.refs_0_, ...), custom_call_target="tpu_custom_call" | custom-call | flops 200540160 | bytes 1003008 | tf_op jit(solution)/shard_map/down/pallas_call | solution.py:43
  122.4 2.3 %collective-permute-start.29 = (bf16[64,2304]{1,0:T(8,128)(2,1)S(1)}, bf16[64,2304]{1,0:T(8,128)(2,1)S(1)}, u32[]{:S(2)}, u32[]{:S(2)}) collective-permute-start(bf16[64,2304]{1,0:T(8,128)(2,1)S(1)} %sum_rows.5), channel_id=1, source_target_pairs={{0,8},{8,0},{16,24},{24,16},{1,9},{9,1},{17,25},{25,17},{2,10},{10... | collective-permute-start | bytes 884744 | tf_op jit(solution)/shard_map/ppermute | solution.py:24
  126.5 1.9 %collective-permute-start.38 = (bf16[64,2304]{1,0:T(8,128)(2,1)S(1)}, bf16[64,2304]{1,0:T(8,128)(2,1)S(1)}, u32[]{:S(2)}, u32[]{:S(2)}) collective-permute-start(bf16[64,2304]{1,0:T(8,128)(2,1)S(1)} %get-tuple-element.198), channel_id=1, source_target_pairs={{0,4},{1,3},{2,6},{3,1},{4,0},{5,7},{6,2},{7,5},{8,12},{9,11},{10,... | collective-permute-start | bytes 884744 | tf_op jit(solution)/shard_map/ppermute | solution.py:38
  128.5 2.8 %collective-permute-done.39.b_ref = bf16[64,2304]{1,0:T(8,128)(2,1)S(1)} collective-permute-done((bf16[64,2304]{1,0:T(8,128)(2,1)S(1)}, bf16[64,2304]{1,0:T(8,128)(2,1)S(1)}, u32[]{:S(2)}, u32[]{:S(2)}) %collective-permute-start.39) | collective-permute-done | bytes 294944 | tf_op jit(solution)/shard_map/ppermute | solution.py:38
  132.5 3.2 %collective-permute-done.35.refs_2_ = bf16[64,2304]{1,0:T(8,128)(2,1)S(1)} collective-permute-done((bf16[64,2304]{1,0:T(8,128)(2,1)S(1)}, bf16[64,2304]{1,0:T(8,128)(2,1)S(1)}, u32[]{:S(2)}, u32[]{:S(2)}) %collective-permute-start.35) | collective-permute-done | bytes 294944 | tf_op jit(solution)/shard_map/ppermute | solution.py:24
  135.8 2.4 %collective-permute-done.40.refs_2_ = bf16[64,2304]{1,0:T(8,128)(2,1)S(1)} collective-permute-done((bf16[64,2304]{1,0:T(8,128)(2,1)S(1)}, bf16[64,2304]{1,0:T(8,128)(2,1)S(1)}, u32[]{:S(2)}, u32[]{:S(2)}) %collective-permute-start.40) | collective-permute-done | bytes 294944 | tf_op jit(solution)/shard_map/ppermute | solution.py:38
  138.3 3.8 %collective-permute-start.41 = (bf16[64,2304]{1,0:T(8,128)(2,1)S(1)}, bf16[64,2304]{1,0:T(8,128)(2,1)S(1)}, u32[]{:S(2)}, u32[]{:S(2)}) collective-permute-start(bf16[64,2304]{1,0:T(8,128)(2,1)S(1)} %sum_rows.7), channel_id=1, source_target_pairs={{0,24},{8,16},{16,8},{24,0},{1,25},{9,17},{17,9},{25,1},{2,26},{10... | collective-permute-start | bytes 884744 | tf_op jit(solution)/shard_map/ppermute | solution.py:24
  142.3 4.7 %collective-permute-done.41.refs_3_ = bf16[64,2304]{1,0:T(8,128)(2,1)S(1)} collective-permute-done((bf16[64,2304]{1,0:T(8,128)(2,1)S(1)}, bf16[64,2304]{1,0:T(8,128)(2,1)S(1)}, u32[]{:S(2)}, u32[]{:S(2)}) %collective-permute-start.41) | collective-permute-done | bytes 294944 | tf_op jit(solution)/shard_map/ppermute | solution.py:24
  (138 shorter events, 51.1 us)
Async XLA Ops:
  2.6 14.0 %collective-permute-start.5 = (bf16[2,720,2304]{2,1,0:T(8,128)(2,1)}, bf16[2,720,2304]{2,1,0:T(8,128)(2,1)}, u32[]{:S(2)}, u32[]{:S(2)}) collective-permute-start(bf16[2,720,2304]{2,1,0:T(8,128)(2,1)} %bitcast.13), channel_id=1, source_target_pairs={{0,1},{1,0},{2,3},{3,2},{4,5},{5,4},{6,7},{7,6},{8,9},{9,8},{10,11... | collective-permute-start | bytes 19906568 | tf_op jit(solution)/shard_map/ppermute | solution.py:24
  3.1 13.5 %collective-permute-start.3 = (bf16[2304,256]{1,0:T(8,128)(2,1)}, bf16[2304,256]{1,0:T(8,128)(2,1)S(1)}, u32[]{:S(2)}, u32[]{:S(2)}) collective-permute-start(bf16[2304,256]{1,0:T(8,128)(2,1)} %bitcast.19), channel_id=1, source_target_pairs={{0,1},{1,0},{2,3},{3,2},{4,5},{5,4},{6,7},{7,6},{8,9},{9,8},{10,11... | collective-permute-start | bytes 3538952 | tf_op jit(solution)/shard_map/ppermute | solution.py:24
  3.2 10.7 %collective-permute-start = (bf16[64,2432]{1,0:T(8,128)(2,1)}, bf16[64,2432]{1,0:T(8,128)(2,1)S(1)}, u32[]{:S(2)}, u32[]{:S(2)}) collective-permute-start(bf16[64,2432]{1,0:T(8,128)(2,1)} %get-tuple-element.111.refs_0_), channel_id=1, source_target_pairs={{0,2},{1,5},{2,0},{3,7},{4,6},{5,1},{6,4},{7,3},{8,10},{9,13},{10,... | collective-permute-start | bytes 933896 | tf_op jit(solution)/shard_map/ppermute | solution.py:38
  6.1 7.8 %collective-permute-start.1 = (bf16[64,2432]{1,0:T(8,128)(2,1)}, bf16[64,2432]{1,0:T(8,128)(2,1)S(1)}, u32[]{:S(2)}, u32[]{:S(2)}) collective-permute-start(bf16[64,2432]{1,0:T(8,128)(2,1)} %get-tuple-element.111.refs_0_), channel_id=1, source_target_pairs={{0,4},{1,3},{2,6},{3,1},{4,0},{5,7},{6,2},{7,5},{8,12},{9,11},{10,... | collective-permute-start | bytes 933896 | tf_op jit(solution)/shard_map/ppermute | solution.py:38
  7.6 9.0 %collective-permute-start.2 = (bf16[64,2432]{1,0:T(8,128)(2,1)}, bf16[64,2432]{1,0:T(8,128)(2,1)S(1)}, u32[]{:S(2)}, u32[]{:S(2)}) collective-permute-start(bf16[64,2432]{1,0:T(8,128)(2,1)} %get-tuple-element.104), channel_id=1, source_target_pairs={{0,8},{8,0},{16,24},{24,16},{1,9},{9,1},{17,25},{25,17},{2,10},{10... | collective-permute-start | bytes 933896 | tf_op jit(solution)/shard_map/ppermute | solution.py:24
  26.3 20.1 %collective-permute-start.9 = (bf16[720,2304]{1,0:T(8,128)(2,1)}, bf16[720,2304]{1,0:T(8,128)(2,1)S(1)}, u32[]{:S(2)}, u32[]{:S(2)}) collective-permute-start(bf16[720,2304]{1,0:T(8,128)(2,1)} %bitcast.15), channel_id=1, source_target_pairs={{0,1},{1,0},{2,3},{3,2},{4,5},{5,4},{6,7},{7,6},{8,9},{9,8},{10,11... | collective-permute-start | bytes 9953288 | tf_op jit(solution)/shard_map/ppermute | solution.py:24
  26.4 17.6 %collective-permute-start.14 = (bf16[64,2432]{1,0:T(8,128)(2,1)}, bf16[64,2432]{1,0:T(8,128)(2,1)}, u32[]{:S(2)}, u32[]{:S(2)}) collective-permute-start(bf16[64,2432]{1,0:T(8,128)(2,1)} %get-tuple-element.108), channel_id=1, source_target_pairs={{0,16},{8,24},{16,0},{24,8},{1,17},{9,25},{17,1},{25,9},{2,18},{10... | collective-permute-start | bytes 933896 | tf_op jit(solution)/shard_map/ppermute | solution.py:24
  35.5 10.0 %collective-permute-start.6 = (bf16[64,2432]{1,0:T(8,128)(2,1)S(1)}, bf16[64,2432]{1,0:T(8,128)(2,1)S(1)}, u32[]{:S(2)}, u32[]{:S(2)}) collective-permute-start(bf16[64,2432]{1,0:T(8,128)(2,1)S(1)} %copy-done.9), channel_id=1, source_target_pairs={{0,2},{1,5},{2,0},{3,7},{4,6},{5,1},{6,4},{7,3},{8,10},{9,13},{10,... | collective-permute-start | bytes 933896 | tf_op jit(solution)/shard_map/ppermute | solution.py:38
  36.3 9.2 %collective-permute-start.7 = (bf16[64,2432]{1,0:T(8,128)(2,1)S(1)}, bf16[64,2432]{1,0:T(8,128)(2,1)S(1)}, u32[]{:S(2)}, u32[]{:S(2)}) collective-permute-start(bf16[64,2432]{1,0:T(8,128)(2,1)S(1)} %copy-done.9), channel_id=1, source_target_pairs={{0,4},{1,3},{2,6},{3,1},{4,0},{5,7},{6,2},{7,5},{8,12},{9,11},{10,... | collective-permute-start | bytes 933896 | tf_op jit(solution)/shard_map/ppermute | solution.py:38
  40.2 12.5 %collective-permute-start.10 = (bf16[64,128]{1,0:T(8,128)(2,1)S(1)}, bf16[64,128]{1,0:T(8,128)(2,1)S(1)}, u32[]{:S(2)}, u32[]{:S(2)}) collective-permute-start(bf16[64,128]{1,0:T(8,128)(2,1)S(1)} %get-tuple-element.122), channel_id=1, source_target_pairs={{0,2},{1,5},{2,0},{3,7},{4,6},{5,1},{6,4},{7,3},{8,10},{9,13},{10,... | collective-permute-start | bytes 49160 | tf_op jit(solution)/shard_map/ppermute | solution.py:38
  44.0 10.4 %collective-permute-start.15 = (bf16[64,2432]{1,0:T(8,128)(2,1)}, bf16[64,2432]{1,0:T(8,128)(2,1)S(1)}, u32[]{:S(2)}, u32[]{:S(2)}) collective-permute-start(bf16[64,2432]{1,0:T(8,128)(2,1)} %collective-permute-done.14.refs_0_), channel_id=1, source_target_pairs={{0,2},{1,5},{2,0},{3,7},{4,6},{5,1},{6,4},{7,3},{8,10},{9,13},{10,... | collective-permute-start | bytes 933896 | tf_op jit(solution)/shard_map/ppermute | solution.py:38
  45.5 14.1 %collective-permute-start.12 = (bf16[64,2432]{1,0:T(8,128)(2,1)S(1)}, bf16[64,2432]{1,0:T(8,128)(2,1)S(1)}, u32[]{:S(2)}, u32[]{:S(2)}) collective-permute-start(bf16[64,2432]{1,0:T(8,128)(2,1)S(1)} %collective-permute-done.6.refs_1_), channel_id=1, source_target_pairs={{0,4},{1,3},{2,6},{3,1},{4,0},{5,7},{6,2},{7,5},{8,12},{9,11},{10,... | collective-permute-start | bytes 933896 | tf_op jit(solution)/shard_map/ppermute | solution.py:38
  48.4 14.4 %collective-permute-start.22 = (bf16[64,2432]{1,0:T(8,128)(2,1)S(1)}, bf16[64,2432]{1,0:T(8,128)(2,1)S(1)}, u32[]{:S(2)}, u32[]{:S(2)}) collective-permute-start(bf16[64,2432]{1,0:T(8,128)(2,1)S(1)} %copy-done.21), channel_id=1, source_target_pairs={{0,24},{8,16},{16,8},{24,0},{1,25},{9,17},{17,9},{25,1},{2,26},{10... | collective-permute-start | bytes 933896 | tf_op jit(solution)/shard_map/ppermute | solution.py:24
  52.1 18.5 %collective-permute-start.16 = (bf16[64,2432]{1,0:T(8,128)(2,1)}, bf16[64,2432]{1,0:T(8,128)(2,1)S(1)}, u32[]{:S(2)}, u32[]{:S(2)}) collective-permute-start(bf16[64,2432]{1,0:T(8,128)(2,1)} %collective-permute-done.14.refs_0_), channel_id=1, source_target_pairs={{0,4},{1,3},{2,6},{3,1},{4,0},{5,7},{6,2},{7,5},{8,12},{9,11},{10,... | collective-permute-start | bytes 933896 | tf_op jit(solution)/shard_map/ppermute | solution.py:38
  52.8 11.7 %collective-permute-start.11 = (bf16[64,128]{1,0:T(8,128)(2,1)S(1)}, bf16[64,128]{1,0:T(8,128)(2,1)S(1)}, u32[]{:S(2)}, u32[]{:S(2)}) collective-permute-start(bf16[64,128]{1,0:T(8,128)(2,1)S(1)} %get-tuple-element.124), channel_id=1, source_target_pairs={{0,4},{1,3},{2,6},{3,1},{4,0},{5,7},{6,2},{7,5},{8,12},{9,11},{10,... | collective-permute-start | bytes 49160 | tf_op jit(solution)/shard_map/ppermute | solution.py:38
  54.4 24.5 %collective-permute-start.21 = (bf16[64,2432]{1,0:T(8,128)(2,1)S(1)}, bf16[64,2432]{1,0:T(8,128)(2,1)S(1)}, u32[]{:S(2)}, u32[]{:S(2)}) collective-permute-start(bf16[64,2432]{1,0:T(8,128)(2,1)S(1)} %collective-permute-done.15.refs_1_), channel_id=1, source_target_pairs={{0,4},{1,3},{2,6},{3,1},{4,0},{5,7},{6,2},{7,5},{8,12},{9,11},{10,... | collective-permute-start | bytes 933896 | tf_op jit(solution)/shard_map/ppermute | solution.py:38
  62.8 16.8 %collective-permute-start.23 = (bf16[64,2432]{1,0:T(8,128)(2,1)S(1)}, bf16[64,2432]{1,0:T(8,128)(2,1)S(1)}, u32[]{:S(2)}, u32[]{:S(2)}) collective-permute-start(bf16[64,2432]{1,0:T(8,128)(2,1)S(1)} %collective-permute-done.22.refs_0_), channel_id=1, source_target_pairs={{0,2},{1,5},{2,0},{3,7},{4,6},{5,1},{6,4},{7,3},{8,10},{9,13},{10,... | collective-permute-start | bytes 933896 | tf_op jit(solution)/shard_map/ppermute | solution.py:38
  68.6 7.0 %collective-permute-start.17 = (bf16[64,2304]{1,0:T(8,128)(2,1)S(1)}, bf16[64,2304]{1,0:T(8,128)(2,1)S(1)}, u32[]{:S(2)}, u32[]{:S(2)}) collective-permute-start(bf16[64,2304]{1,0:T(8,128)(2,1)S(1)} %get-tuple-element.142), channel_id=1, source_target_pairs={{0,4},{1,3},{2,6},{3,1},{4,0},{5,7},{6,2},{7,5},{8,12},{9,11},{10,... | collective-permute-start | bytes 884744 | tf_op jit(solution)/shard_map/ppermute | solution.py:38
  69.0 13.7 %collective-permute-start.24 = (bf16[64,2432]{1,0:T(8,128)(2,1)S(1)}, bf16[64,2432]{1,0:T(8,128)(2,1)S(1)}, u32[]{:S(2)}, u32[]{:S(2)}) collective-permute-start(bf16[64,2432]{1,0:T(8,128)(2,1)S(1)} %collective-permute-done.22.refs_0_), channel_id=1, source_target_pairs={{0,4},{1,3},{2,6},{3,1},{4,0},{5,7},{6,2},{7,5},{8,12},{9,11},{10,... | collective-permute-start | bytes 933896 | tf_op jit(solution)/shard_map/ppermute | solution.py:38
  77.5 10.3 %collective-permute-start.13 = (bf16[64,2304]{1,0:T(8,128)(2,1)S(1)}, bf16[64,2304]{1,0:T(8,128)(2,1)S(1)}, u32[]{:S(2)}, u32[]{:S(2)}) collective-permute-start(bf16[64,2304]{1,0:T(8,128)(2,1)S(1)} %get-tuple-element.133), channel_id=1, source_target_pairs={{0,4},{1,3},{2,6},{3,1},{4,0},{5,7},{6,2},{7,5},{8,12},{9,11},{10,... | collective-permute-start | bytes 884744 | tf_op jit(solution)/shard_map/ppermute | solution.py:38
  79.0 9.1 %collective-permute-start.18 = (bf16[64,2304]{1,0:T(8,128)(2,1)S(1)}, bf16[64,2304]{1,0:T(8,128)(2,1)S(1)}, u32[]{:S(2)}, u32[]{:S(2)}) collective-permute-start(bf16[64,2304]{1,0:T(8,128)(2,1)S(1)} %add_rows.4), channel_id=1, source_target_pairs={{0,2},{1,5},{2,0},{3,7},{4,6},{5,1},{6,4},{7,3},{8,10},{9,13},{10,... | collective-permute-start | bytes 884744 | tf_op jit(solution)/shard_map/ppermute | solution.py:38
  79.6 12.2 %collective-permute-start.26 = (bf16[64,2432]{1,0:T(8,128)(2,1)S(1)}, bf16[64,2432]{1,0:T(8,128)(2,1)S(1)}, u32[]{:S(2)}, u32[]{:S(2)}) collective-permute-start(bf16[64,2432]{1,0:T(8,128)(2,1)S(1)} %collective-permute-done.23.refs_1_), channel_id=1, source_target_pairs={{0,4},{1,3},{2,6},{3,1},{4,0},{5,7},{6,2},{7,5},{8,12},{9,11},{10,... | collective-permute-start | bytes 933896 | tf_op jit(solution)/shard_map/ppermute | solution.py:38
  95.6 9.0 %collective-permute-start.25 = (bf16[64,2304]{1,0:T(8,128)(2,1)S(1)}, bf16[64,2304]{1,0:T(8,128)(2,1)S(1)}, u32[]{:S(2)}, u32[]{:S(2)}) collective-permute-start(bf16[64,2304]{1,0:T(8,128)(2,1)S(1)} %get-tuple-element.156), channel_id=1, source_target_pairs={{0,4},{1,3},{2,6},{3,1},{4,0},{5,7},{6,2},{7,5},{8,12},{9,11},{10,... | collective-permute-start | bytes 884744 | tf_op jit(solution)/shard_map/ppermute | solution.py:38
  96.5 9.3 %collective-permute-start.28 = (bf16[64,2304]{1,0:T(8,128)(2,1)S(1)}, bf16[64,2304]{1,0:T(8,128)(2,1)S(1)}, u32[]{:S(2)}, u32[]{:S(2)}) collective-permute-start(bf16[64,2304]{1,0:T(8,128)(2,1)S(1)} %add_rows.5), channel_id=1, source_target_pairs={{0,2},{1,5},{2,0},{3,7},{4,6},{5,1},{6,4},{7,3},{8,10},{9,13},{10,... | collective-permute-start | bytes 884744 | tf_op jit(solution)/shard_map/ppermute | solution.py:38
  103.7 7.9 %collective-permute-start.33 = (bf16[64,2304]{1,0:T(8,128)(2,1)S(1)}, bf16[64,2304]{1,0:T(8,128)(2,1)S(1)}, u32[]{:S(2)}, u32[]{:S(2)}) collective-permute-start(bf16[64,2304]{1,0:T(8,128)(2,1)S(1)} %get-tuple-element.185), channel_id=1, source_target_pairs={{0,4},{1,3},{2,6},{3,1},{4,0},{5,7},{6,2},{7,5},{8,12},{9,11},{10,... | collective-permute-start | bytes 884744 | tf_op jit(solution)/shard_map/ppermute | solution.py:38
  113.4 11.4 %collective-permute-start.32 = (bf16[64,2304]{1,0:T(8,128)(2,1)S(1)}, bf16[64,2304]{1,0:T(8,128)(2,1)S(1)}, u32[]{:S(2)}, u32[]{:S(2)}) collective-permute-start(bf16[64,2304]{1,0:T(8,128)(2,1)S(1)} %get-tuple-element.177), channel_id=1, source_target_pairs={{0,4},{1,3},{2,6},{3,1},{4,0},{5,7},{6,2},{7,5},{8,12},{9,11},{10,... | collective-permute-start | bytes 884744 | tf_op jit(solution)/shard_map/ppermute | solution.py:38
  114.3 10.5 %collective-permute-start.34 = (bf16[64,2304]{1,0:T(8,128)(2,1)S(1)}, bf16[64,2304]{1,0:T(8,128)(2,1)S(1)}, u32[]{:S(2)}, u32[]{:S(2)}) collective-permute-start(bf16[64,2304]{1,0:T(8,128)(2,1)S(1)} %add_rows.6), channel_id=1, source_target_pairs={{0,2},{1,5},{2,0},{3,7},{4,6},{5,1},{6,4},{7,3},{8,10},{9,13},{10,... | collective-permute-start | bytes 884744 | tf_op jit(solution)/shard_map/ppermute | solution.py:38
  122.0 9.3 %collective-permute-start.39 = (bf16[64,2304]{1,0:T(8,128)(2,1)S(1)}, bf16[64,2304]{1,0:T(8,128)(2,1)S(1)}, u32[]{:S(2)}, u32[]{:S(2)}) collective-permute-start(bf16[64,2304]{1,0:T(8,128)(2,1)S(1)} %get-tuple-element.200), channel_id=1, source_target_pairs={{0,4},{1,3},{2,6},{3,1},{4,0},{5,7},{6,2},{7,5},{8,12},{9,11},{10,... | collective-permute-start | bytes 884744 | tf_op jit(solution)/shard_map/ppermute | solution.py:38
  122.4 10.1 %collective-permute-start.29 = (bf16[64,2304]{1,0:T(8,128)(2,1)S(1)}, bf16[64,2304]{1,0:T(8,128)(2,1)S(1)}, u32[]{:S(2)}, u32[]{:S(2)}) collective-permute-start(bf16[64,2304]{1,0:T(8,128)(2,1)S(1)} %sum_rows.5), channel_id=1, source_target_pairs={{0,8},{8,0},{16,24},{24,16},{1,9},{9,1},{17,25},{25,17},{2,10},{10... | collective-permute-start | bytes 884744 | tf_op jit(solution)/shard_map/ppermute | solution.py:24
  124.9 10.9 %collective-permute-start.35 = (bf16[64,2304]{1,0:T(8,128)(2,1)S(1)}, bf16[64,2304]{1,0:T(8,128)(2,1)S(1)}, u32[]{:S(2)}, u32[]{:S(2)}) collective-permute-start(bf16[64,2304]{1,0:T(8,128)(2,1)S(1)} %sum_rows.6), channel_id=1, source_target_pairs={{0,16},{8,24},{16,0},{24,8},{1,17},{9,25},{17,1},{25,9},{2,18},{10... | collective-permute-start | bytes 884744 | tf_op jit(solution)/shard_map/ppermute | solution.py:24
  126.5 9.3 %collective-permute-start.38 = (bf16[64,2304]{1,0:T(8,128)(2,1)S(1)}, bf16[64,2304]{1,0:T(8,128)(2,1)S(1)}, u32[]{:S(2)}, u32[]{:S(2)}) collective-permute-start(bf16[64,2304]{1,0:T(8,128)(2,1)S(1)} %get-tuple-element.198), channel_id=1, source_target_pairs={{0,4},{1,3},{2,6},{3,1},{4,0},{5,7},{6,2},{7,5},{8,12},{9,11},{10,... | collective-permute-start | bytes 884744 | tf_op jit(solution)/shard_map/ppermute | solution.py:38
  138.3 8.7 %collective-permute-start.41 = (bf16[64,2304]{1,0:T(8,128)(2,1)S(1)}, bf16[64,2304]{1,0:T(8,128)(2,1)S(1)}, u32[]{:S(2)}, u32[]{:S(2)}) collective-permute-start(bf16[64,2304]{1,0:T(8,128)(2,1)S(1)} %sum_rows.7), channel_id=1, source_target_pairs={{0,24},{8,16},{16,8},{24,0},{1,25},{9,17},{17,9},{25,1},{2,26},{10... | collective-permute-start | bytes 884744 | tf_op jit(solution)/shard_map/ppermute | solution.py:24
  (32 other events, 175.7 us)
